TPU v7x, 256 devices: a whole 4x4x8 slice. The times are simulated.
256 devices in a mesh: blk: 64 (over x, z, core), rep: 4 (over y).
Axes of the slice: x: 4, y: 4, z: 8, core: 2. Of those that a mesh axis runs over, the one named last changes fastest.
Arguments:
- query_embed: bfloat16 [64, 4, 256, 256], P('blk', 'rep'), may hold values from -96 to 96
- positive_ids: int32 [64, 4, 256], P('blk'), may hold values from 0 to 16383, as said below
- pair_blocks: int32 [64, 64], P('blk'), may hold values from 0 to 255, as said below
- code_ids: int32 [64, 4, 8, 64], P('blk', 'rep'), may hold values from 0 to 255
- codebooks: bfloat16 [2048, 256], replicated, may hold values from -3 to 3
Outputs:
- query_loss: float32 [64, 4, 256], P('blk', 'rep')
- query_grad: float32 [64, 4, 256, 256], P('blk', 'rep')
- passage_grad: float32 [64, 4, 64, 256], P('blk', 'rep')
- codebook_grad: float32 [2048, 256], P(('blk', 'rep'))
Inputs may be any that keep to these rules, and one draw needn't show every extreme that they name: `pair_blocks`: each row names 64 different passage blocks; at most 2 of them belong to one owner o (blocks o * 4 to o * 4 + 3), and in every row some owner has exactly 2. Some blocks are named in many rows. `positive_ids`: the positive passage of a query lies in a block named in its query block's row of pair_blocks.
All inputs are finite; a program needn't handle non-finite values.
Results may differ from a plain program's by a relative error of at most 0.0079.
Values may be sent and summed in bfloat16 or wider, within the bound.
No kernel may reach another device: no remote copies, remote signals or barrier semaphores. Data moves between devices by JAX's collectives and lax.ppermute only.
A program may use at most 64 MiB of HBM per device.

v0:
```python
import jax
import jax.numpy as jnp
from jax import lax
from jax.sharding import Mesh
from jax.sharding import PartitionSpec as P

CODES = 256
PR = 16
PBLK_DEV = 4
CAP = 2
BLK = ("blk_0", "blk_1", "blk_2")
BLK_REP = ("blk_0", "blk_1", "blk_2", "rep")


EPS = 1e-06


def from_everyone(x, axis):
    count = lax.axis_size(axis)
    return lax.all_to_all(jnp.broadcast_to(x[None], (count, *x.shape)), axis, 0, 0, tiled=True)


def joined_along(tiles, dim):
    lengths = list(tiles.shape[1:])
    lengths[dim] *= tiles.shape[0]
    return jnp.moveaxis(tiles, 0, dim).reshape(lengths)


def gather_directly(x, axis, dim):
    tiles = from_everyone(x, axis)
    return joined_along(tiles, dim)


def collected_together(x, axis):
    leaves = jax.tree.leaves(x)
    sequence = sorted(range(len(leaves)), key=lambda k: -leaves[k].size)
    width = (1, *leaves[sequence[0]].shape)[-1]
    lines = [
        jnp.pad(leaves[k].reshape(-1), (0, -leaves[k].size % width)).reshape(-1, width)
        for k in sequence
    ]
    both, at, found = (from_everyone(jnp.concatenate(lines), axis), 0, {})
    for k, line in zip(sequence, lines):
        section = both[:, at : at + len(line)].reshape(len(both), -1)
        found[k] = section[:, : leaves[k].size].reshape(-1, *leaves[k].shape)
        at += len(line)
    numbers = iter(range(len(leaves)))
    return jax.tree.map(lambda _: found[next(numbers)], x)


def combined_pairwise(pieces, combine):
    while len(jax.tree.leaves(pieces)[0]) > 1:
        pieces = jax.vmap(combine)(
            *(jax.tree.map(lambda part: part[side::2], pieces) for side in (0, 1))
        )
    return jax.tree.map(lambda part: part[0], pieces)


def combined_all(x, axis, combine):
    pieces = collected_together(x, axis)
    return combined_pairwise(pieces, combine)


def split_up(x, dim, count):
    lengths = x.shape
    tiles = x.reshape(*lengths[:dim], count, lengths[dim] // count, *lengths[dim + 1 :])
    return jnp.moveaxis(tiles, dim, 0)


def sent_and_summed(x, axis, dim):
    count = lax.axis_size(axis)
    tiles = lax.all_to_all(split_up(x, dim, count), axis, 0, 0, tiled=True)
    return jnp.sum(tiles, axis=0)


def sum_at_owner(x, axis, dim):
    tiles = split_up(x, dim, lax.axis_size(axis))
    arrived = lax.all_to_all(tiles, axis, split_axis=0, concat_axis=0, tiled=True)
    return arrived.astype(jnp.float32).sum(axis=0)


def sum_in_two_steps(x, axes, dim):
    far, near = axes
    tiles = split_up(x, dim, lax.axis_size(far))
    nearer = sum_at_owner(tiles, near, dim + 1)
    arrived = lax.all_to_all(
        nearer.astype(jnp.bfloat16), far, split_axis=0, concat_axis=0, tiled=True
    )
    return arrived.astype(jnp.float32).sum(axis=0)


def unit_rows(local_codes, codebooks):
    book_total = local_codes.shape[0]
    table_rows = codebooks.shape[0] // book_total
    code_iota = jnp.arange(table_rows, dtype=jnp.int32)
    pieces = []
    for book_index in range(book_total):
        pieces.append((local_codes[book_index][:, None] == code_iota[None, :]).astype(jnp.bfloat16))
    onehot = jnp.concatenate(pieces, axis=1)
    quant = jnp.dot(onehot, codebooks, preferred_element_type=jnp.float32)
    inverse = lax.rsqrt(jnp.sum(quant * quant, axis=1, keepdims=True) + EPS)
    return (quant * inverse, inverse)


def group_view(blocks):
    pair_count, span_rows, feat_count = blocks.shape
    group_size = min(8, pair_count)
    return blocks.reshape(pair_count // group_size, group_size * span_rows, feat_count)


def score_block(row_block, group_rows):
    return lax.dot_general(
        row_block, group_rows, (((1,), (1,)), ((), ())), preferred_element_type=jnp.float32
    )


def column_stats(row_block, grouped, target_col):
    row_count = row_block.shape[0]
    span_cols = grouped.shape[1]
    column_iota = jnp.arange(span_cols, dtype=jnp.int32)

    def visit(carry, item):
        peak_old, total_old, hit_old = carry
        group_index, group_rows = item
        scores = score_block(row_block, group_rows)
        peak_new = jnp.maximum(peak_old, jnp.max(scores, axis=1))
        total_new = total_old * jnp.exp(peak_old - peak_new) + jnp.sum(
            jnp.exp(scores - peak_new[:, None]), axis=1
        )
        here_cols = group_index * span_cols + column_iota
        hit_new = hit_old + jnp.sum(
            jnp.where(here_cols[None, :] == target_col[:, None], scores, 0.0), axis=1
        )
        return ((peak_new, total_new, hit_new), None)

    start = (
        jnp.full((row_count,), -1e30, jnp.float32),
        jnp.zeros((row_count,), jnp.float32),
        jnp.zeros((row_count,), jnp.float32),
    )
    group_ids = jnp.arange(grouped.shape[0], dtype=jnp.int32)
    result, unused = lax.scan(visit, start, (group_ids, grouped))
    return result


def column_grads(row_block, grouped, target_col, lse):
    span_cols = grouped.shape[1]
    column_iota = jnp.arange(span_cols, dtype=jnp.int32)

    def visit(grad_rows, item):
        group_index, group_rows = item
        scores = score_block(row_block, group_rows)
        here_cols = group_index * span_cols + column_iota
        hit_mask = (here_cols[None, :] == target_col[:, None]).astype(jnp.float32)
        weight = (jnp.exp(scores - lse[:, None]) - hit_mask).astype(jnp.bfloat16)
        grad_rows = grad_rows + jnp.dot(weight, group_rows, preferred_element_type=jnp.float32)
        grad_cols = lax.dot_general(
            weight, row_block, (((0,), (0,)), ((), ())), preferred_element_type=jnp.float32
        )
        return (grad_rows, grad_cols)

    start = jnp.zeros((row_block.shape[0], row_block.shape[1]), jnp.float32)
    group_ids = jnp.arange(grouped.shape[0], dtype=jnp.int32)
    return lax.scan(visit, start, (group_ids, grouped))


def merge_partials(first, second):
    peak_both = jnp.maximum(first[0], second[0])
    total_both = first[1] * jnp.exp(first[0] - peak_both) + second[1] * jnp.exp(
        second[0] - peak_both
    )
    return (peak_both, total_both, first[2] + second[2])


def find_slot(wanted, target_block):
    slot_iota = jnp.arange(wanted.shape[0], dtype=jnp.int32)
    return jnp.sum(
        jnp.where(wanted[None, :] == target_block[:, None], slot_iota[None, :], 0), axis=1
    )


def shards(query_embed, positive_ids, pair_blocks, code_ids, codebooks):
    rep_count = lax.axis_size("rep")
    here_blk = lax.axis_index(BLK)
    here_rep = lax.axis_index("rep")
    rows_mine = query_embed[0, 0]
    wanted = pair_blocks[0]
    pair_count = wanted.shape[0]
    feat_count = rows_mine.shape[1]
    block_rows = PR * rep_count
    local_codes = code_ids[0, 0]
    unit, inverse = unit_rows(local_codes, codebooks)
    unit_bf = unit.astype(jnp.bfloat16)
    directory = gather_directly(pair_blocks, BLK, 0)
    owner_count = directory.shape[0]
    local_iota = jnp.arange(PBLK_DEV, dtype=jnp.int32)
    named = jnp.sum(
        (directory[:, :, None] == here_blk * PBLK_DEV + local_iota[None, None, :]).astype(
            jnp.int32
        ),
        axis=1,
    )
    earlier_named = jnp.cumsum(named, axis=1) - named
    cap_iota = jnp.arange(CAP, dtype=jnp.int32)
    selector = (named[:, None, :] > 0) & (earlier_named[:, None, :] == cap_iota[None, :, None])
    outbound = jnp.einsum(
        "bkj,jie->bkie",
        selector.astype(jnp.bfloat16),
        unit_bf.reshape(PBLK_DEV, PR, feat_count),
        preferred_element_type=jnp.float32,
    ).astype(jnp.bfloat16)
    arrived = lax.all_to_all(outbound, BLK, split_axis=0, concat_axis=0, tiled=True)
    owner_of = wanted // PBLK_DEV
    within_of = wanted % PBLK_DEV
    before_me = jnp.sum(
        (
            (owner_of[None, :] == owner_of[:, None]) & (within_of[None, :] < within_of[:, None])
        ).astype(jnp.int32),
        axis=1,
    )
    slot_index = owner_of * CAP + before_me
    fetched = jnp.take(arrived.reshape(owner_count * CAP, PR, feat_count), slot_index, axis=0)
    every_row = gather_directly(rows_mine, "rep", 0)
    all_targets = positive_ids[0].reshape(-1)
    row_in = all_targets % block_rows
    target_slot = find_slot(wanted, all_targets // block_rows)
    target_col = jnp.where(row_in // PR == here_rep, target_slot * PR + row_in % PR, -1)
    grouped = group_view(fetched)
    partial_stats = column_stats(every_row, grouped, target_col)
    peak_all, total_all, hit_all = combined_all(partial_stats, "rep", merge_partials)
    lse = peak_all + jnp.log(total_all)
    query_loss = lax.dynamic_slice_in_dim(
        lse - hit_all, here_rep * rows_mine.shape[0], rows_mine.shape[0]
    )
    grad_rows, grad_cols = column_grads(every_row, grouped, target_col, lse)
    query_grad = sent_and_summed(grad_rows, "rep", 0)
    quarter_grad = grad_cols.reshape(pair_count, PR, feat_count)
    backward = (
        jnp.zeros((owner_count * CAP, PR, feat_count), jnp.float32).at[slot_index].set(quarter_grad)
    )
    returned = lax.all_to_all(
        backward.reshape(owner_count, CAP, PR, feat_count).astype(jnp.bfloat16),
        BLK,
        split_axis=0,
        concat_axis=0,
        tiled=True,
    ).astype(jnp.float32)
    unit_grad = jnp.einsum(
        "bkj,bkie->jie", selector.astype(jnp.float32), returned, precision=lax.Precision.HIGHEST
    ).reshape(PBLK_DEV * PR, feat_count)
    passage_grad = inverse * (unit_grad - unit * jnp.sum(unit * unit_grad, axis=1, keepdims=True))
    share_rows = codebooks.shape[0] // (owner_count * rep_count)
    row_ids = jnp.arange(share_rows * lax.axis_size(BLK_REP), dtype=jnp.int32)
    book_of = row_ids // CODES
    code_of = row_ids % CODES
    picked = jnp.take(local_codes, book_of, axis=0)
    member = (picked == code_of[:, None]).astype(jnp.float32)
    codebook_grad = sum_in_two_steps(
        jnp.dot(member, passage_grad, precision=lax.Precision.HIGHEST).astype(jnp.bfloat16),
        (("blk_0", "blk_1"), ("blk_2", "rep")),
        0,
    )
    return (query_loss[None, None], query_grad[None, None], passage_grad[None, None], codebook_grad)


def solution(mesh):
    torus = Mesh(
        mesh.devices.reshape(4, 8, 2, mesh.shape["rep"]), ("blk_0", "blk_1", "blk_2", "rep")
    )
    in_specs = (
        P(BLK, "rep", None, None),
        P(BLK, None, None),
        P(BLK, None),
        P(BLK, "rep", None, None),
        P(),
    )
    out_specs = (
        P(BLK, "rep", None),
        P(BLK, "rep", None, None),
        P(BLK, "rep", None, None),
        P(BLK_REP, None),
    )
    return jax.shard_map(
        shards, mesh=torus, in_specs=in_specs, out_specs=out_specs, check_vma=False
    )
```

profile of v0, /device:TPU:32, one launch (start us, length us, event | category | flops | bytes accessed | tf_op | source)
XLA Modules:
  0.0 237.1 jit_solution(17036860873164268734)
XLA Ops:
  0.6 1.4 broadcast_in_dim.118
  2.0 11.6 %all-to-all-start = ((s32[64,1,64]{2,1,0:T(1,128)}), s32[64,1,64]{2,1,0:T(1,128)S(1)}, u32[]{:S(2)}, u32[]{:S(2)}) async-start(s32[64,1,64]{2,1,0:T(1,128)} %broadcast_in_dim.118), calls=%async_computation | async-start | bytes 65536 | tf_op jit(solution)/shard_map/all_to_all | solution.py:20
  13.6 1.0 slice_bitcast_fusion
  15.8 6.3 %all-to-all-done = s32[64,1,64]{2,1,0:T(1,128)S(1)} async-done(((s32[64,1,64]{2,1,0:T(1,128)}), s32[64,1,64]{2,1,0:T(1,128)S(1)}, u32[]{:S(2)}, u32[]{:S(2)}) %all-to-all-start) | async-done | bytes 16416 | tf_op jit(solution)/shard_map/all_to_all | solution.py:20
  22.9 1.6 copy.32
  24.5 5.5 %all-to-all-start.1 = ((bf16[64,2,16,256]{3,2,1,0:T(8,128)(2,1)}), bf16[64,2,16,256]{3,2,1,0:T(8,128)(2,1)S(1)}, u32[]{:S(2)}, u32[]{:S(2)}) async-start(bf16[64,2,16,256]{3,2,1,0:T(8,128)(2,1)} %copy.32), calls=%async_computation.1 | async-start | bytes 2097152 | tf_op jit(solution)/shard_map/all_to_all | solution.py:212
  30.5 0.7 fusion.77
  31.7 26.2 %all-to-all-done.1 = bf16[64,2,16,256]{3,2,1,0:T(8,128)(2,1)S(1)} async-done(((bf16[64,2,16,256]{3,2,1,0:T(8,128)(2,1)}), bf16[64,2,16,256]{3,2,1,0:T(8,128)(2,1)S(1)}, u32[]{:S(2)}, u32[]{:S(2)}) %all-to-all-start.1) | async-done | bytes 1048608 | tf_op jit(solution)/shard_map/all_to_all | solution.py:212
  58.0 0.8 broadcast_in_dim.121
  58.8 4.5 %all-to-all-start.2 = ((bf16[4,256,256]{2,1,0:T(8,128)(2,1)}), bf16[4,256,256]{2,1,0:T(8,128)(2,1)S(1)}, u32[]{:S(2)}, u32[]{:S(2)}) async-start(bf16[4,256,256]{2,1,0:T(8,128)(2,1)} %broadcast_in_dim.121), calls=%async_computation.2 | async-start | bytes 1048576 | tf_op jit(solution)/shard_map/all_to_all | solution.py:20
  64.3 8.6 %all-to-all-done.2 = bf16[4,256,256]{2,1,0:T(8,128)(2,1)S(1)} async-done(((bf16[4,256,256]{2,1,0:T(8,128)(2,1)}), bf16[4,256,256]{2,1,0:T(8,128)(2,1)S(1)}, u32[]{:S(2)}, u32[]{:S(2)}) %all-to-all-start.2) | async-done | bytes 524320 | tf_op jit(solution)/shard_map/all_to_all | solution.py:20
  72.9 14.3 %while.28 = (s32[]{:T(128)}, f32[1024]{0:T(1024)S(1)}, f32[1024]{0:T(1024)S(1)}, f32[1024]{0:T(1024)S(1)}, bf16[8,128,256]{2,1,0:T(8,128)(2,1)S(1)}, /*index=5*/...) while((s32[]{:T(128)}, f32[1024]{0:T(1024)S(1)}, ...), condition=%wide.region_9.10_spmd.clone, body=%wide.region_5.9_spmd.clone.sunk | while | flops 67901568 | bytes 1713312 | solution.py:142
  87.2 0.6 broadcast_in_dim.124
  87.8 3.3 %all-to-all-start.3 = ((f32[4,3,1024]{2,1,0:T(4,128)}), f32[4,3,1024]{2,1,0:T(4,128)S(1)}, u32[]{:S(2)}, u32[]{:S(2)}) async-start(f32[4,3,1024]{2,1,0:T(4,128)} %broadcast_in_dim.124), calls=%async_computation.3 | async-start | bytes 131072 | tf_op jit(solution)/shard_map/all_to_all | solution.py:20
  91.1 5.6 %all-to-all-done.3 = f32[4,3,1024]{2,1,0:T(4,128)S(1)} async-done(((f32[4,3,1024]{2,1,0:T(4,128)}), f32[4,3,1024]{2,1,0:T(4,128)S(1)}, u32[]{:S(2)}, u32[]{:S(2)}) %all-to-all-start.3) | async-done | bytes 49184 | tf_op jit(solution)/shard_map/all_to_all | solution.py:20
  97.0 38.9 %while.29 = (s32[]{:T(128)}, f32[1024,256]{1,0:T(8,128)}, f32[8,128,256]{2,1,0:T(8,128)}, bf16[8,128,256]{2,1,0:T(8,128)(2,1)S(1)}, bf16[1024,256]{1,0:T(8,128)(...) while((s32[]{:T(128)}, f32[1024,256]{1,0:T(8,128)}, ...), condition=%wide.region_11.12_spmd.clone, body=%wide.region_10.11_spmd.clone.sunk | while | flops 202506368 | bytes 4203687 | solution.py:164
  98.5 1.3 convolution_add_fusion.2
  99.9 0.9 fusion.107
  102.3 2.5 %convolution_add_fusion.2 = f32[1024,256]{1,0:T(8,128)} fusion(bf16[1024,128]{0,1:T(8,128)(2,1)S(1)} %fusion.106, f32[1024,256]{1,0:T(8,128)} %get-tuple-element.379, pred[]{:T(512)S(6)} %compare.53, bf16[8,128,256]{2,1,0:T(8,128)(2,1)S(1)} %get-tuple-element.392, s32[]{:T(128)S(6)} %copy.79), kind=kOutput, calls=%fused_computation.19.clone.1 | convolution fusion | flops 67633152 | bytes 2424837 | tf_op jit(solution)/shard_map/while/body/eval_jaxpr/dot_general | solution.py:156
  104.9 0.9 fusion.107
  107.4 2.5 %convolution_add_fusion.2 = f32[1024,256]{1,0:T(8,128)} fusion(bf16[1024,128]{0,1:T(8,128)(2,1)S(1)} %fusion.106, f32[1024,256]{1,0:T(8,128)} %get-tuple-element.379, pred[]{:T(512)S(6)} %compare.53, bf16[8,128,256]{2,1,0:T(8,128)(2,1)S(1)} %get-tuple-element.392, s32[]{:T(128)S(6)} %copy.79), kind=kOutput, calls=%fused_computation.19.clone.1 | convolution fusion | flops 67633152 | bytes 2424837 | tf_op jit(solution)/shard_map/while/body/eval_jaxpr/dot_general | solution.py:156
  109.9 0.9 fusion.107
  112.4 2.5 %convolution_add_fusion.2 = f32[1024,256]{1,0:T(8,128)} fusion(bf16[1024,128]{0,1:T(8,128)(2,1)S(1)} %fusion.106, f32[1024,256]{1,0:T(8,128)} %get-tuple-element.379, pred[]{:T(512)S(6)} %compare.53, bf16[8,128,256]{2,1,0:T(8,128)(2,1)S(1)} %get-tuple-element.392, s32[]{:T(128)S(6)} %copy.79), kind=kOutput, calls=%fused_computation.19.clone.1 | convolution fusion | flops 67633152 | bytes 2424837 | tf_op jit(solution)/shard_map/while/body/eval_jaxpr/dot_general | solution.py:156
  114.9 0.9 fusion.107
  117.4 2.5 %convolution_add_fusion.2 = f32[1024,256]{1,0:T(8,128)} fusion(bf16[1024,128]{0,1:T(8,128)(2,1)S(1)} %fusion.106, f32[1024,256]{1,0:T(8,128)} %get-tuple-element.379, pred[]{:T(512)S(6)} %compare.53, bf16[8,128,256]{2,1,0:T(8,128)(2,1)S(1)} %get-tuple-element.392, s32[]{:T(128)S(6)} %copy.79), kind=kOutput, calls=%fused_computation.19.clone.1 | convolution fusion | flops 67633152 | bytes 2424837 | tf_op jit(solution)/shard_map/while/body/eval_jaxpr/dot_general | solution.py:156
  119.9 0.9 fusion.107
  122.4 2.5 %convolution_add_fusion.2 = f32[1024,256]{1,0:T(8,128)} fusion(bf16[1024,128]{0,1:T(8,128)(2,1)S(1)} %fusion.106, f32[1024,256]{1,0:T(8,128)} %get-tuple-element.379, pred[]{:T(512)S(6)} %compare.53, bf16[8,128,256]{2,1,0:T(8,128)(2,1)S(1)} %get-tuple-element.392, s32[]{:T(128)S(6)} %copy.79), kind=kOutput, calls=%fused_computation.19.clone.1 | convolution fusion | flops 67633152 | bytes 2424837 | tf_op jit(solution)/shard_map/while/body/eval_jaxpr/dot_general | solution.py:156
  124.9 0.9 fusion.107
  127.4 2.5 %convolution_add_fusion.2 = f32[1024,256]{1,0:T(8,128)} fusion(bf16[1024,128]{0,1:T(8,128)(2,1)S(1)} %fusion.106, f32[1024,256]{1,0:T(8,128)} %get-tuple-element.379, pred[]{:T(512)S(6)} %compare.53, bf16[8,128,256]{2,1,0:T(8,128)(2,1)S(1)} %get-tuple-element.392, s32[]{:T(128)S(6)} %copy.79), kind=kOutput, calls=%fused_computation.19.clone.1 | convolution fusion | flops 67633152 | bytes 2424837 | tf_op jit(solution)/shard_map/while/body/eval_jaxpr/dot_general | solution.py:156
  129.9 0.9 fusion.107
  132.4 2.5 %convolution_add_fusion.2 = f32[1024,256]{1,0:T(8,128)} fusion(bf16[1024,128]{0,1:T(8,128)(2,1)S(1)} %fusion.106, f32[1024,256]{1,0:T(8,128)} %get-tuple-element.379, pred[]{:T(512)S(6)} %compare.53, bf16[8,128,256]{2,1,0:T(8,128)(2,1)S(1)} %get-tuple-element.392, s32[]{:T(128)S(6)} %copy.79), kind=kOutput, calls=%fused_computation.19.clone.1 | convolution fusion | flops 67633152 | bytes 2424837 | tf_op jit(solution)/shard_map/while/body/eval_jaxpr/dot_general | solution.py:156
  134.9 0.9 fusion.107
  136.1 6.2 %scatter_fusion = f32[128,16,256]{2,1,0:T(8,128)S(1)} fusion(f32[128,16,256]{2,1,0:T(8,128)S(1)} %broadcast_in_dim.129, s32[64]{0:T(128)S(1)} %fusion.72, f32[64,16,256]{2,1,0:T(8,128)} %bitcast.169), kind=kCustom, calls=%fused_computation.2 | custom fusion | bytes 3145984 | tf_op jit(solution)/shard_map/scatter | solution.py:239
  142.4 2.1 copy.34
  144.6 6.8 %all-to-all-start.5 = ((bf16[64,2,16,256]{3,1,2,0:T(2,128)(2,1)}), bf16[64,2,16,256]{3,1,2,0:T(2,128)(2,1)S(1)}, u32[]{:S(2)}, u32[]{:S(2)}) async-start(bf16[64,2,16,256]{3,1,2,0:T(2,128)(2,1)} %copy.34), calls=%async_computation.5 | async-start | bytes 2097152 | tf_op jit(solution)/shard_map/all_to_all | solution.py:241
  151.5 5.5 %gather_fusion.1 = s32[2048,64]{1,0:T(8,128)S(1)} fusion(s32[8,64]{1,0:T(8,128)S(1)} %bitcast.162, s32[2048]{0:T(1024)S(1)} %broadcast_clamp_fusion), kind=kCustom, calls=%fused_computation.1 | custom fusion | bytes 1056768 | tf_op jit(solution)/shard_map/jit(_take)/gather | solution.py:256
  156.9 22.3 %all-to-all-done.5 = bf16[64,2,16,256]{3,1,2,0:T(2,128)(2,1)S(1)} async-done(((bf16[64,2,16,256]{3,1,2,0:T(2,128)(2,1)}), bf16[64,2,16,256]{3,1,2,0:T(2,128)(2,1)S(1)}, u32[]{:S(2)}, u32[]{:S(2)}) %all-to-all-start.5) | async-done | bytes 1048608 | tf_op jit(solution)/shard_map/all_to_all | solution.py:241
  179.3 1.2 convolution_bitcast_fusion.1
  180.8 2.4 %convolution_convert_fusion = bf16[2048,256]{1,0:T(8,128)(2,1)S(1)} fusion(f32[64,256]{1,0:T(8,128)S(1)} %fusion.28, s32[2048,64]{1,0:T(8,128)S(1)} %gather_fusion.1, s32[2048]{0:T(1024)S(1)} %fusion.39, pred[2048]{0:T(1024)(128)(4,1)S(1)} %fusion.48), kind=kOutput, calls=%fused_computation.34 | convolution fusion | flops 403439616 | bytes 1648640 | tf_op jit(solution)/shard_map/dot_general | solution.py:259
  183.3 17.7 %all_to_all.40 = bf16[8,32,8,256]{3,2,1,0:T(8,128)(2,1)S(1)} all-to-all(bf16[8,32,8,256]{3,2,1,0:T(8,128)(2,1)S(1)} %bitcast.166), channel_id=1, replica_groups=mesh['blk_0'=4,'blk_1'=8,'blk_2'=2,'rep'=4] {'blk_2','rep'}, dimensions={0} | all-to-all | bytes 2097152 | tf_op jit(solution)/shard_map/all_to_all | solution.py:78
  201.0 3.5 %all-to-all-start.4 = ((f32[4,256,256]{2,1,0:T(8,128)}), f32[4,256,256]{2,1,0:T(8,128)S(1)}, u32[]{:S(2)}, u32[]{:S(2)}) async-start(f32[4,256,256]{2,1,0:T(8,128)} %bitcast.30), calls=%async_computation.4 | async-start | bytes 2097152 | tf_op jit(solution)/shard_map/all_to_all | solution.py:72
  204.5 0.8 reduce_sum.105
  205.3 14.9 %all-to-all-done.4 = f32[4,256,256]{2,1,0:T(8,128)S(1)} async-done(((f32[4,256,256]{2,1,0:T(8,128)}), f32[4,256,256]{2,1,0:T(8,128)S(1)}, u32[]{:S(2)}, u32[]{:S(2)}) %all-to-all-start.4) | async-done | bytes 1048608 | tf_op jit(solution)/shard_map/all_to_all | solution.py:72
  220.2 6.5 %all-to-all-start.7 = ((bf16[32,8,256]{2,1,0:T(8,128)(2,1)}), bf16[32,8,256]{2,1,0:T(8,128)(2,1)S(1)}, u32[]{:S(2)}, u32[]{:S(2)}) async-start(bf16[32,8,256]{2,1,0:T(8,128)(2,1)} %reduce_sum.105), calls=%async_computation.7 | async-start | bytes 262144 | tf_op jit(solution)/shard_map/all_to_all | solution.py:86
  226.8 0.6 dynamic_slice.17
  227.4 0.8 reduce_sum.103
  228.2 8.2 %all-to-all-done.7 = bf16[32,8,256]{2,1,0:T(8,128)(2,1)S(1)} async-done(((bf16[32,8,256]{2,1,0:T(8,128)(2,1)}), bf16[32,8,256]{2,1,0:T(8,128)(2,1)S(1)}, u32[]{:S(2)}, u32[]{:S(2)}) %all-to-all-start.7) | async-done | bytes 131104 | tf_op jit(solution)/shard_map/all_to_all | solution.py:86
  236.4 0.6 convert_reduce_fusion
  (157 shorter events, 20.9 us)
Async XLA Ops:
  0.6 14.7 %copy-start = (bf16[2048,256]{1,0:T(8,128)(2,1)S(1)}, bf16[2048,256]{1,0:T(8,128)(2,1)}, u32[]{:S(2)}) copy-start(bf16[2048,256]{1,0:T(8,128)(2,1)} %param.13) | copy-start | bytes 3145732
  2.0 20.1 %all-to-all-start = ((s32[64,1,64]{2,1,0:T(1,128)}), s32[64,1,64]{2,1,0:T(1,128)S(1)}, u32[]{:S(2)}, u32[]{:S(2)}) async-start(s32[64,1,64]{2,1,0:T(1,128)} %broadcast_in_dim.118), calls=%async_computation | async-start | bytes 65536 | tf_op jit(solution)/shard_map/all_to_all | solution.py:20
  22.9 7.6 %copy-start.4 = (s32[1,64]{1,0:T(1,128)S(1)}, s32[1,64]{1,0:T(1,128)}, u32[]{:S(2)}) copy-start(s32[1,64]{1,0:T(1,128)} %param.11) | copy-start | bytes 772
  22.9 8.6 %copy-start.5 = (s32[1,4,256]{2,1,0:T(4,128)S(1)}, s32[1,4,256]{2,1,0:T(4,128)}, u32[]{:S(2)}) copy-start(s32[1,4,256]{2,1,0:T(4,128)} %param.10) | copy-start | bytes 12292
  22.9 35.1 %copy-start.3 = (bf16[1,1,256,256]{3,2,1,0:T(8,128)(2,1)S(1)}, bf16[1,1,256,256]{3,2,1,0:T(8,128)(2,1)}, u32[]{:S(2)}) copy-start(bf16[1,1,256,256]{3,2,1,0:T(8,128)(2,1)} %param.9) | copy-start | bytes 393220
  24.5 33.5 %all-to-all-start.1 = ((bf16[64,2,16,256]{3,2,1,0:T(8,128)(2,1)}), bf16[64,2,16,256]{3,2,1,0:T(8,128)(2,1)S(1)}, u32[]{:S(2)}, u32[]{:S(2)}) async-start(bf16[64,2,16,256]{3,2,1,0:T(8,128)(2,1)} %copy.32), calls=%async_computation.1 | async-start | bytes 2097152 | tf_op jit(solution)/shard_map/all_to_all | solution.py:212
  58.8 14.1 %all-to-all-start.2 = ((bf16[4,256,256]{2,1,0:T(8,128)(2,1)}), bf16[4,256,256]{2,1,0:T(8,128)(2,1)S(1)}, u32[]{:S(2)}, u32[]{:S(2)}) async-start(bf16[4,256,256]{2,1,0:T(8,128)(2,1)} %broadcast_in_dim.121), calls=%async_computation.2 | async-start | bytes 1048576 | tf_op jit(solution)/shard_map/all_to_all | solution.py:20
  87.8 8.9 %all-to-all-start.3 = ((f32[4,3,1024]{2,1,0:T(4,128)}), f32[4,3,1024]{2,1,0:T(4,128)S(1)}, u32[]{:S(2)}, u32[]{:S(2)}) async-start(f32[4,3,1024]{2,1,0:T(4,128)} %broadcast_in_dim.124), calls=%async_computation.3 | async-start | bytes 131072 | tf_op jit(solution)/shard_map/all_to_all | solution.py:20
  142.4 9.0 %copy-start.1 = (s32[1,1,8,64]{3,2,1,0:T(8,128)S(1)}, s32[1,1,8,64]{3,2,1,0:T(8,128)}, u32[]{:S(2)}) copy-start(s32[1,1,8,64]{3,2,1,0:T(8,128)} %param.12) | copy-start | bytes 6148
  144.6 34.7 %all-to-all-start.5 = ((bf16[64,2,16,256]{3,1,2,0:T(2,128)(2,1)}), bf16[64,2,16,256]{3,1,2,0:T(2,128)(2,1)S(1)}, u32[]{:S(2)}, u32[]{:S(2)}) async-start(bf16[64,2,16,256]{3,1,2,0:T(2,128)(2,1)} %copy.34), calls=%async_computation.5 | async-start | bytes 2097152 | tf_op jit(solution)/shard_map/all_to_all | solution.py:241
  180.8 2.5 %copy-start.2 = (f32[64,256]{1,0:T(8,128)}, f32[64,256]{1,0:T(8,128)S(1)}, u32[]{:S(2)}) copy-start(f32[64,256]{1,0:T(8,128)S(1)} %fusion.28) | copy-start | bytes 196612
  201.0 19.2 %all-to-all-start.4 = ((f32[4,256,256]{2,1,0:T(8,128)}), f32[4,256,256]{2,1,0:T(8,128)S(1)}, u32[]{:S(2)}, u32[]{:S(2)}) async-start(f32[4,256,256]{2,1,0:T(8,128)} %bitcast.30), calls=%async_computation.4 | async-start | bytes 2097152 | tf_op jit(solution)/shard_map/all_to_all | solution.py:72
  220.2 16.2 %all-to-all-start.7 = ((bf16[32,8,256]{2,1,0:T(8,128)(2,1)}), bf16[32,8,256]{2,1,0:T(8,128)(2,1)S(1)}, u32[]{:S(2)}, u32[]{:S(2)}) async-start(bf16[32,8,256]{2,1,0:T(8,128)(2,1)} %reduce_sum.105), calls=%async_computation.7 | async-start | bytes 262144 | tf_op jit(solution)/shard_map/all_to_all | solution.py:86
where the time goes:
time: 238 us; the launch traced here: 237 us
  waiting for transfers between devices  92.1 us (39%)
  starting transfers between devices  41.7 us (18%)
  matrix products  35.8 us (15%)
  local copies, waits for them, and re-layouts  31.2 us (13%)
  blocking collectives  17.7 us (7%)
  loops' own time  11.1 us (5%)
  other arithmetic  6.37 us (3%)
    all_to_all x1, waiting for transfers between devices, shards(): lax.all_to_all(outbound, BLK, split_axis=0, concat_axis=0, tiled=True)  26.2 us
    all_to_all x1, waiting for transfers between devices, shards(): lax.all_to_all(backward.reshape(owner_count, CAP, PR, feat_count).astype(...  22.3 us
    all_to_all x3, waiting for transfers between devices, from_everyone(): lax.all_to_all(jnp.broadcast_to(x[None], (count, *x.shape)), axis, 0, 0,...  20.5 us
    all_to_all x3, starting transfers between devices, from_everyone(): lax.all_to_all(jnp.broadcast_to(x[None], (count, *x.shape)), axis, 0, 0,...  19.3 us
    dot_general x8, matrix products, visit(): jnp.dot(weight, group_rows, preferred_element_type=jnp.float32)  19.2 us
    all_to_all x1, blocking collectives, sum_at_owner(): lax.all_to_all(tiles, axis, split_axis=0, concat_axis=0, tiled=True)  17.7 us
    all_to_all x1, waiting for transfers between devices, sent_and_summed(): tiles = lax.all_to_all(split_up(x, dim, count), axis, 0, 0, tiled=True)  14.9 us
    dynamic_slice x16, local copies, waits for them, and re-layouts, column_stats(): result, unused = lax.scan(visit, start, (group_ids, grouped))  9.37 us
  transfers between devices with their start and end apart: 7, of which 7 were waited for; matrix products, arithmetic and copies ran while one was open for 5% of the time, Pallas kernels for 0%

commit v1 on v0

v1 whole, which is shorter than its diff:
```python
import jax
import jax.numpy as jnp
from jax import lax
from jax.experimental import pallas as pl
from jax.experimental.pallas import tpu as pltpu
from jax.sharding import Mesh
from jax.sharding import PartitionSpec as P


CODES = 256
BOOKS = 8
PR = 16
PBLK_DEV = 4
CAP = 2
LANES = 128
AXES = ("x", "z", "c", "rep")
BLK = ("x", "z", "c")
EPS = 1e-06
INTERPRET = False
VMEM_LIMIT = 24 << 20

F32 = jnp.float32
BF16 = jnp.bfloat16
VMEM = pl.BlockSpec(memory_space=pltpu.VMEM)
SMEM = pl.BlockSpec(memory_space=pltpu.SMEM)
CONTRACT_LAST = (((1,), (1,)), ((), ()))
CONTRACT_FIRST = (((0,), (0,)), ((), ()))


def call(kernel, out_shape, scratch, smem_count, vmem_count, flops):
    out_bytes = sum(s.size * s.dtype.itemsize for s in jax.tree.leaves(out_shape))
    return pl.pallas_call(
        kernel,
        out_shape=out_shape,
        in_specs=[SMEM] * smem_count + [VMEM] * vmem_count,
        out_specs=jax.tree.map(lambda _: VMEM, out_shape),
        scratch_shapes=scratch,
        interpret=INTERPRET,
        compiler_params=pltpu.CompilerParams(vmem_limit_bytes=VMEM_LIMIT),
        cost_estimate=pl.CostEstimate(
            flops=flops, bytes_accessed=2 * out_bytes, transcendentals=0
        ),
    )


def sds(shape, dtype):
    return jax.ShapeDtypeStruct(shape, dtype)


def one_hot_of(codes_ref, book, rows):
    cols = codes_ref.shape[1]
    row = codes_ref[book : book + 1, :]
    iota = lax.broadcasted_iota(jnp.int32, (rows, cols), 0).astype(F32)
    return jnp.where(row == iota, 1.0, 0.0).astype(BF16)


def fill_keys(pair_s, key_ref, pair_count):
    sub = lax.broadcasted_iota(jnp.int32, (PR, LANES), 0)
    for slot in range(pair_count):
        key_ref[slot * PR : (slot + 1) * PR, :] = sub + pair_s[slot] * PR


def hits(key_ref, start, count, tkey_ref):
    keys = key_ref[start : start + count, :]
    width = tkey_ref.shape[1]
    wide = jnp.concatenate([keys] * (width // LANES), axis=1)
    return wide == tkey_ref[...]


def stats_kernel(
    pair_s, place_s, recv_ref, q0, q1, q2, q3, tkey_ref, cbt_ref,
    u_ref, q_ref, st_ref, codes_ref, rows_ref, key_ref,
):
    cols = u_ref.shape[0]
    pair_count = cols // PR
    rep = place_s[3]
    rows = q0.shape[0]
    parts = (q0, q1, q2, q3)
    for k in range(len(parts)):
        owner = lax.rem(rep + len(parts) - k, len(parts))
        q_ref[pl.ds(pl.multiple_of(owner * rows, rows), rows), :] = parts[k][...]
    rows_ref[...] = recv_ref[...].astype(F32)
    lane_group = lax.broadcasted_iota(jnp.int32, (BOOKS, LANES), 1) // PR
    per_tile = LANES // PR
    for tile in range(cols // LANES):
        held = jnp.zeros((BOOKS, LANES), F32)
        for place in range(per_tile):
            block = pair_s[tile * per_tile + place]
            owner = block >> 2
            within = block & 3
            codes = rows_ref[pl.ds(pl.multiple_of(owner * BOOKS, BOOKS), BOOKS), :]
            turned = pltpu.roll(codes, lax.rem(LANES + (place - within) * PR, LANES), axis=1)
            held = jnp.where(lane_group == place, turned, held)
        codes_ref[:, tile * LANES : (tile + 1) * LANES] = held
    fill_keys(pair_s, key_ref, pair_count)
    quant = jnp.zeros((cbt_ref.shape[0], cols), F32)
    for book in range(BOOKS):
        quant = quant + jnp.dot(
            cbt_ref[:, book * CODES : (book + 1) * CODES],
            one_hot_of(codes_ref, book, CODES),
            preferred_element_type=F32,
        )
    inverse = lax.rsqrt(jnp.sum(quant * quant, axis=0, keepdims=True) + EPS)
    u_ref[...] = (quant * inverse).T.astype(BF16)
    total_rows = q_ref.shape[0]
    peak = jnp.full((1, total_rows), -1e30, F32)
    total = jnp.zeros((1, total_rows), F32)
    hit = jnp.zeros((1, total_rows), F32)
    step = min(256, cols)
    for start in range(0, cols, step):
        scores = lax.dot_general(
            u_ref[start : start + step, :], q_ref[...], CONTRACT_LAST, preferred_element_type=F32
        )
        fresh = jnp.maximum(peak, jnp.max(scores, axis=0, keepdims=True))
        total = total * jnp.exp(peak - fresh) + jnp.sum(
            jnp.exp(scores - fresh), axis=0, keepdims=True
        )
        peak = fresh
        hit = hit + jnp.sum(
            jnp.where(hits(key_ref, start, step, tkey_ref), scores, 0.0), axis=0, keepdims=True
        )
    st_ref[0:1, :] = peak
    st_ref[1:2, :] = total
    st_ref[2:3, :] = hit
    st_ref[3:8, :] = jnp.zeros((5, total_rows), F32)


def merged(first, second):
    peak = jnp.maximum(first[0:1], second[0:1])
    total = first[1:2] * jnp.exp(first[0:1] - peak) + second[1:2] * jnp.exp(second[0:1] - peak)
    return peak, total, first[2:3] + second[2:3]


def grads_kernel(
    pair_s, slot_s, place_s, sta_ref, stb_ref, tkey_ref, u_ref, q_ref,
    send_ref, g_ref, loss_ref, own_ref, far1, far2, far3, key_ref, lse_ref, qgt_ref,
):
    cols = u_ref.shape[0]
    pair_count = cols // PR
    rep = place_s[3]
    rows = own_ref.shape[1]
    peak, total, hit = merged(sta_ref[...], stb_ref[...])
    lse = peak + jnp.log(total)
    lse_ref[0:1, :] = lse - hit
    loss_ref[...] = lse_ref[0:1, pl.ds(pl.multiple_of(rep * rows, rows), rows)]
    fill_keys(pair_s, key_ref, pair_count)
    send_ref[...] = jnp.zeros(send_ref.shape, BF16)
    step = min(256, cols)
    grown = None
    for start in range(0, cols, step):
        u_part = u_ref[start : start + step, :]
        scores = lax.dot_general(u_part, q_ref[...], CONTRACT_LAST, preferred_element_type=F32)
        hit_mask = hits(key_ref, start, step, tkey_ref)
        weight = (jnp.exp(scores - lse) - jnp.where(hit_mask, 1.0, 0.0)).astype(BF16)
        grad = jnp.dot(weight, q_ref[...], preferred_element_type=F32)
        g_ref[start : start + step, :] = grad
        narrow = grad.astype(BF16)
        for place in range(step // PR):
            send_ref[slot_s[start // PR + place]] = narrow[place * PR : (place + 1) * PR, :]
        term = lax.dot_general(u_part, weight, CONTRACT_FIRST, preferred_element_type=F32)
        grown = term if grown is None else grown + term
    qgt_ref[...] = grown
    count = q_ref.shape[0] // rows
    for k, out in enumerate((own_ref, far1, far2, far3)):
        owner = lax.rem(rep + k, count)
        part = qgt_ref[:, pl.ds(pl.multiple_of(owner * rows, rows), rows)]
        out[...] = part.astype(out.dtype)


def books_kernel(place_s, codes_ref, cbt_ref, g_ref, keep_ref, send_ref, hot_ref, sum_ref):
    cols = codes_ref.shape[1]
    core = place_s[2]
    quant = jnp.zeros((cbt_ref.shape[0], cols), F32)
    for book in range(BOOKS):
        hot_ref[book] = one_hot_of(codes_ref, book, CODES)
        quant = quant + jnp.dot(
            cbt_ref[:, book * CODES : (book + 1) * CODES],
            hot_ref[book],
            preferred_element_type=F32,
        )
    inverse = lax.rsqrt(jnp.sum(quant * quant, axis=0, keepdims=True) + EPS)
    unit = quant * inverse
    grad = g_ref[...].T
    grad = inverse * (grad - unit * jnp.sum(unit * grad, axis=0, keepdims=True))
    narrow = grad.astype(BF16)
    for book in range(BOOKS):
        sum_ref[book * CODES : (book + 1) * CODES, :] = lax.dot_general(
            hot_ref[book], narrow, CONTRACT_LAST, preferred_element_type=F32
        )
    half = keep_ref.shape[1]
    for chunk in range(keep_ref.shape[0]):
        base = chunk * 2 * half
        keep_ref[chunk] = sum_ref[pl.ds(pl.multiple_of(base + core * half, half), half), :]
        send_ref[chunk] = sum_ref[
            pl.ds(pl.multiple_of(base + (1 - core) * half, half), half), :
        ].astype(BF16)


def x_order(here, count):
    if count == 4:
        return (here, 3 - here, here ^ 1, 3 - (here ^ 1))
    return tuple(here ^ k for k in range(count))


def deal_kernel(place_s, keep_ref, recv_ref, own_ref, far1, far2, far3, sum_ref):
    x_here, z_here, rep = place_s[0], place_s[1], place_s[3]
    x_count, z_count, reps = place_sizes(own_ref, keep_ref)
    share = keep_ref.shape[1] // reps
    sum_ref[...] = keep_ref[...] + recv_ref[...].astype(F32)
    order = x_order(x_here, x_count)
    for k, out in enumerate((own_ref, far1, far2, far3)):
        owner = lax.rem(rep + k, reps)
        at = pl.ds(pl.multiple_of(owner * share, share), share)
        for px in range(x_count):
            for pz in range(z_count):
                chunk = order[px] * z_count + (z_here ^ pz)
                out[px * z_count + pz] = sum_ref[chunk, at, :].astype(out.dtype)


def place_sizes(own_ref, keep_ref):
    chunks = keep_ref.shape[0]
    x_count = 4
    return x_count, chunks // x_count, keep_ref.shape[1] // own_ref.shape[1]


def return_kernel(slot_j, ret_ref, unit_ref, inv_ref, out_ref, *sums):
    for part in sums:
        part[...] = jnp.zeros(part.shape, F32)
    for slot in range(ret_ref.shape[0]):
        part = sums[slot % len(sums)]
        j = slot_j[slot]
        part[j] = part[j] + ret_ref[slot].astype(F32)
    for j in range(PBLK_DEV):
        grad = sums[0][j]
        for part in sums[1:]:
            grad = grad + part[j]
        unit = unit_ref[j * PR : (j + 1) * PR, :]
        inverse = inv_ref[j * PR : (j + 1) * PR, 0:1]
        out_ref[j * PR : (j + 1) * PR, :] = inverse * (
            grad - unit * jnp.sum(unit * grad, axis=1, keepdims=True)
        )


def unit_rows(local_codes, codebooks):
    iota = jnp.arange(CODES, dtype=jnp.int32)
    pieces = [
        (local_codes[book][:, None] == iota[None, :]).astype(BF16)
        for book in range(local_codes.shape[0])
    ]
    quant = jnp.dot(jnp.concatenate(pieces, axis=1), codebooks, preferred_element_type=F32)
    inverse = lax.rsqrt(jnp.sum(quant * quant, axis=1, keepdims=True) + EPS)
    return (quant * inverse, inverse)


def shifted(x, k):
    count = lax.axis_size("rep")
    return lax.ppermute(x, "rep", [(i, (i + k) % count) for i in range(count)])


def halved(own, axis, partner):
    half = own.shape[0] // 2
    pairs = [(i, partner(i)) for i in range(lax.axis_size(axis))]
    arrived = lax.ppermute(own[half:].astype(BF16), axis, pairs)
    return own[:half] + arrived.astype(F32)


def shards(query_embed, positive_ids, pair_blocks, code_ids, codebooks):
    reps = lax.axis_size("rep")
    x_count, z_count, cores = (lax.axis_size(a) for a in BLK)
    owners = x_count * z_count * cores
    here_blk = lax.axis_index(BLK)
    here_rep = lax.axis_index("rep")
    rows_mine = query_embed[0, 0]
    row_count, feat = rows_mine.shape
    all_rows = reps * row_count
    wanted = pair_blocks[0]
    pair_count = wanted.shape[0]
    cols = pair_count * PR
    local_codes = code_ids[0, 0]
    place = jnp.stack([lax.axis_index(a) for a in AXES]).astype(jnp.int32)

    held = local_codes.shape[1]
    listed = jnp.broadcast_to(
        jnp.pad(wanted, (0, LANES - held - pair_count))[None, :], (BOOKS, LANES - held)
    )
    message = jnp.concatenate([local_codes, listed], axis=1).astype(BF16)
    message = jnp.broadcast_to(message[None], (owners, BOOKS, LANES))
    arrived = lax.all_to_all(message, BLK, 0, 0, tiled=True)
    query_parts = [rows_mine] + [shifted(rows_mine, k) for k in range(1, reps)]

    targets = positive_ids[0].reshape(1, all_rows)
    row_in = targets % (PR * reps)
    tkey = jnp.where(
        row_in // PR == here_rep, (targets // (PR * reps)) * PR + row_in % PR, -1
    ).astype(jnp.int32)
    owner_of = wanted // PBLK_DEV
    before_me = jnp.sum(
        ((owner_of[None, :] == owner_of[:, None]) & (wanted[None, :] < wanted[:, None])).astype(
            jnp.int32
        ),
        axis=1,
    )
    slot_of = owner_of * CAP + before_me
    turned_books = codebooks.T
    unit, inverse = unit_rows(local_codes, codebooks)
    inverse_wide = jnp.broadcast_to(inverse, (inverse.shape[0], LANES))

    units, queries, stats, codes = call(
        stats_kernel,
        (
            sds((cols, feat), BF16),
            sds((all_rows, feat), BF16),
            sds((8, all_rows), F32),
            sds((BOOKS, cols), F32),
        ),
        [pltpu.VMEM((owners * BOOKS, LANES), F32), pltpu.VMEM((cols, LANES), jnp.int32)],
        2,
        7,
        2 * cols * feat * (BOOKS * CODES + all_rows),
    )(wanted, place, arrived.reshape(owners * BOOKS, LANES), *query_parts, tkey, turned_books)

    near = [(i, i ^ 1) for i in range(reps)]
    cross = [(i, reps - 1 - i) for i in range(reps)]
    peak, total, hit = merged(stats, lax.ppermute(stats, "rep", near))
    stats_two = jnp.concatenate(
        [peak, total, hit, jnp.zeros((5, all_rows), F32)], axis=0
    )
    stats_far = lax.ppermute(stats_two, "rep", cross)

    outbound, grad_cols, loss, own_t, far1, far2, far3 = call(
        grads_kernel,
        (
            sds((owners * CAP, PR, feat), BF16),
            sds((cols, feat), F32),
            sds((1, row_count), F32),
            sds((feat, row_count), F32),
            *[sds((feat, row_count), BF16)] * 3,
        ),
        [
            pltpu.VMEM((cols, LANES), jnp.int32),
            pltpu.VMEM((8, all_rows), F32),
            pltpu.VMEM((feat, all_rows), F32),
        ],
        3,
        5,
        6 * cols * feat * all_rows,
    )(wanted, slot_of, place, stats_two, stats_far, tkey, units, queries)

    outbound = outbound.reshape(owners, CAP * PR, feat)
    returned = lax.all_to_all(outbound, BLK, 0, 0, tiled=True)
    returned = returned.reshape(owners * CAP, PR, feat)

    query_grad_t = own_t
    for k, part in enumerate((far1, far2, far3)):
        query_grad_t = query_grad_t + shifted(part, k + 1).astype(F32)

    chunk_rows = codebooks.shape[0] // (x_count * z_count)
    keep, send = call(
        books_kernel,
        (
            sds((x_count * z_count, chunk_rows // 2, feat), F32),
            sds((x_count * z_count, chunk_rows // 2, feat), BF16),
        ),
        [pltpu.VMEM((BOOKS, CODES, cols), BF16), pltpu.VMEM((BOOKS * CODES, feat), F32)],
        1,
        3,
        4 * cols * feat * BOOKS * CODES,
    )(place, codes, turned_books, grad_cols)
    other = lax.ppermute(send, "c", [(0, 1), (1, 0)])
    share_rows = chunk_rows // 2 // reps
    share = (x_count * z_count, share_rows, feat)
    mine, *parts = call(
        deal_kernel,
        (sds(share, F32), *[sds(share, BF16)] * 3),
        [pltpu.VMEM((x_count * z_count, chunk_rows // 2, feat), F32)],
        1,
        2,
        cols * feat,
    )(place, keep, other)
    for k, part in enumerate(parts):
        mine = mine + shifted(part, k + 1).astype(F32)
    mine = halved(mine, "x", lambda i: i ^ 1)
    mine = halved(mine, "x", lambda i: x_count - 1 - i)
    bit = z_count // 2
    while bit:
        mine = halved(mine, "z", lambda i, bit=bit: i ^ bit)
        bit //= 2
    codebook_grad = mine.reshape(share_rows, feat)

    directory = arrived[:, 0, held : held + pair_count].astype(jnp.int32)
    local_iota = jnp.arange(PBLK_DEV, dtype=jnp.int32)
    named = jnp.any(
        directory[:, :, None] == here_blk * PBLK_DEV + local_iota[None, None, :], axis=1
    )
    slot_j = []
    for k in range(CAP):
        rank = jnp.zeros((owners,), jnp.int32)
        found = jnp.full((owners,), PBLK_DEV, jnp.int32)
        for j in range(PBLK_DEV):
            found = jnp.where(named[:, j] & (rank == k), j, found)
            rank = rank + named[:, j].astype(jnp.int32)
        slot_j.append(found)
    slot_j = jnp.stack(slot_j, axis=1).reshape(-1)
    passage_grad = call(
        return_kernel,
        sds((PBLK_DEV * PR, feat), F32),
        [pltpu.VMEM((PBLK_DEV + 1, PR, feat), F32) for _ in range(4)],
        1,
        3,
        owners * CAP * PR * feat,
    )(slot_j, returned, unit, inverse_wide)
    return (
        loss[None],
        query_grad_t.T[None, None],
        passage_grad[None, None],
        codebook_grad,
    )


def solution(mesh):
    reps = mesh.shape["rep"]
    torus = Mesh(mesh.devices.reshape(4, -1, 2, reps), AXES)
    in_specs = (
        P(BLK, "rep", None, None),
        P(BLK, None, None),
        P(BLK, None),
        P(BLK, "rep", None, None),
        P(),
    )
    out_specs = (
        P(BLK, "rep", None),
        P(BLK, "rep", None, None),
        P(BLK, "rep", None, None),
        P(AXES, None),
    )
    return jax.shard_map(
        shards, mesh=torus, in_specs=in_specs, out_specs=out_specs, check_vma=False
    )
```

time: 238 us -> 104 us (0.44)
  waiting for transfers between devices: 92.1 us -> 36.7 us
  matrix products: 35.8 us -> 0.37 us
  local copies, waits for them, and re-layouts: 31.2 us -> 4.23 us
  blocking collectives: 17.7 us -> 0 us
  Pallas kernels: 0 us -> 13.1 us
  loops' own time: 11.1 us -> 0 us
  other arithmetic: 6.37 us -> 3.02 us
  starting transfers between devices: 41.7 us -> 44.2 us
    all_to_all x7 -> x2, waiting for transfers between devices: 92.1 us -> 6.95 us  [the longest x1 6.95 us: shards(): arrived = lax.all_to_all(message, BLK, 0, 0, tiled=True)]
    dot_general x36 -> x1, matrix products: 35.8 us -> 0.37 us  [unit_rows(): jnp.dot(jnp.concatenate(pieces, axis=1), codebooks, preferred_element_typ...]
    ppermute x0 -> x17, waiting for transfers between devices: none -> 29.7 us  [the longest x5 19.4 us: halved(): arrived = lax.ppermute(own[half:].astype(BF16), axis, pairs)]
    ppermute x0 -> x17, starting transfers between devices: none -> 27.3 us  [the longest x9 13.6 us: shifted(): return lax.ppermute(x, 'rep', [(i, (i + k) % count) for i in range(count)])]
    all_to_all x7 -> x2, starting transfers between devices: 41.7 us -> 16.9 us  [the longest x1 11.7 us: shards(): arrived = lax.all_to_all(message, BLK, 0, 0, tiled=True)]
    all_to_all x1 -> x0, blocking collectives: 17.7 us -> none  [sum_at_owner(): lax.all_to_all(tiles, axis, split_axis=0, concat_axis=0, tiled=True)]
    pallas_call x0 -> x5, Pallas kernels: none -> 13.1 us  [the longest x1 3.9 us: shards(): call(stats_kernel, (sds((cols, feat), BF16), sds((all_rows, feat), BF16),...]
    another operation x2 -> x0, loops' own time: 11.1 us -> none  [the longest x1 5.7 us: column_stats(): result, unused = lax.scan(visit, start, (group_ids, grouped))]
  transfers between devices with their start and end apart: 7 -> 19, of which waited for: 7 -> 11; matrix products, arithmetic and copies ran while one was open for 5% -> 7% of each run, Pallas kernels for 0% -> 0%
where the time goes in v1:
time: 104 us; the launch traced here: 102 us
  starting transfers between devices  44.2 us (42%)
  waiting for transfers between devices  36.7 us (35%)
  Pallas kernels  13.1 us (13%)
  local copies, waits for them, and re-layouts  4.23 us (4%)
  other arithmetic  3.02 us (3%)
    ppermute x5, waiting for transfers between devices, halved(): arrived = lax.ppermute(own[half:].astype(BF16), axis, pairs)  19.4 us
    ppermute x9, starting transfers between devices, shifted(): return lax.ppermute(x, 'rep', [(i, (i + k) % count) for i in range(count)])  13.6 us
    all_to_all x1, starting transfers between devices, shards(): arrived = lax.all_to_all(message, BLK, 0, 0, tiled=True)  11.7 us
    ppermute x5, starting transfers between devices, halved(): arrived = lax.ppermute(own[half:].astype(BF16), axis, pairs)  9.07 us
    all_to_all x1, waiting for transfers between devices, shards(): arrived = lax.all_to_all(message, BLK, 0, 0, tiled=True)  6.95 us
    all_to_all x1, starting transfers between devices, shards(): returned = lax.all_to_all(outbound, BLK, 0, 0, tiled=True)  5.21 us
    ppermute x9, waiting for transfers between devices, shifted(): return lax.ppermute(x, 'rep', [(i, (i + k) % count) for i in range(count)])  4.24 us
    pallas_call x1, Pallas kernels, shards(): call(stats_kernel, (sds((cols, feat), BF16), sds((all_rows, feat), BF16),...  3.9 us
  transfers between devices with their start and end apart: 19, of which 11 were waited for; matrix products, arithmetic and copies ran while one was open for 7% of the time, Pallas kernels for 0%

profile of v1, /device:TPU:32, one launch (start us, length us, event | category | flops | bytes accessed | tf_op | source)
XLA Modules:
  0.0 102.4 jit_solution(14823471044787115643)
XLA Ops:
  0.6 3.1 %collective-permute-start.2 = (bf16[256,256]{1,0:T(8,128)(2,1)}, bf16[256,256]{1,0:T(8,128)(2,1)S(1)}, u32[]{:S(2)}, u32[]{:S(2)}) collective-permute-start(bf16[256,256]{1,0:T(8,128)(2,1)} %bitcast.54), channel_id=1, source_target_pairs={{0,3},{1,0},{2,1},{3,2},{4,7},{5,4},{6,5},{7,6},{8,11},{9,8},{10,9... | collective-permute-start | bytes 393224 | tf_op jit(solution)/shard_map/ppermute | solution.py:257
  3.7 0.6 collective-permute-start.1
  4.4 1.0 collective-permute-start
  5.3 0.7 convert_bitcast_fusion
  6.1 0.7 broadcast_in_dim.25
  6.8 11.7 %all-to-all-start = ((bf16[64,8,128]{2,1,0:T(8,128)(2,1)}), bf16[64,8,128]{2,1,0:T(8,128)(2,1)S(1)}, u32[]{:S(2)}, u32[]{:S(2)}) async-start(bf16[64,8,128]{2,1,0:T(8,128)(2,1)} %broadcast_in_dim.25), calls=%async_computation | async-start | bytes 262144 | tf_op jit(solution)/shard_map/all_to_all | solution.py:288
  18.6 0.7 copy-done.4
  19.4 0.1 fusion.1
  19.5 0.1 fusion.2
  19.6 0.1 fusion.3
  20.0 1.5 %copy.16 = bf16[2048,256]{0,1:T(8,128)(2,1)S(1)} copy(bf16[2048,256]{1,0:T(8,128)(2,1)} %param.9) | data formatting | bytes 2097152 | tf_op args[4]
  21.6 6.9 %all-to-all-done = bf16[64,8,128]{2,1,0:T(8,128)(2,1)S(1)} async-done(((bf16[64,8,128]{2,1,0:T(8,128)(2,1)}), bf16[64,8,128]{2,1,0:T(8,128)(2,1)S(1)}, u32[]{:S(2)}, u32[]{:S(2)}) %all-to-all-start) | async-done | bytes 131104 | tf_op jit(solution)/shard_map/all_to_all | solution.py:288
  28.6 3.9 %shard_map.84 = (bf16[1024,256]{1,0:T(8,128)(2,1)S(1)}, bf16[1024,256]{1,0:T(8,128)(2,1)S(1)}, f32[8,1024]{1,0:T(8,128)S(1)}, f32[8,1024]{1,0:T(8,128)S(1)}) custom-call(s32[64]{0:T(128)S(1)} %bitcast.51, s32[4]{0:T(128)S(1)} %pad_add_fusion.1.place_s, bf16[512,128]{1,0:T(8,128)(2,1)S(1)} %bitcast.50, bf16[256,256]{1,0:T(8,128)(2,1)S(1)} %bitcast.57, ...), custom_call_target="tpu_custom_call" | custom-call | flops 1610612736 | bytes 2228224 | tf_op jit(solution)/shard_map/pallas_call | solution.py:308
  32.5 2.0 %collective-permute-start.3 = (f32[8,1024]{1,0:T(8,128)S(1)}, f32[8,1024]{1,0:T(8,128)S(1)}, u32[]{:S(2)}, u32[]{:S(2)}) collective-permute-start(f32[8,1024]{1,0:T(8,128)S(1)} %get-tuple-element.21), channel_id=1, source_target_pairs={{0,1},{1,0},{2,3},{3,2},{4,5},{5,4},{6,7},{7,6},{8,9},{9,8},{10,11... | collective-permute-start | bytes 98312 | tf_op jit(solution)/shard_map/ppermute | solution.py:324
  34.4 0.2 convert_reduce_fusion
  34.7 1.8 %collective-permute-done.3 = f32[8,1024]{1,0:T(8,128)S(1)} collective-permute-done((f32[8,1024]{1,0:T(8,128)S(1)}, f32[8,1024]{1,0:T(8,128)S(1)}, u32[]{:S(2)}, u32[]{:S(2)}) %collective-permute-start.3) | collective-permute-done | bytes 32800 | tf_op jit(solution)/shard_map/ppermute | solution.py:324
  36.6 2.5 %collective-permute-start.4 = (f32[8,1024]{1,0:T(8,128)S(1)}, f32[8,1024]{1,0:T(8,128)S(1)}, u32[]{:S(2)}, u32[]{:S(2)}) collective-permute-start(f32[8,1024]{1,0:T(8,128)S(1)} %maximum_maximum_fusion.sta_ref), channel_id=1, source_target_pairs={{0,3},{1,2},{2,1},{3,0},{4,7},{5,6},{6,5},{7,4},{8,11},{9,10},{10,... | collective-permute-start | bytes 98312 | tf_op jit(solution)/shard_map/ppermute | solution.py:328
  39.1 2.8 %collective-permute-done.4.stb_ref = f32[8,1024]{1,0:T(8,128)S(1)} collective-permute-done((f32[8,1024]{1,0:T(8,128)S(1)}, f32[8,1024]{1,0:T(8,128)S(1)}, u32[]{:S(2)}, u32[]{:S(2)}) %collective-permute-start.4) | collective-permute-done | bytes 32800 | tf_op jit(solution)/shard_map/ppermute | solution.py:328
  41.9 3.6 %shard_map.85 = (bf16[128,16,256]{2,1,0:T(8,128)(2,1)}, f32[1024,256]{1,0:T(8,128)S(1)}, f32[1,256]{1,0:T(1,128)}, f32[256,256]{1,0:T(8,128)S(1)}, bf16[256,256]...) custom-call(s32[64]{0:T(128)S(1)} %bitcast.53, s32[64]{0:T(128)S(1)} %multiply_add_fusion.slot_s, ...), custom_call_target="tpu_custom_call" | custom-call | flops 1610612736 | bytes 5507072 | tf_op jit(solution)/shard_map/pallas_call | solution.py:330
  45.5 3.3 %shard_map.87 = (f32[32,32,256]{2,1,0:T(8,128)S(1)}, bf16[32,32,256]{2,1,0:T(8,128)(2,1)S(1)}) custom-call(s32[4]{0:T(128)S(1)} %pad_add_fusion.1.place_s, f32[8,1024]{1,0:T(8,128)S(1)} %get-tuple-element.30.codes_ref, bf16[256,2048]{1,0:T(8,128)(2,1)S(1)} %bitcast.49, f32[1024,256]{1,0:T(8,128)S(1)} %get-tuple-element.31.g_ref), custom_call_target="tpu_custom_call" | custom-call | flops 2147483648 | bytes 3145728 | tf_op jit(solution)/shard_map/pallas_call | solution.py:358
  48.8 0.1 collective-permute-start.8
  49.0 0.4 multiply_reduce_fusion
  49.3 1.4 %collective-permute-done.8.recv_ref = bf16[32,32,256]{2,1,0:T(8,128)(2,1)S(1)} collective-permute-done((bf16[32,32,256]{2,1,0:T(8,128)(2,1)S(1)}, bf16[32,32,256]{2,1,0:T(8,128)(2,1)S(1)}, u32[]{:S(2)}, u32[]{:S(2)}) %collective-permute-start.8) | collective-permute-done | bytes 524320 | tf_op jit(solution)/shard_map/ppermute | solution.py:369
  50.8 0.8 shard_map.88
  51.5 0.7 collective-permute-start.9
  52.3 3.1 %collective-permute-start.10 = (bf16[32,8,256]{2,1,0:T(8,128)(2,1)S(1)}, bf16[32,8,256]{2,1,0:T(8,128)(2,1)S(1)}, u32[]{:S(2)}, u32[]{:S(2)}) collective-permute-start(bf16[32,8,256]{2,1,0:T(8,128)(2,1)S(1)} %get-tuple-element.36), channel_id=1, source_target_pairs={{0,2},{1,3},{2,0},{3,1},{4,6},{5,7},{6,4},{7,5},{8,10},{9,11},{10,... | collective-permute-start | bytes 393224 | tf_op jit(solution)/shard_map/ppermute | solution.py:257
  55.4 5.2 %all-to-all-start.1 = ((bf16[64,32,256]{2,1,0:T(8,128)(2,1)}), bf16[64,32,256]{2,1,0:T(8,128)(2,1)S(1)}, u32[]{:S(2)}, u32[]{:S(2)}) async-start(bf16[64,32,256]{2,1,0:T(8,128)(2,1)} %bitcast.14), calls=%async_computation.1 | async-start | bytes 2097152 | tf_op jit(solution)/shard_map/all_to_all | solution.py:350
  60.7 1.0 collective-permute-done.10
  61.8 0.8 collective-permute-start.12
  62.6 0.1 slice_convert_fusion.3
  62.7 4.7 %collective-permute-done.12 = bf16[16,8,256]{2,1,0:T(8,128)(2,1)S(1)} collective-permute-done((bf16[16,8,256]{2,1,0:T(8,128)(2,1)S(1)}, bf16[16,8,256]{2,1,0:T(8,128)(2,1)S(1)}, u32[]{:S(2)}, u32[]{:S(2)}) %collective-permute-start.12) | collective-permute-done | bytes 65568 | tf_op jit(solution)/shard_map/ppermute | solution.py:263
  67.4 1.7 %collective-permute-start.13 = (bf16[8,8,256]{2,1,0:T(8,128)(2,1)S(1)}, bf16[8,8,256]{2,1,0:T(8,128)(2,1)S(1)}, u32[]{:S(2)}, u32[]{:S(2)}) collective-permute-start(bf16[8,8,256]{2,1,0:T(8,128)(2,1)S(1)} %slice.202), channel_id=1, source_target_pairs={{0,192},{64,128},{128,64},{192,0},{1,193},{65,129},{129,65},{193,1... | collective-permute-start | bytes 98312 | tf_op jit(solution)/shard_map/ppermute | solution.py:263
  69.1 0.2 compare_reduce_fusion
  69.3 3.7 %collective-permute-done.13 = bf16[8,8,256]{2,1,0:T(8,128)(2,1)S(1)} collective-permute-done((bf16[8,8,256]{2,1,0:T(8,128)(2,1)S(1)}, bf16[8,8,256]{2,1,0:T(8,128)(2,1)S(1)}, u32[]{:S(2)}, u32[]{:S(2)}) %collective-permute-start.13) | collective-permute-done | bytes 32800 | tf_op jit(solution)/shard_map/ppermute | solution.py:263
  73.1 5.0 %collective-permute-start.14 = (bf16[4,8,256]{2,1,0:T(8,128)(2,1)S(1)}, bf16[4,8,256]{2,1,0:T(8,128)(2,1)S(1)}, u32[]{:S(2)}, u32[]{:S(2)}) collective-permute-start(bf16[4,8,256]{2,1,0:T(8,128)(2,1)S(1)} %slice.203), channel_id=1, source_target_pairs={{0,32},{8,40},{16,48},{24,56},{32,0},{40,8},{48,16},{56,24},{1,33}... | collective-permute-start | bytes 49160 | tf_op jit(solution)/shard_map/ppermute | solution.py:263
  78.0 11.1 %collective-permute-done.14 = bf16[4,8,256]{2,1,0:T(8,128)(2,1)S(1)} collective-permute-done((bf16[4,8,256]{2,1,0:T(8,128)(2,1)S(1)}, bf16[4,8,256]{2,1,0:T(8,128)(2,1)S(1)}, u32[]{:S(2)}, u32[]{:S(2)}) %collective-permute-start.14) | collective-permute-done | bytes 16416 | tf_op jit(solution)/shard_map/ppermute | solution.py:263
  89.1 0.1 collective-permute-start.15
  89.2 0.1 copy.17
  89.3 0.1 reshape.357.slot_j
  89.5 2.1 %collective-permute-start.5 = (bf16[256,256]{1,0:T(8,128)(2,1)S(1)}, bf16[256,256]{1,0:T(8,128)(2,1)S(1)}, u32[]{:S(2)}, u32[]{:S(2)}) collective-permute-start(bf16[256,256]{1,0:T(8,128)(2,1)S(1)} %get-tuple-element.26), channel_id=1, source_target_pairs={{0,1},{1,2},{2,3},{3,0},{4,5},{5,6},{6,7},{7,4},{8,9},{9,10},{10,1... | collective-permute-start | bytes 393224 | tf_op jit(solution)/shard_map/ppermute | solution.py:257
  91.6 0.5 collective-permute-start.6
  92.1 2.5 %collective-permute-start.7 = (bf16[256,256]{1,0:T(8,128)(2,1)S(1)}, bf16[256,256]{1,0:T(8,128)(2,1)S(1)}, u32[]{:S(2)}, u32[]{:S(2)}) collective-permute-start(bf16[256,256]{1,0:T(8,128)(2,1)S(1)} %get-tuple-element.28), channel_id=1, source_target_pairs={{0,3},{1,0},{2,1},{3,2},{4,7},{5,4},{6,5},{7,6},{8,11},{9,8},{10,9... | collective-permute-start | bytes 393224 | tf_op jit(solution)/shard_map/ppermute | solution.py:257
  94.6 1.5 %collective-permute-start.16 = (bf16[1,8,256]{2,1,0:T(8,128)(2,1)S(1)}, bf16[1,8,256]{2,1,0:T(8,128)(2,1)S(1)}, u32[]{:S(2)}, u32[]{:S(2)}) collective-permute-start(bf16[1,8,256]{2,1,0:T(8,128)(2,1)S(1)} %slice.205), channel_id=1, source_target_pairs={{0,8},{8,0},{16,24},{24,16},{32,40},{40,32},{48,56},{56,48},{1,9},... | collective-permute-start | bytes 12296 | tf_op jit(solution)/shard_map/ppermute | solution.py:263
  96.2 2.6 %collective-permute-done.5 = bf16[256,256]{1,0:T(8,128)(2,1)S(1)} collective-permute-done((bf16[256,256]{1,0:T(8,128)(2,1)S(1)}, bf16[256,256]{1,0:T(8,128)(2,1)S(1)}, u32[]{:S(2)}, u32[]{:S(2)}) %collective-permute-start.5) | collective-permute-done | bytes 131104 | tf_op jit(solution)/shard_map/ppermute | solution.py:257
  98.7 0.6 collective-permute-done.7
  99.4 0.8 copy.18
  100.2 0.6 fusion.8
  100.9 1.6 %shard_map.86 = f32[64,256]{1,0:T(8,128)} custom-call(s32[128]{0:T(128)S(1)} %reshape.357.slot_j, bf16[128,16,256]{2,1,0:T(8,128)(2,1)S(1)} %bitcast.47, f32[64,256]{1,0:T(8,128)S(1)} %broadcast_multiply_fusion.unit_ref, f32[64,128]{1,0:T(8,128)S(1)} %broadcast_in_dim.30.inv_ref), custom_call_target="tpu_custom_call" | custom-call | flops 524288 | bytes 131072 | tf_op jit(solution)/shard_map/pallas_call | solution.py:404
  (54 shorter events, 1.4 us)
Async XLA Ops:
  0.6 4.7 %copy-start = (s32[1,64]{1,0:T(1,128)S(1)}, s32[1,64]{1,0:T(1,128)}, u32[]{:S(2)}) copy-start(s32[1,64]{1,0:T(1,128)} %param.7) | copy-start | bytes 772
  0.6 21.0 %collective-permute-start.2 = (bf16[256,256]{1,0:T(8,128)(2,1)}, bf16[256,256]{1,0:T(8,128)(2,1)S(1)}, u32[]{:S(2)}, u32[]{:S(2)}) collective-permute-start(bf16[256,256]{1,0:T(8,128)(2,1)} %bitcast.54), channel_id=1, source_target_pairs={{0,3},{1,0},{2,1},{3,2},{4,7},{5,4},{6,5},{7,6},{8,11},{9,8},{10,9... | collective-permute-start | bytes 393224 | tf_op jit(solution)/shard_map/ppermute | solution.py:257
  3.7 17.9 %collective-permute-start.1 = (bf16[256,256]{1,0:T(8,128)(2,1)}, bf16[256,256]{1,0:T(8,128)(2,1)S(1)}, u32[]{:S(2)}, u32[]{:S(2)}) collective-permute-start(bf16[256,256]{1,0:T(8,128)(2,1)} %bitcast.55), channel_id=1, source_target_pairs={{0,2},{1,3},{2,0},{3,1},{4,6},{5,7},{6,4},{7,5},{8,10},{9,11},{10,... | collective-permute-start | bytes 393224 | tf_op jit(solution)/shard_map/ppermute | solution.py:257
  4.4 17.2 %collective-permute-start = (bf16[256,256]{1,0:T(8,128)(2,1)}, bf16[256,256]{1,0:T(8,128)(2,1)S(1)}, u32[]{:S(2)}, u32[]{:S(2)}) collective-permute-start(bf16[256,256]{1,0:T(8,128)(2,1)} %bitcast.56), channel_id=1, source_target_pairs={{0,1},{1,2},{2,3},{3,0},{4,5},{5,6},{6,7},{7,4},{8,9},{9,10},{10,1... | collective-permute-start | bytes 393224 | tf_op jit(solution)/shard_map/ppermute | solution.py:257
  6.8 11.7 %copy-start.3 = (s32[1,1,8,64]{3,2,1,0:T(8,128)S(1)}, s32[1,1,8,64]{3,2,1,0:T(8,128)}, u32[]{:S(2)}) copy-start(s32[1,1,8,64]{3,2,1,0:T(8,128)} %param.8) | copy-start | bytes 6148
  6.8 21.8 %all-to-all-start = ((bf16[64,8,128]{2,1,0:T(8,128)(2,1)}), bf16[64,8,128]{2,1,0:T(8,128)(2,1)S(1)}, u32[]{:S(2)}, u32[]{:S(2)}) async-start(bf16[64,8,128]{2,1,0:T(8,128)(2,1)} %broadcast_in_dim.25), calls=%async_computation | async-start | bytes 262144 | tf_op jit(solution)/shard_map/all_to_all | solution.py:288
  18.6 0.7 copy-start.4
  20.0 8.6 %copy-start.1 = (bf16[1,1,256,256]{3,2,1,0:T(8,128)(2,1)S(1)}, bf16[1,1,256,256]{3,2,1,0:T(8,128)(2,1)}, u32[]{:S(2)}) copy-start(bf16[1,1,256,256]{3,2,1,0:T(8,128)(2,1)} %param.5) | copy-start | bytes 393220
  32.5 4.0 %collective-permute-start.3 = (f32[8,1024]{1,0:T(8,128)S(1)}, f32[8,1024]{1,0:T(8,128)S(1)}, u32[]{:S(2)}, u32[]{:S(2)}) collective-permute-start(f32[8,1024]{1,0:T(8,128)S(1)} %get-tuple-element.21), channel_id=1, source_target_pairs={{0,1},{1,0},{2,3},{3,2},{4,5},{5,4},{6,7},{7,6},{8,9},{9,8},{10,11... | collective-permute-start | bytes 98312 | tf_op jit(solution)/shard_map/ppermute | solution.py:324
  36.6 5.3 %collective-permute-start.4 = (f32[8,1024]{1,0:T(8,128)S(1)}, f32[8,1024]{1,0:T(8,128)S(1)}, u32[]{:S(2)}, u32[]{:S(2)}) collective-permute-start(f32[8,1024]{1,0:T(8,128)S(1)} %maximum_maximum_fusion.sta_ref), channel_id=1, source_target_pairs={{0,3},{1,2},{2,1},{3,0},{4,7},{5,6},{6,5},{7,4},{8,11},{9,10},{10,... | collective-permute-start | bytes 98312 | tf_op jit(solution)/shard_map/ppermute | solution.py:328
  45.5 3.5 %copy-start.2 = (bf16[2048,256]{1,0:T(8,128)(2,1)S(1)}, bf16[2048,256]{1,0:T(8,128)(2,1)}, u32[]{:S(2)}) copy-start(bf16[2048,256]{1,0:T(8,128)(2,1)} %param.9) | copy-start | bytes 3145732
  48.8 2.0 %collective-permute-start.8 = (bf16[32,32,256]{2,1,0:T(8,128)(2,1)S(1)}, bf16[32,32,256]{2,1,0:T(8,128)(2,1)S(1)}, u32[]{:S(2)}, u32[]{:S(2)}) collective-permute-start(bf16[32,32,256]{2,1,0:T(8,128)(2,1)S(1)} %get-tuple-element.33), channel_id=1, source_target_pairs={{0,4},{4,0},{1,5},{5,1},{2,6},{6,2},{3,7},{7,3},{8,12},{12,8},{9,1... | collective-permute-start | bytes 1572872 | tf_op jit(solution)/shard_map/ppermute | solution.py:369
  51.5 9.1 %collective-permute-start.9 = (bf16[32,8,256]{2,1,0:T(8,128)(2,1)S(1)}, bf16[32,8,256]{2,1,0:T(8,128)(2,1)S(1)}, u32[]{:S(2)}, u32[]{:S(2)}) collective-permute-start(bf16[32,8,256]{2,1,0:T(8,128)(2,1)S(1)} %get-tuple-element.35), channel_id=1, source_target_pairs={{0,1},{1,2},{2,3},{3,0},{4,5},{5,6},{6,7},{7,4},{8,9},{9,10},{10,1... | collective-permute-start | bytes 393224 | tf_op jit(solution)/shard_map/ppermute | solution.py:257
  52.3 9.4 %collective-permute-start.10 = (bf16[32,8,256]{2,1,0:T(8,128)(2,1)S(1)}, bf16[32,8,256]{2,1,0:T(8,128)(2,1)S(1)}, u32[]{:S(2)}, u32[]{:S(2)}) collective-permute-start(bf16[32,8,256]{2,1,0:T(8,128)(2,1)S(1)} %get-tuple-element.36), channel_id=1, source_target_pairs={{0,2},{1,3},{2,0},{3,1},{4,6},{5,7},{6,4},{7,5},{8,10},{9,11},{10,... | collective-permute-start | bytes 393224 | tf_op jit(solution)/shard_map/ppermute | solution.py:257
  55.3 6.4 %collective-permute-start.11 = (bf16[32,8,256]{2,1,0:T(8,128)(2,1)S(1)}, bf16[32,8,256]{2,1,0:T(8,128)(2,1)S(1)}, u32[]{:S(2)}, u32[]{:S(2)}) collective-permute-start(bf16[32,8,256]{2,1,0:T(8,128)(2,1)S(1)} %get-tuple-element.37), channel_id=1, source_target_pairs={{0,3},{1,0},{2,1},{3,2},{4,7},{5,4},{6,5},{7,6},{8,11},{9,8},{10,9... | collective-permute-start | bytes 393224 | tf_op jit(solution)/shard_map/ppermute | solution.py:257
  55.4 45.4 %all-to-all-start.1 = ((bf16[64,32,256]{2,1,0:T(8,128)(2,1)}), bf16[64,32,256]{2,1,0:T(8,128)(2,1)S(1)}, u32[]{:S(2)}, u32[]{:S(2)}) async-start(bf16[64,32,256]{2,1,0:T(8,128)(2,1)} %bitcast.14), calls=%async_computation.1 | async-start | bytes 2097152 | tf_op jit(solution)/shard_map/all_to_all | solution.py:350
  61.8 5.5 %collective-permute-start.12 = (bf16[16,8,256]{2,1,0:T(8,128)(2,1)S(1)}, bf16[16,8,256]{2,1,0:T(8,128)(2,1)S(1)}, u32[]{:S(2)}, u32[]{:S(2)}) collective-permute-start(bf16[16,8,256]{2,1,0:T(8,128)(2,1)S(1)} %slice.201), channel_id=1, source_target_pairs={{0,64},{64,0},{128,192},{192,128},{1,65},{65,1},{129,193},{193,129... | collective-permute-start | bytes 196616 | tf_op jit(solution)/shard_map/ppermute | solution.py:263
  67.4 5.6 %collective-permute-start.13 = (bf16[8,8,256]{2,1,0:T(8,128)(2,1)S(1)}, bf16[8,8,256]{2,1,0:T(8,128)(2,1)S(1)}, u32[]{:S(2)}, u32[]{:S(2)}) collective-permute-start(bf16[8,8,256]{2,1,0:T(8,128)(2,1)S(1)} %slice.202), channel_id=1, source_target_pairs={{0,192},{64,128},{128,64},{192,0},{1,193},{65,129},{129,65},{193,1... | collective-permute-start | bytes 98312 | tf_op jit(solution)/shard_map/ppermute | solution.py:263
  73.1 16.1 %collective-permute-start.14 = (bf16[4,8,256]{2,1,0:T(8,128)(2,1)S(1)}, bf16[4,8,256]{2,1,0:T(8,128)(2,1)S(1)}, u32[]{:S(2)}, u32[]{:S(2)}) collective-permute-start(bf16[4,8,256]{2,1,0:T(8,128)(2,1)S(1)} %slice.203), channel_id=1, source_target_pairs={{0,32},{8,40},{16,48},{24,56},{32,0},{40,8},{48,16},{56,24},{1,33}... | collective-permute-start | bytes 49160 | tf_op jit(solution)/shard_map/ppermute | solution.py:263
  89.1 5.5 %collective-permute-start.15 = (bf16[2,8,256]{2,1,0:T(8,128)(2,1)S(1)}, bf16[2,8,256]{2,1,0:T(8,128)(2,1)S(1)}, u32[]{:S(2)}, u32[]{:S(2)}) collective-permute-start(bf16[2,8,256]{2,1,0:T(8,128)(2,1)S(1)} %slice.204), channel_id=1, source_target_pairs={{0,16},{8,24},{16,0},{24,8},{32,48},{40,56},{48,32},{56,40},{1,17}... | collective-permute-start | bytes 24584 | tf_op jit(solution)/shard_map/ppermute | solution.py:263
  89.5 9.3 %collective-permute-start.5 = (bf16[256,256]{1,0:T(8,128)(2,1)S(1)}, bf16[256,256]{1,0:T(8,128)(2,1)S(1)}, u32[]{:S(2)}, u32[]{:S(2)}) collective-permute-start(bf16[256,256]{1,0:T(8,128)(2,1)S(1)} %get-tuple-element.26), channel_id=1, source_target_pairs={{0,1},{1,2},{2,3},{3,0},{4,5},{5,6},{6,7},{7,4},{8,9},{9,10},{10,1... | collective-permute-start | bytes 393224 | tf_op jit(solution)/shard_map/ppermute | solution.py:257
  91.6 7.2 %collective-permute-start.6 = (bf16[256,256]{1,0:T(8,128)(2,1)S(1)}, bf16[256,256]{1,0:T(8,128)(2,1)S(1)}, u32[]{:S(2)}, u32[]{:S(2)}) collective-permute-start(bf16[256,256]{1,0:T(8,128)(2,1)S(1)} %get-tuple-element.27), channel_id=1, source_target_pairs={{0,2},{1,3},{2,0},{3,1},{4,6},{5,7},{6,4},{7,5},{8,10},{9,11},{10,... | collective-permute-start | bytes 393224 | tf_op jit(solution)/shard_map/ppermute | solution.py:257
  92.1 7.2 %collective-permute-start.7 = (bf16[256,256]{1,0:T(8,128)(2,1)S(1)}, bf16[256,256]{1,0:T(8,128)(2,1)S(1)}, u32[]{:S(2)}, u32[]{:S(2)}) collective-permute-start(bf16[256,256]{1,0:T(8,128)(2,1)S(1)} %get-tuple-element.28), channel_id=1, source_target_pairs={{0,3},{1,0},{2,1},{3,2},{4,7},{5,4},{6,5},{7,6},{8,11},{9,8},{10,9... | collective-permute-start | bytes 393224 | tf_op jit(solution)/shard_map/ppermute | solution.py:257
  94.6 5.6 %collective-permute-start.16 = (bf16[1,8,256]{2,1,0:T(8,128)(2,1)S(1)}, bf16[1,8,256]{2,1,0:T(8,128)(2,1)S(1)}, u32[]{:S(2)}, u32[]{:S(2)}) collective-permute-start(bf16[1,8,256]{2,1,0:T(8,128)(2,1)S(1)} %slice.205), channel_id=1, source_target_pairs={{0,8},{8,0},{16,24},{24,16},{32,40},{40,32},{48,56},{56,48},{1,9},... | collective-permute-start | bytes 12296 | tf_op jit(solution)/shard_map/ppermute | solution.py:263

commit v2 on v1

--- a/solution.py
+++ b/solution.py
@@ -1,3 +1,5 @@
+import functools
+
 import jax
 import jax.numpy as jnp
 from jax import lax
@@ -69,7 +71,7 @@
 
 def stats_kernel(
     pair_s, place_s, recv_ref, q0, q1, q2, q3, tkey_ref, cbt_ref,
-    u_ref, q_ref, st_ref, codes_ref, rows_ref, key_ref,
+    u_ref, q_ref, st_ref, codes_ref, unit_ref, inv_ref, rows_ref, key_ref,
 ):
     cols = u_ref.shape[0]
     pair_count = cols // PR
@@ -101,7 +103,10 @@
             preferred_element_type=F32,
         )
     inverse = lax.rsqrt(jnp.sum(quant * quant, axis=0, keepdims=True) + EPS)
-    u_ref[...] = (quant * inverse).T.astype(BF16)
+    unit = quant * inverse
+    unit_ref[...] = unit
+    inv_ref[...] = inverse
+    u_ref[...] = unit.T.astype(BF16)
     total_rows = q_ref.shape[0]
     peak = jnp.full((1, total_rows), -1e30, F32)
     total = jnp.zeros((1, total_rows), F32)
@@ -122,7 +127,22 @@
     st_ref[0:1, :] = peak
     st_ref[1:2, :] = total
     st_ref[2:3, :] = hit
-    st_ref[3:8, :] = jnp.zeros((5, total_rows), F32)
+
+
+def hot_kernel(codes_ref, hot_ref):
+    for book in range(BOOKS):
+        hot_ref[book] = one_hot_of(codes_ref, book, CODES)
+
+
+def pack_kernel(codes_ref, pairs_ref, out_ref):
+    codes = codes_ref[...]
+    spare = LANES - codes.shape[1] - pairs_ref.shape[1]
+    pieces = [codes, jnp.broadcast_to(pairs_ref[...], (BOOKS, pairs_ref.shape[1]))]
+    if spare:
+        pieces.append(jnp.zeros((BOOKS, spare), jnp.int32))
+    message = jnp.concatenate(pieces, axis=1).astype(F32).astype(BF16)
+    for peer in range(out_ref.shape[0]):
+        out_ref[peer] = message
 
 
 def merged(first, second):
@@ -132,12 +152,13 @@
 
 
 def grads_kernel(
-    pair_s, slot_s, place_s, sta_ref, stb_ref, tkey_ref, u_ref, q_ref,
-    send_ref, g_ref, loss_ref, own_ref, far1, far2, far3, key_ref, lse_ref, qgt_ref,
+    pair_s, slot_s, place_s, sta_ref, stb_ref, tkey_ref, u_ref, q_ref, unit_ref, inv_ref, hot_ref,
+    send_ref, loss_ref, own_ref, far1, far2, far3, keep_ref, give_ref,
+    key_ref, lse_ref, qgt_ref, pg_ref, sum_ref,
 ):
     cols = u_ref.shape[0]
     pair_count = cols // PR
-    rep = place_s[3]
+    core, rep = place_s[2], place_s[3]
     rows = own_ref.shape[1]
     peak, total, hit = merged(sta_ref[...], stb_ref[...])
     lse = peak + jnp.log(total)
@@ -148,15 +169,19 @@
     step = min(256, cols)
     grown = None
     for start in range(0, cols, step):
-        u_part = u_ref[start : start + step, :]
+        span = slice(start, start + step)
+        u_part = u_ref[span, :]
         scores = lax.dot_general(u_part, q_ref[...], CONTRACT_LAST, preferred_element_type=F32)
         hit_mask = hits(key_ref, start, step, tkey_ref)
         weight = (jnp.exp(scores - lse) - jnp.where(hit_mask, 1.0, 0.0)).astype(BF16)
         grad = jnp.dot(weight, q_ref[...], preferred_element_type=F32)
-        g_ref[start : start + step, :] = grad
         narrow = grad.astype(BF16)
         for place in range(step // PR):
             send_ref[slot_s[start // PR + place]] = narrow[place * PR : (place + 1) * PR, :]
+        turned = grad.T
+        unit = unit_ref[:, span]
+        along = jnp.sum(unit * turned, axis=0, keepdims=True)
+        pg_ref[:, span] = (inv_ref[0:1, span] * (turned - unit * along)).astype(BF16)
         term = lax.dot_general(u_part, weight, CONTRACT_FIRST, preferred_element_type=F32)
         grown = term if grown is None else grown + term
     qgt_ref[...] = grown
@@ -165,65 +190,76 @@
         owner = lax.rem(rep + k, count)
         part = qgt_ref[:, pl.ds(pl.multiple_of(owner * rows, rows), rows)]
         out[...] = part.astype(out.dtype)
-
-
-def books_kernel(place_s, codes_ref, cbt_ref, g_ref, keep_ref, send_ref, hot_ref, sum_ref):
-    cols = codes_ref.shape[1]
-    core = place_s[2]
-    quant = jnp.zeros((cbt_ref.shape[0], cols), F32)
-    for book in range(BOOKS):
-        hot_ref[book] = one_hot_of(codes_ref, book, CODES)
-        quant = quant + jnp.dot(
-            cbt_ref[:, book * CODES : (book + 1) * CODES],
-            hot_ref[book],
-            preferred_element_type=F32,
-        )
-    inverse = lax.rsqrt(jnp.sum(quant * quant, axis=0, keepdims=True) + EPS)
-    unit = quant * inverse
-    grad = g_ref[...].T
-    grad = inverse * (grad - unit * jnp.sum(unit * grad, axis=0, keepdims=True))
-    narrow = grad.astype(BF16)
     for book in range(BOOKS):
         sum_ref[book * CODES : (book + 1) * CODES, :] = lax.dot_general(
-            hot_ref[book], narrow, CONTRACT_LAST, preferred_element_type=F32
+            hot_ref[book], pg_ref[...], CONTRACT_LAST, preferred_element_type=F32
         )
     half = keep_ref.shape[1]
     for chunk in range(keep_ref.shape[0]):
         base = chunk * 2 * half
         keep_ref[chunk] = sum_ref[pl.ds(pl.multiple_of(base + core * half, half), half), :]
-        send_ref[chunk] = sum_ref[
+        give_ref[chunk] = sum_ref[
             pl.ds(pl.multiple_of(base + (1 - core) * half, half), half), :
         ].astype(BF16)
 
 
-def x_order(here, count):
+def x_partners(count):
     if count == 4:
-        return (here, 3 - here, here ^ 1, 3 - (here ^ 1))
-    return tuple(here ^ k for k in range(count))
-
-
-def deal_kernel(place_s, keep_ref, recv_ref, own_ref, far1, far2, far3, sum_ref):
+        return [lambda i: i ^ 1, lambda i: 3 - i]
+    return [lambda i: i ^ 1][: count - 1]
+
+
+def z_partners(count):
+    if count == 8:
+        return [
+            lambda i: (i + 3 - 6 * (i & 1)) & 7,
+            lambda i: (i - 1 + 2 * (i & 1)) & 7,
+            lambda i: i ^ 1,
+        ]
+    return [lambda i: i ^ 1][: count - 1]
+
+
+def halving_order(here, partners):
+    order = [here]
+    for partner in reversed(partners):
+        order = order + halving_tail(partner(here), partners, len(order))
+    return order
+
+
+def halving_tail(there, partners, length):
+    order = [there]
+    for partner in reversed(partners):
+        if len(order) == length:
+            break
+        order = order + halving_tail(partner(there), partners, len(order))
+    return order
+
+
+def deal_kernel(place_s, keep_ref, recv_ref, qg1, qg2, qg3, own_ref, far1, far2, far3, sum_ref, *, sizes):
     x_here, z_here, rep = place_s[0], place_s[1], place_s[3]
-    x_count, z_count, reps = place_sizes(own_ref, keep_ref)
+    x_count, z_count, reps = sizes
     share = keep_ref.shape[1] // reps
     sum_ref[...] = keep_ref[...] + recv_ref[...].astype(F32)
-    order = x_order(x_here, x_count)
+    order = [
+        px * z_count + pz
+        for px in halving_order(x_here, x_partners(x_count))
+        for pz in halving_order(z_here, z_partners(z_count))
+    ]
     for k, out in enumerate((own_ref, far1, far2, far3)):
         owner = lax.rem(rep + k, reps)
         at = pl.ds(pl.multiple_of(owner * share, share), share)
-        for px in range(x_count):
-            for pz in range(z_count):
-                chunk = order[px] * z_count + (z_here ^ pz)
-                out[px * z_count + pz] = sum_ref[chunk, at, :].astype(out.dtype)
-
-
-def place_sizes(own_ref, keep_ref):
-    chunks = keep_ref.shape[0]
-    x_count = 4
-    return x_count, chunks // x_count, keep_ref.shape[1] // own_ref.shape[1]
-
-
-def return_kernel(slot_j, ret_ref, unit_ref, inv_ref, out_ref, *sums):
+        for pair in range(len(order) // 2):
+            rows = jnp.concatenate(
+                [sum_ref[order[2 * pair], at, :], sum_ref[order[2 * pair + 1], at, :]], axis=0
+            )
+            out[2 * pair * share : (2 * pair + 2) * share, :] = rows.astype(out.dtype)
+    dealt = len(order) * share
+    for out, part in zip((far1, far2, far3), (qg1, qg2, qg3)):
+        out[dealt : dealt + part.shape[0], :] = part[...]
+
+
+def return_kernel(slot_j, ret_ref, unit_ref, inv_ref, book_ref, more_ref, out_ref, total_ref, *sums):
+    total_ref[...] = book_ref[...] + more_ref[...].astype(F32)
     for part in sums:
         part[...] = jnp.zeros(part.shape, F32)
     for slot in range(ret_ref.shape[0]):
@@ -260,8 +296,7 @@
 def halved(own, axis, partner):
     half = own.shape[0] // 2
     pairs = [(i, partner(i)) for i in range(lax.axis_size(axis))]
-    arrived = lax.ppermute(own[half:].astype(BF16), axis, pairs)
-    return own[:half] + arrived.astype(F32)
+    return own[:half], lax.ppermute(own[half:].astype(BF16), axis, pairs)
 
 
 def shards(query_embed, positive_ids, pair_blocks, code_ids, codebooks):
@@ -280,11 +315,9 @@
     place = jnp.stack([lax.axis_index(a) for a in AXES]).astype(jnp.int32)
 
     held = local_codes.shape[1]
-    listed = jnp.broadcast_to(
-        jnp.pad(wanted, (0, LANES - held - pair_count))[None, :], (BOOKS, LANES - held)
-    )
-    message = jnp.concatenate([local_codes, listed], axis=1).astype(BF16)
-    message = jnp.broadcast_to(message[None], (owners, BOOKS, LANES))
+    message = call(
+        pack_kernel, sds((owners, BOOKS, LANES), BF16), [], 0, 2, owners * BOOKS * LANES
+    )(local_codes, wanted[None, :])
     arrived = lax.all_to_all(message, BLK, 0, 0, tiled=True)
     query_parts = [rows_mine] + [shifted(rows_mine, k) for k in range(1, reps)]
 
@@ -305,13 +338,15 @@
     unit, inverse = unit_rows(local_codes, codebooks)
     inverse_wide = jnp.broadcast_to(inverse, (inverse.shape[0], LANES))
 
-    units, queries, stats, codes = call(
+    units, queries, stats, codes, unit_t, inv_t = call(
         stats_kernel,
         (
             sds((cols, feat), BF16),
             sds((all_rows, feat), BF16),
-            sds((8, all_rows), F32),
+            sds((3, all_rows), F32),
             sds((BOOKS, cols), F32),
+            sds((feat, cols), F32),
+            sds((1, cols), F32),
         ),
         [pltpu.VMEM((owners * BOOKS, LANES), F32), pltpu.VMEM((cols, LANES), jnp.int32)],
         2,
@@ -321,71 +356,62 @@
 
     near = [(i, i ^ 1) for i in range(reps)]
     cross = [(i, reps - 1 - i) for i in range(reps)]
-    peak, total, hit = merged(stats, lax.ppermute(stats, "rep", near))
-    stats_two = jnp.concatenate(
-        [peak, total, hit, jnp.zeros((5, all_rows), F32)], axis=0
-    )
+    stats_near = lax.ppermute(stats, "rep", near)
+    hot = call(hot_kernel, sds((BOOKS, CODES, cols), BF16), [], 0, 1, BOOKS * CODES * cols)(codes)
+    stats_two = jnp.concatenate(merged(stats, stats_near), axis=0)
     stats_far = lax.ppermute(stats_two, "rep", cross)
 
-    outbound, grad_cols, loss, own_t, far1, far2, far3 = call(
+    chunks = x_count * z_count
+    chunk_rows = codebooks.shape[0] // chunks
+    half_rows = chunk_rows // cores
+    outbound, loss, own_t, far1, far2, far3, keep, give = call(
         grads_kernel,
         (
             sds((owners * CAP, PR, feat), BF16),
-            sds((cols, feat), F32),
             sds((1, row_count), F32),
             sds((feat, row_count), F32),
             *[sds((feat, row_count), BF16)] * 3,
+            sds((chunks, half_rows, feat), F32),
+            sds((chunks, half_rows, feat), BF16),
         ),
         [
             pltpu.VMEM((cols, LANES), jnp.int32),
             pltpu.VMEM((8, all_rows), F32),
             pltpu.VMEM((feat, all_rows), F32),
+            pltpu.VMEM((feat, cols), BF16),
+            pltpu.VMEM((BOOKS * CODES, feat), F32),
         ],
         3,
-        5,
-        6 * cols * feat * all_rows,
-    )(wanted, slot_of, place, stats_two, stats_far, tkey, units, queries)
+        8,
+        cols * feat * (6 * all_rows + 2 * BOOKS * CODES),
+    )(wanted, slot_of, place, stats_two, stats_far, tkey, units, queries, unit_t, inv_t, hot)
 
     outbound = outbound.reshape(owners, CAP * PR, feat)
     returned = lax.all_to_all(outbound, BLK, 0, 0, tiled=True)
     returned = returned.reshape(owners * CAP, PR, feat)
 
+    other = lax.ppermute(give, "c", [(0, 1), (1, 0)])
+    share_rows = half_rows // reps
+    dealt = chunks * share_rows
+    mine, *parts = call(
+        functools.partial(deal_kernel, sizes=(x_count, z_count, reps)),
+        (sds((dealt, feat), F32), *[sds((dealt + feat, row_count), BF16)] * 3),
+        [pltpu.VMEM((chunks, half_rows, feat), F32)],
+        1,
+        5,
+        cols * feat,
+    )(place, keep, other, far1, far2, far3)
+    parts = [shifted(part, k + 1) for k, part in enumerate(parts)]
     query_grad_t = own_t
-    for k, part in enumerate((far1, far2, far3)):
-        query_grad_t = query_grad_t + shifted(part, k + 1).astype(F32)
-
-    chunk_rows = codebooks.shape[0] // (x_count * z_count)
-    keep, send = call(
-        books_kernel,
-        (
-            sds((x_count * z_count, chunk_rows // 2, feat), F32),
-            sds((x_count * z_count, chunk_rows // 2, feat), BF16),
-        ),
-        [pltpu.VMEM((BOOKS, CODES, cols), BF16), pltpu.VMEM((BOOKS * CODES, feat), F32)],
-        1,
-        3,
-        4 * cols * feat * BOOKS * CODES,
-    )(place, codes, turned_books, grad_cols)
-    other = lax.ppermute(send, "c", [(0, 1), (1, 0)])
-    share_rows = chunk_rows // 2 // reps
-    share = (x_count * z_count, share_rows, feat)
-    mine, *parts = call(
-        deal_kernel,
-        (sds(share, F32), *[sds(share, BF16)] * 3),
-        [pltpu.VMEM((x_count * z_count, chunk_rows // 2, feat), F32)],
-        1,
-        2,
-        cols * feat,
-    )(place, keep, other)
-    for k, part in enumerate(parts):
-        mine = mine + shifted(part, k + 1).astype(F32)
-    mine = halved(mine, "x", lambda i: i ^ 1)
-    mine = halved(mine, "x", lambda i: x_count - 1 - i)
-    bit = z_count // 2
-    while bit:
-        mine = halved(mine, "z", lambda i, bit=bit: i ^ bit)
-        bit //= 2
-    codebook_grad = mine.reshape(share_rows, feat)
+    for part in parts:
+        mine = mine + part[:dealt].astype(F32)
+        query_grad_t = query_grad_t + part[dealt:].astype(F32)
+    steps = [("x", partner) for partner in x_partners(x_count)]
+    steps += [("z", partner) for partner in z_partners(z_count)]
+    for axis, partner in steps[:-1]:
+        kept, more = halved(mine, axis, partner)
+        mine = kept + more.astype(F32)
+    book_kept, book_more = halved(mine, *steps[-1])
 
     directory = arrived[:, 0, held : held + pair_count].astype(jnp.int32)
     local_iota = jnp.arange(PBLK_DEV, dtype=jnp.int32)
@@ -401,14 +427,14 @@
             rank = rank + named[:, j].astype(jnp.int32)
         slot_j.append(found)
     slot_j = jnp.stack(slot_j, axis=1).reshape(-1)
-    passage_grad = call(
+    passage_grad, codebook_grad = call(
         return_kernel,
-        sds((PBLK_DEV * PR, feat), F32),
+        (sds((PBLK_DEV * PR, feat), F32), sds((share_rows, feat), F32)),
         [pltpu.VMEM((PBLK_DEV + 1, PR, feat), F32) for _ in range(4)],
         1,
-        3,
+        5,
         owners * CAP * PR * feat,
-    )(slot_j, returned, unit, inverse_wide)
+    )(slot_j, returned, unit, inverse_wide, book_kept, book_more)
     return (
         loss[None],
         query_grad_t.T[None, None],

time: 104 us -> 99 us (0.952)
  the two profiles are of different devices: /device:TPU:32 before, /device:TPU:14 now
where the time goes in v2:
time: 99 us; the launch traced here: 98.6 us
  starting transfers between devices  40.8 us (41%)
  waiting for transfers between devices  33.6 us (34%)
  Pallas kernels  12.8 us (13%)
  local copies, waits for them, and re-layouts  7.24 us (7%)
  other arithmetic  2.95 us (3%)
    ppermute x5, waiting for transfers between devices, halved(): return (own[:half], lax.ppermute(own[half:].astype(BF16), axis, pairs))  18.5 us
    all_to_all x1, starting transfers between devices, shards(): arrived = lax.all_to_all(message, BLK, 0, 0, tiled=True)  12.2 us
    ppermute x5, starting transfers between devices, halved(): return (own[:half], lax.ppermute(own[half:].astype(BF16), axis, pairs))  11.5 us
    ppermute x6, starting transfers between devices, shifted(): return lax.ppermute(x, 'rep', [(i, (i + k) % count) for i in range(count)])  10.2 us
    all_to_all x1, starting transfers between devices, shards(): returned = lax.all_to_all(outbound, BLK, 0, 0, tiled=True)  6.7 us
    unnamed x15, local copies, waits for them, and re-layouts  5.92 us
    pallas_call x1, Pallas kernels, shards(): call(grads_kernel, (sds((owners * CAP, PR, feat), BF16), sds((1, row_coun...  5.04 us
    pallas_call x1, Pallas kernels, shards(): call(stats_kernel, (sds((cols, feat), BF16), sds((all_rows, feat), BF16),...  4 us
  transfers between devices with their start and end apart: 16, of which 10 were waited for; matrix products, arithmetic and copies ran while one was open for 8% of the time, Pallas kernels for 1%

profile of v2, /device:TPU:14, one launch (start us, length us, event | category | flops | bytes accessed | tf_op | source)
XLA Modules:
  0.0 98.6 jit_solution(10732881387576329232)
XLA Ops:
  0.6 0.5 collective-permute-start.2
  1.2 2.6 %collective-permute-start.1 = (bf16[256,256]{1,0:T(8,128)(2,1)}, bf16[256,256]{1,0:T(8,128)(2,1)S(1)}, u32[]{:S(2)}, u32[]{:S(2)}) collective-permute-start(bf16[256,256]{1,0:T(8,128)(2,1)} %bitcast.51), channel_id=1, source_target_pairs={{0,2},{1,3},{2,0},{3,1},{4,6},{5,7},{6,4},{7,5},{8,10},{9,11},{10,... | collective-permute-start | bytes 393224 | tf_op jit(solution)/shard_map/ppermute | solution.py:293
  3.7 1.9 %collective-permute-start = (bf16[256,256]{1,0:T(8,128)(2,1)}, bf16[256,256]{1,0:T(8,128)(2,1)S(1)}, u32[]{:S(2)}, u32[]{:S(2)}) collective-permute-start(bf16[256,256]{1,0:T(8,128)(2,1)} %bitcast.52), channel_id=1, source_target_pairs={{0,1},{1,2},{2,3},{3,0},{4,5},{5,6},{6,7},{7,4},{8,9},{9,10},{10,1... | collective-permute-start | bytes 393224 | tf_op jit(solution)/shard_map/ppermute | solution.py:293
  5.6 0.7 copy-done
  6.3 0.7 copy-done.1
  7.0 0.7 shard_map.84
  7.7 12.2 %all-to-all-start = ((bf16[64,8,128]{2,1,0:T(8,128)(2,1)}), bf16[64,8,128]{2,1,0:T(8,128)(2,1)S(1)}, u32[]{:S(2)}, u32[]{:S(2)}) async-start(bf16[64,8,128]{2,1,0:T(8,128)(2,1)} %shard_map.84), calls=%async_computation | async-start | bytes 262144 | tf_op jit(solution)/shard_map/all_to_all | solution.py:321
  19.9 0.7 and_select_fusion.11
  20.6 1.0 slice_bitcast_fusion
  21.5 0.7 copy.19
  22.8 0.7 fusion.10
  23.5 1.5 %copy.16 = bf16[2048,256]{0,1:T(8,128)(2,1)S(1)} copy(bf16[2048,256]{1,0:T(8,128)(2,1)} %param.9) | data formatting | bytes 2097152 | tf_op args[4]
  25.1 3.6 %all-to-all-done = bf16[64,8,128]{2,1,0:T(8,128)(2,1)S(1)} async-done(((bf16[64,8,128]{2,1,0:T(8,128)(2,1)}), bf16[64,8,128]{2,1,0:T(8,128)(2,1)S(1)}, u32[]{:S(2)}, u32[]{:S(2)}) %all-to-all-start) | async-done | bytes 131104 | tf_op jit(solution)/shard_map/all_to_all | solution.py:321
  28.7 0.7 copy-done.2
  29.4 0.9 copy-done.4
  30.3 4.0 %shard_map.85 = (bf16[1024,256]{1,0:T(8,128)(2,1)S(1)}, bf16[1024,256]{1,0:T(8,128)(2,1)S(1)}, f32[3,1024]{1,0:T(4,128)S(1)}, f32[8,1024]{1,0:T(8,128)S(1)}, f32...) custom-call(s32[64]{0:T(128)S(1)} %bitcast.47, s32[4]{0:T(128)S(1)} %pad_add_fusion.1.place_s, bf16[512,128]{1,0:T(8,128)(2,1)S(1)} %bitcast.45, ...), custom_call_target="tpu_custom_call" | custom-call | flops 1610612736 | bytes 4292608 | tf_op jit(solution)/shard_map/pallas_call | solution.py:341
  34.3 0.2 collective-permute-start.3
  34.5 0.2 convert_reduce_fusion
  34.7 3.4 %collective-permute-done.3 = f32[3,1024]{1,0:T(4,128)S(1)} collective-permute-done((f32[3,1024]{1,0:T(4,128)S(1)}, f32[3,1024]{1,0:T(4,128)S(1)}, u32[]{:S(2)}, u32[]{:S(2)}) %collective-permute-start.3) | collective-permute-done | bytes 12320 | tf_op jit(solution)/shard_map/ppermute | solution.py:359
  38.2 0.1 collective-permute-start.4
  38.3 0.7 shard_map.86.hot_ref
  39.0 3.0 %collective-permute-done.4.stb_ref = f32[3,1024]{1,0:T(4,128)S(1)} collective-permute-done((f32[3,1024]{1,0:T(4,128)S(1)}, f32[3,1024]{1,0:T(4,128)S(1)}, u32[]{:S(2)}, u32[]{:S(2)}) %collective-permute-start.4) | collective-permute-done | bytes 12320 | tf_op jit(solution)/shard_map/ppermute | solution.py:362
  42.0 5.0 %shard_map.87 = (bf16[128,16,256]{2,1,0:T(8,128)(2,1)}, f32[1,256]{1,0:T(1,128)}, f32[256,256]{1,0:T(8,128)S(1)}, bf16[256,256]{1,0:T(8,128)(2,1)S(1)}, bf16[256...) custom-call(s32[64]{0:T(128)S(1)} %bitcast.49, ...), custom_call_target="tpu_custom_call" | custom-call | flops 2684354560 | bytes 6555648 | tf_op jit(solution)/shard_map/pallas_call | solution.py:367
  47.2 0.4 multiply_reduce_fusion
  47.6 1.4 %collective-permute-done.5.recv_ref = bf16[32,32,256]{2,1,0:T(8,128)(2,1)S(1)} collective-permute-done((bf16[32,32,256]{2,1,0:T(8,128)(2,1)S(1)}, bf16[32,32,256]{2,1,0:T(8,128)(2,1)S(1)}, u32[]{:S(2)}, u32[]{:S(2)}) %collective-permute-start.5) | collective-permute-done | bytes 524320 | tf_op jit(solution)/shard_map/ppermute | solution.py:393
  49.0 0.8 shard_map.88
  49.7 0.1 collective-permute-start.6
  49.8 3.4 %collective-permute-start.7 = (bf16[512,256]{1,0:T(8,128)(2,1)S(1)}, bf16[512,256]{1,0:T(8,128)(2,1)S(1)}, u32[]{:S(2)}, u32[]{:S(2)}) collective-permute-start(bf16[512,256]{1,0:T(8,128)(2,1)S(1)} %get-tuple-element.38), channel_id=1, source_target_pairs={{0,2},{1,3},{2,0},{3,1},{4,6},{5,7},{6,4},{7,5},{8,10},{9,11},{10,... | collective-permute-start | bytes 786440 | tf_op jit(solution)/shard_map/ppermute | solution.py:293
  53.2 1.7 %collective-permute-start.8 = (bf16[512,256]{1,0:T(8,128)(2,1)S(1)}, bf16[512,256]{1,0:T(8,128)(2,1)S(1)}, u32[]{:S(2)}, u32[]{:S(2)}) collective-permute-start(bf16[512,256]{1,0:T(8,128)(2,1)S(1)} %get-tuple-element.39), channel_id=1, source_target_pairs={{0,3},{1,0},{2,1},{3,2},{4,7},{5,4},{6,5},{7,6},{8,11},{9,8},{10,9... | collective-permute-start | bytes 786440 | tf_op jit(solution)/shard_map/ppermute | solution.py:293
  54.9 6.7 %all-to-all-start.1 = ((bf16[64,32,256]{2,1,0:T(8,128)(2,1)}), bf16[64,32,256]{2,1,0:T(8,128)(2,1)S(1)}, u32[]{:S(2)}, u32[]{:S(2)}) async-start(bf16[64,32,256]{2,1,0:T(8,128)(2,1)} %bitcast.14), calls=%async_computation.1 | async-start | bytes 2097152 | tf_op jit(solution)/shard_map/all_to_all | solution.py:390
  61.7 3.7 %collective-permute-done.8 = bf16[512,256]{1,0:T(8,128)(2,1)S(1)} collective-permute-done((bf16[512,256]{1,0:T(8,128)(2,1)S(1)}, bf16[512,256]{1,0:T(8,128)(2,1)S(1)}, u32[]{:S(2)}, u32[]{:S(2)}) %collective-permute-start.8) | collective-permute-done | bytes 262176 | tf_op jit(solution)/shard_map/ppermute | solution.py:293
  65.4 0.1 convert_add_fusion
  65.5 1.0 %collective-permute-start.9 = (bf16[128,256]{1,0:T(8,128)(2,1)S(1)}, bf16[128,256]{1,0:T(8,128)(2,1)S(1)}, u32[]{:S(2)}, u32[]{:S(2)}) collective-permute-start(bf16[128,256]{1,0:T(8,128)(2,1)S(1)} %slice.234), channel_id=1, source_target_pairs={{0,64},{64,0},{128,192},{192,128},{1,65},{65,1},{129,193},{193,129... | collective-permute-start | bytes 196616 | tf_op jit(solution)/shard_map/ppermute | solution.py:299
  66.5 4.1 %collective-permute-done.9 = bf16[128,256]{1,0:T(8,128)(2,1)S(1)} collective-permute-done((bf16[128,256]{1,0:T(8,128)(2,1)S(1)}, bf16[128,256]{1,0:T(8,128)(2,1)S(1)}, u32[]{:S(2)}, u32[]{:S(2)}) %collective-permute-start.9) | collective-permute-done | bytes 65568 | tf_op jit(solution)/shard_map/ppermute | solution.py:299
  70.6 1.7 %collective-permute-start.10 = (bf16[64,256]{1,0:T(8,128)(2,1)S(1)}, bf16[64,256]{1,0:T(8,128)(2,1)S(1)}, u32[]{:S(2)}, u32[]{:S(2)}) collective-permute-start(bf16[64,256]{1,0:T(8,128)(2,1)S(1)} %slice.235), channel_id=1, source_target_pairs={{0,192},{64,128},{128,64},{192,0},{1,193},{65,129},{129,65},{193,1... | collective-permute-start | bytes 98312 | tf_op jit(solution)/shard_map/ppermute | solution.py:299
  72.4 0.1 slice_convert_fusion.3
  72.5 3.5 %collective-permute-done.10 = bf16[64,256]{1,0:T(8,128)(2,1)S(1)} collective-permute-done((bf16[64,256]{1,0:T(8,128)(2,1)S(1)}, bf16[64,256]{1,0:T(8,128)(2,1)S(1)}, u32[]{:S(2)}, u32[]{:S(2)}) %collective-permute-start.10) | collective-permute-done | bytes 32800 | tf_op jit(solution)/shard_map/ppermute | solution.py:299
  76.0 3.2 %collective-permute-start.11 = (bf16[32,256]{1,0:T(8,128)(2,1)S(1)}, bf16[32,256]{1,0:T(8,128)(2,1)S(1)}, u32[]{:S(2)}, u32[]{:S(2)}) collective-permute-start(bf16[32,256]{1,0:T(8,128)(2,1)S(1)} %slice.236), channel_id=1, source_target_pairs={{0,24},{8,48},{16,40},{24,0},{32,56},{40,16},{48,8},{56,32},{1,25}... | collective-permute-start | bytes 49160 | tf_op jit(solution)/shard_map/ppermute | solution.py:299
  79.2 0.2 compare_reduce_fusion
  79.4 7.3 %collective-permute-done.11 = bf16[32,256]{1,0:T(8,128)(2,1)S(1)} collective-permute-done((bf16[32,256]{1,0:T(8,128)(2,1)S(1)}, bf16[32,256]{1,0:T(8,128)(2,1)S(1)}, u32[]{:S(2)}, u32[]{:S(2)}) %collective-permute-start.11) | collective-permute-done | bytes 16416 | tf_op jit(solution)/shard_map/ppermute | solution.py:299
  86.8 4.9 %collective-permute-start.12 = (bf16[16,256]{1,0:T(8,128)(2,1)S(1)}, bf16[16,256]{1,0:T(8,128)(2,1)S(1)}, u32[]{:S(2)}, u32[]{:S(2)}) collective-permute-start(bf16[16,256]{1,0:T(8,128)(2,1)S(1)} %slice.237), channel_id=1, source_target_pairs={{0,56},{8,16},{16,8},{24,32},{32,24},{40,48},{48,40},{56,0},{1,57}... | collective-permute-start | bytes 24584 | tf_op jit(solution)/shard_map/ppermute | solution.py:299
  91.7 1.6 %collective-permute-done.12 = bf16[16,256]{1,0:T(8,128)(2,1)S(1)} collective-permute-done((bf16[16,256]{1,0:T(8,128)(2,1)S(1)}, bf16[16,256]{1,0:T(8,128)(2,1)S(1)}, u32[]{:S(2)}, u32[]{:S(2)}) %collective-permute-start.12) | collective-permute-done | bytes 8224 | tf_op jit(solution)/shard_map/ppermute | solution.py:299
  93.3 0.7 collective-permute-start.13
  94.0 0.1 copy.17
  94.1 0.1 reshape.330.slot_j
  94.2 0.8 copy.18
  95.1 1.9 %collective-permute-done.13.more_ref = bf16[8,256]{1,0:T(8,128)(2,1)S(1)} collective-permute-done((bf16[8,256]{1,0:T(8,128)(2,1)S(1)}, bf16[8,256]{1,0:T(8,128)(2,1)S(1)}, u32[]{:S(2)}, u32[]{:S(2)}) %collective-permute-start.13) | collective-permute-done | bytes 4128 | tf_op jit(solution)/shard_map/ppermute | solution.py:299
  97.1 1.6 %shard_map.89 = (f32[64,256]{1,0:T(8,128)}, f32[8,256]{1,0:T(8,128)}) custom-call(s32[128]{0:T(128)S(1)} %reshape.330.slot_j, bf16[128,16,256]{2,1,0:T(8,128)(2,1)S(1)} %bitcast.43, f32[64,256]{1,0:T(8,128)S(1)} %broadcast_multiply_fusion.unit_ref, f32[64,128]{1,0:T(8,128)S(1)} %broadcast_in_dim.21.inv_ref, f32[8,256]{1,0:T(8,128)S(1)} %slice.182.book_ref, ...), custom_call_target="tpu_custom_call" | custom-call | flops 524288 | bytes 147456 | tf_op jit(solution)/shard_map/pallas_call | solution.py:430
  (44 shorter events, 1.2 us)
Async XLA Ops:
  0.6 24.4 %collective-permute-start.2 = (bf16[256,256]{1,0:T(8,128)(2,1)}, bf16[256,256]{1,0:T(8,128)(2,1)S(1)}, u32[]{:S(2)}, u32[]{:S(2)}) collective-permute-start(bf16[256,256]{1,0:T(8,128)(2,1)} %bitcast.50), channel_id=1, source_target_pairs={{0,3},{1,0},{2,1},{3,2},{4,7},{5,4},{6,5},{7,6},{8,11},{9,8},{10,9... | collective-permute-start | bytes 393224 | tf_op jit(solution)/shard_map/ppermute | solution.py:293
  1.2 23.9 %collective-permute-start.1 = (bf16[256,256]{1,0:T(8,128)(2,1)}, bf16[256,256]{1,0:T(8,128)(2,1)S(1)}, u32[]{:S(2)}, u32[]{:S(2)}) collective-permute-start(bf16[256,256]{1,0:T(8,128)(2,1)} %bitcast.51), channel_id=1, source_target_pairs={{0,2},{1,3},{2,0},{3,1},{4,6},{5,7},{6,4},{7,5},{8,10},{9,11},{10,... | collective-permute-start | bytes 393224 | tf_op jit(solution)/shard_map/ppermute | solution.py:293
  3.7 21.3 %collective-permute-start = (bf16[256,256]{1,0:T(8,128)(2,1)}, bf16[256,256]{1,0:T(8,128)(2,1)S(1)}, u32[]{:S(2)}, u32[]{:S(2)}) collective-permute-start(bf16[256,256]{1,0:T(8,128)(2,1)} %bitcast.52), channel_id=1, source_target_pairs={{0,1},{1,2},{2,3},{3,0},{4,5},{5,6},{6,7},{7,4},{8,9},{9,10},{10,1... | collective-permute-start | bytes 393224 | tf_op jit(solution)/shard_map/ppermute | solution.py:293
  5.6 0.7 copy-start
  6.3 0.7 copy-start.1
  7.7 21.0 %all-to-all-start = ((bf16[64,8,128]{2,1,0:T(8,128)(2,1)}), bf16[64,8,128]{2,1,0:T(8,128)(2,1)S(1)}, u32[]{:S(2)}, u32[]{:S(2)}) async-start(bf16[64,8,128]{2,1,0:T(8,128)(2,1)} %shard_map.84), calls=%async_computation | async-start | bytes 262144 | tf_op jit(solution)/shard_map/all_to_all | solution.py:321
  28.7 0.7 copy-start.2
  29.4 0.9 copy-start.4
  30.3 11.7 %copy-start.3 = (s32[1,64]{1,0:T(1,128)S(1)}, s32[1,64]{1,0:T(1,128)}, u32[]{:S(2)}) copy-start(s32[1,64]{1,0:T(1,128)} %pairs_ref.1) | copy-start | bytes 772
  34.3 3.8 %collective-permute-start.3 = (f32[3,1024]{1,0:T(4,128)S(1)}, f32[3,1024]{1,0:T(4,128)S(1)}, u32[]{:S(2)}, u32[]{:S(2)}) collective-permute-start(f32[3,1024]{1,0:T(4,128)S(1)} %get-tuple-element.24), channel_id=1, source_target_pairs={{0,1},{1,0},{2,3},{3,2},{4,5},{5,4},{6,7},{7,6},{8,9},{9,8},{10,11... | collective-permute-start | bytes 36872 | tf_op jit(solution)/shard_map/ppermute | solution.py:359
  38.2 3.8 %collective-permute-start.4 = (f32[3,1024]{1,0:T(4,128)S(1)}, f32[3,1024]{1,0:T(4,128)S(1)}, u32[]{:S(2)}, u32[]{:S(2)}) collective-permute-start(f32[3,1024]{1,0:T(4,128)S(1)} %pad_maximum_fusion.sta_ref), channel_id=1, source_target_pairs={{0,3},{1,2},{2,1},{3,0},{4,7},{5,6},{6,5},{7,4},{8,11},{9,10},{10,... | collective-permute-start | bytes 36872 | tf_op jit(solution)/shard_map/ppermute | solution.py:362
  42.0 5.2 %copy-start.5 = (bf16[2048,256]{1,0:T(8,128)(2,1)S(1)}, bf16[2048,256]{1,0:T(8,128)(2,1)}, u32[]{:S(2)}) copy-start(bf16[2048,256]{1,0:T(8,128)(2,1)} %param.9) | copy-start | bytes 3145732
  47.0 1.9 %collective-permute-start.5 = (bf16[32,32,256]{2,1,0:T(8,128)(2,1)S(1)}, bf16[32,32,256]{2,1,0:T(8,128)(2,1)S(1)}, u32[]{:S(2)}, u32[]{:S(2)}) collective-permute-start(bf16[32,32,256]{2,1,0:T(8,128)(2,1)S(1)} %get-tuple-element.33), channel_id=1, source_target_pairs={{0,4},{4,0},{1,5},{5,1},{2,6},{6,2},{3,7},{7,3},{8,12},{12,8},{9,1... | collective-permute-start | bytes 1572872 | tf_op jit(solution)/shard_map/ppermute | solution.py:393
  49.7 11.9 %collective-permute-start.6 = (bf16[512,256]{1,0:T(8,128)(2,1)S(1)}, bf16[512,256]{1,0:T(8,128)(2,1)S(1)}, u32[]{:S(2)}, u32[]{:S(2)}) collective-permute-start(bf16[512,256]{1,0:T(8,128)(2,1)S(1)} %get-tuple-element.37), channel_id=1, source_target_pairs={{0,1},{1,2},{2,3},{3,0},{4,5},{5,6},{6,7},{7,4},{8,9},{9,10},{10,1... | collective-permute-start | bytes 786440 | tf_op jit(solution)/shard_map/ppermute | solution.py:293
  49.8 11.9 %collective-permute-start.7 = (bf16[512,256]{1,0:T(8,128)(2,1)S(1)}, bf16[512,256]{1,0:T(8,128)(2,1)S(1)}, u32[]{:S(2)}, u32[]{:S(2)}) collective-permute-start(bf16[512,256]{1,0:T(8,128)(2,1)S(1)} %get-tuple-element.38), channel_id=1, source_target_pairs={{0,2},{1,3},{2,0},{3,1},{4,6},{5,7},{6,4},{7,5},{8,10},{9,11},{10,... | collective-permute-start | bytes 786440 | tf_op jit(solution)/shard_map/ppermute | solution.py:293
  53.2 12.2 %collective-permute-start.8 = (bf16[512,256]{1,0:T(8,128)(2,1)S(1)}, bf16[512,256]{1,0:T(8,128)(2,1)S(1)}, u32[]{:S(2)}, u32[]{:S(2)}) collective-permute-start(bf16[512,256]{1,0:T(8,128)(2,1)S(1)} %get-tuple-element.39), channel_id=1, source_target_pairs={{0,3},{1,0},{2,1},{3,2},{4,7},{5,4},{6,5},{7,6},{8,11},{9,8},{10,9... | collective-permute-start | bytes 786440 | tf_op jit(solution)/shard_map/ppermute | solution.py:293
  54.9 42.1 %all-to-all-start.1 = ((bf16[64,32,256]{2,1,0:T(8,128)(2,1)}), bf16[64,32,256]{2,1,0:T(8,128)(2,1)S(1)}, u32[]{:S(2)}, u32[]{:S(2)}) async-start(bf16[64,32,256]{2,1,0:T(8,128)(2,1)} %bitcast.14), calls=%async_computation.1 | async-start | bytes 2097152 | tf_op jit(solution)/shard_map/all_to_all | solution.py:390
  65.5 5.1 %collective-permute-start.9 = (bf16[128,256]{1,0:T(8,128)(2,1)S(1)}, bf16[128,256]{1,0:T(8,128)(2,1)S(1)}, u32[]{:S(2)}, u32[]{:S(2)}) collective-permute-start(bf16[128,256]{1,0:T(8,128)(2,1)S(1)} %slice.234), channel_id=1, source_target_pairs={{0,64},{64,0},{128,192},{192,128},{1,65},{65,1},{129,193},{193,129... | collective-permute-start | bytes 196616 | tf_op jit(solution)/shard_map/ppermute | solution.py:299
  70.6 5.4 %collective-permute-start.10 = (bf16[64,256]{1,0:T(8,128)(2,1)S(1)}, bf16[64,256]{1,0:T(8,128)(2,1)S(1)}, u32[]{:S(2)}, u32[]{:S(2)}) collective-permute-start(bf16[64,256]{1,0:T(8,128)(2,1)S(1)} %slice.235), channel_id=1, source_target_pairs={{0,192},{64,128},{128,64},{192,0},{1,193},{65,129},{129,65},{193,1... | collective-permute-start | bytes 98312 | tf_op jit(solution)/shard_map/ppermute | solution.py:299
  76.0 10.7 %collective-permute-start.11 = (bf16[32,256]{1,0:T(8,128)(2,1)S(1)}, bf16[32,256]{1,0:T(8,128)(2,1)S(1)}, u32[]{:S(2)}, u32[]{:S(2)}) collective-permute-start(bf16[32,256]{1,0:T(8,128)(2,1)S(1)} %slice.236), channel_id=1, source_target_pairs={{0,24},{8,48},{16,40},{24,0},{32,56},{40,16},{48,8},{56,32},{1,25}... | collective-permute-start | bytes 49160 | tf_op jit(solution)/shard_map/ppermute | solution.py:299
  86.8 6.5 %collective-permute-start.12 = (bf16[16,256]{1,0:T(8,128)(2,1)S(1)}, bf16[16,256]{1,0:T(8,128)(2,1)S(1)}, u32[]{:S(2)}, u32[]{:S(2)}) collective-permute-start(bf16[16,256]{1,0:T(8,128)(2,1)S(1)} %slice.237), channel_id=1, source_target_pairs={{0,56},{8,16},{16,8},{24,32},{32,24},{40,48},{48,40},{56,0},{1,57}... | collective-permute-start | bytes 24584 | tf_op jit(solution)/shard_map/ppermute | solution.py:299
  93.3 3.7 %collective-permute-start.13 = (bf16[8,256]{1,0:T(8,128)(2,1)S(1)}, bf16[8,256]{1,0:T(8,128)(2,1)S(1)}, u32[]{:S(2)}, u32[]{:S(2)}) collective-permute-start(bf16[8,256]{1,0:T(8,128)(2,1)S(1)} %slice.238), channel_id=1, source_target_pairs={{0,8},{8,0},{16,24},{24,16},{32,40},{40,32},{48,56},{56,48},{1,9},... | collective-permute-start | bytes 12296 | tf_op jit(solution)/shard_map/ppermute | solution.py:299

commit v3 on v2

--- a/solution.py
+++ b/solution.py
@@ -20,25 +20,28 @@
 EPS = 1e-06
 INTERPRET = False
 VMEM_LIMIT = 24 << 20
+WHOLE_VMEM = 63_000_000
 
 F32 = jnp.float32
 BF16 = jnp.bfloat16
 VMEM = pl.BlockSpec(memory_space=pltpu.VMEM)
 SMEM = pl.BlockSpec(memory_space=pltpu.SMEM)
+HBM = pl.BlockSpec(memory_space=pltpu.HBM)
 CONTRACT_LAST = (((1,), (1,)), ((), ()))
 CONTRACT_FIRST = (((0,), (0,)), ((), ()))
 
 
-def call(kernel, out_shape, scratch, smem_count, vmem_count, flops):
+def call(kernel, out_shape, scratch, smem_count, vmem_count, flops, hbm_count=0,
+         limit=VMEM_LIMIT):
     out_bytes = sum(s.size * s.dtype.itemsize for s in jax.tree.leaves(out_shape))
     return pl.pallas_call(
         kernel,
         out_shape=out_shape,
-        in_specs=[SMEM] * smem_count + [VMEM] * vmem_count,
+        in_specs=[SMEM] * smem_count + [HBM] * hbm_count + [VMEM] * vmem_count,
         out_specs=jax.tree.map(lambda _: VMEM, out_shape),
         scratch_shapes=scratch,
         interpret=INTERPRET,
-        compiler_params=pltpu.CompilerParams(vmem_limit_bytes=VMEM_LIMIT),
+        compiler_params=pltpu.CompilerParams(vmem_limit_bytes=limit),
         cost_estimate=pl.CostEstimate(
             flops=flops, bytes_accessed=2 * out_bytes, transcendentals=0
         ),
@@ -59,7 +62,7 @@
 def fill_keys(pair_s, key_ref, pair_count):
     sub = lax.broadcasted_iota(jnp.int32, (PR, LANES), 0)
     for slot in range(pair_count):
-        key_ref[slot * PR : (slot + 1) * PR, :] = sub + pair_s[slot] * PR
+        key_ref[slot * PR : (slot + 1) * PR, :] = sub + pair_s[0, slot] * PR
 
 
 def hits(key_ref, start, count, tkey_ref):
@@ -70,24 +73,28 @@
 
 
 def stats_kernel(
-    pair_s, place_s, recv_ref, q0, q1, q2, q3, tkey_ref, cbt_ref,
+    pair_s, place_s, recv_ref, near_ref, far_ref, tkey_ref, cbt_ref,
     u_ref, q_ref, st_ref, codes_ref, unit_ref, inv_ref, rows_ref, key_ref,
 ):
     cols = u_ref.shape[0]
     pair_count = cols // PR
     rep = place_s[3]
-    rows = q0.shape[0]
-    parts = (q0, q1, q2, q3)
-    for k in range(len(parts)):
-        owner = lax.rem(rep + len(parts) - k, len(parts))
-        q_ref[pl.ds(pl.multiple_of(owner * rows, rows), rows), :] = parts[k][...]
+    rows = near_ref.shape[0] // 2
+    across = q_ref.shape[0] // rows - 1 - rep
+    for owner, part in (
+        (rep, near_ref[0:rows, :]),
+        (rep ^ 1, near_ref[rows : 2 * rows, :]),
+        (across, far_ref[0:rows, :]),
+        (across ^ 1, far_ref[rows : 2 * rows, :]),
+    ):
+        q_ref[pl.ds(pl.multiple_of(owner * rows, rows), rows), :] = part
     rows_ref[...] = recv_ref[...].astype(F32)
     lane_group = lax.broadcasted_iota(jnp.int32, (BOOKS, LANES), 1) // PR
     per_tile = LANES // PR
     for tile in range(cols // LANES):
         held = jnp.zeros((BOOKS, LANES), F32)
         for place in range(per_tile):
-            block = pair_s[tile * per_tile + place]
+            block = pair_s[0, tile * per_tile + place]
             owner = block >> 2
             within = block & 3
             codes = rows_ref[pl.ds(pl.multiple_of(owner * BOOKS, BOOKS), BOOKS), :]
@@ -134,7 +141,15 @@
         hot_ref[book] = one_hot_of(codes_ref, book, CODES)
 
 
-def pack_kernel(codes_ref, pairs_ref, out_ref):
+def pack_kernel(codes_hbm, pairs_hbm, out_ref, codes_ref, pairs_ref, sems):
+    copies = [
+        pltpu.make_async_copy(codes_hbm, codes_ref, sems.at[0]),
+        pltpu.make_async_copy(pairs_hbm, pairs_ref, sems.at[1]),
+    ]
+    for copy in copies:
+        copy.start()
+    for copy in copies:
+        copy.wait()
     codes = codes_ref[...]
     spare = LANES - codes.shape[1] - pairs_ref.shape[1]
     pieces = [codes, jnp.broadcast_to(pairs_ref[...], (BOOKS, pairs_ref.shape[1]))]
@@ -143,6 +158,54 @@
     message = jnp.concatenate(pieces, axis=1).astype(F32).astype(BF16)
     for peer in range(out_ref.shape[0]):
         out_ref[peer] = message
+
+
+def side_kernel(
+    place_s, codes_hbm, pairs_hbm, targets_hbm, books_hbm,
+    pairs_ref, slot_ref, tkey_ref, cbt_ref, unit_ref, inv_ref,
+    codes_ref, near_ref, targets_ref, books_ref, float_ref, sems,
+):
+    moves = (
+        (codes_hbm, codes_ref),
+        (pairs_hbm, near_ref),
+        (targets_hbm, targets_ref),
+        (books_hbm, books_ref),
+    )
+    copies = [pltpu.make_async_copy(a, b, sems.at[k]) for k, (a, b) in enumerate(moves)]
+    for copy in copies:
+        copy.start()
+    for copy in copies:
+        copy.wait()
+    rep = place_s[3]
+    pairs_ref[...] = near_ref[...]
+    count = near_ref.shape[1]
+    wide = jnp.broadcast_to(near_ref[...], (count, count))
+    tall = wide.astype(F32).T.astype(jnp.int32)
+    before = ((tall >> 2) == (wide >> 2)) & (tall < wide)
+    slot_ref[...] = (near_ref[...] >> 2) * CAP + jnp.sum(
+        jnp.where(before, 1, 0), axis=0, keepdims=True
+    )
+    reps, rows = targets_ref.shape
+    for k in range(reps):
+        target = targets_ref[k : k + 1, :]
+        block = target // (PR * reps)
+        within = target - block * (PR * reps)
+        mine = within // PR == rep
+        tkey_ref[:, k * rows : (k + 1) * rows] = jnp.where(
+            mine, block * PR + within - rep * PR, -1
+        )
+    float_ref[...] = codes_ref[...].astype(F32)
+    quant = jnp.zeros(unit_ref.shape, F32)
+    for book in range(BOOKS):
+        span = slice(book * CODES, (book + 1) * CODES)
+        words = books_ref[span, :]
+        cbt_ref[:, span] = words.T
+        quant = quant + lax.dot_general(
+            one_hot_of(float_ref, book, CODES), words, CONTRACT_FIRST, preferred_element_type=F32
+        )
+    inverse = lax.rsqrt(jnp.sum(quant * quant, axis=1, keepdims=True) + EPS)
+    unit_ref[...] = quant * inverse
+    inv_ref[...] = jnp.broadcast_to(inverse, inv_ref.shape)
 
 
 def merged(first, second):
@@ -177,7 +240,7 @@
         grad = jnp.dot(weight, q_ref[...], preferred_element_type=F32)
         narrow = grad.astype(BF16)
         for place in range(step // PR):
-            send_ref[slot_s[start // PR + place]] = narrow[place * PR : (place + 1) * PR, :]
+            send_ref[slot_s[0, start // PR + place]] = narrow[place * PR : (place + 1) * PR, :]
         turned = grad.T
         unit = unit_ref[:, span]
         along = jnp.sum(unit * turned, axis=0, keepdims=True)
@@ -212,9 +275,9 @@
 def z_partners(count):
     if count == 8:
         return [
+            lambda i: i ^ 1,
+            lambda i: (i - 1 + 2 * (i & 1)) & 7,
             lambda i: (i + 3 - 6 * (i & 1)) & 7,
-            lambda i: (i - 1 + 2 * (i & 1)) & 7,
-            lambda i: i ^ 1,
         ]
     return [lambda i: i ^ 1][: count - 1]
 
@@ -235,31 +298,38 @@
     return order
 
 
-def deal_kernel(place_s, keep_ref, recv_ref, qg1, qg2, qg3, own_ref, far1, far2, far3, sum_ref, *, sizes):
-    x_here, z_here, rep = place_s[0], place_s[1], place_s[3]
-    x_count, z_count, reps = sizes
-    share = keep_ref.shape[1] // reps
+def split_kernel(place_s, keep_ref, recv_ref, stay_ref, give_ref, sum_ref, *, sizes):
+    x_here, z_here = place_s[0], place_s[1]
+    x_count, z_count = sizes
+    half = z_count // 2
     sum_ref[...] = keep_ref[...] + recv_ref[...].astype(F32)
-    order = [
-        px * z_count + pz
-        for px in halving_order(x_here, x_partners(x_count))
-        for pz in halving_order(z_here, z_partners(z_count))
-    ]
+    z_order = halving_order(z_here, z_partners(z_count))
+    for at, px in enumerate(halving_order(x_here, x_partners(x_count))):
+        for k in range(half):
+            stay_ref[at * half + k] = sum_ref[px * z_count + z_order[k]]
+            give_ref[at * half + k] = sum_ref[px * z_count + z_order[half + k]].astype(BF16)
+
+
+def deal_kernel(place_s, stay_ref, recv_ref, qg1, qg2, qg3, own_ref, far1, far2, far3, sum_ref):
+    rep = place_s[3]
+    chunks = stay_ref.shape[0]
+    share = own_ref.shape[0] // chunks
+    reps = stay_ref.shape[1] // share
+    sum_ref[...] = stay_ref[...] + recv_ref[...].astype(F32)
     for k, out in enumerate((own_ref, far1, far2, far3)):
         owner = lax.rem(rep + k, reps)
         at = pl.ds(pl.multiple_of(owner * share, share), share)
-        for pair in range(len(order) // 2):
+        for pair in range(chunks // 2):
             rows = jnp.concatenate(
-                [sum_ref[order[2 * pair], at, :], sum_ref[order[2 * pair + 1], at, :]], axis=0
+                [sum_ref[2 * pair, at, :], sum_ref[2 * pair + 1, at, :]], axis=0
             )
             out[2 * pair * share : (2 * pair + 2) * share, :] = rows.astype(out.dtype)
-    dealt = len(order) * share
+    dealt = own_ref.shape[0]
     for out, part in zip((far1, far2, far3), (qg1, qg2, qg3)):
         out[dealt : dealt + part.shape[0], :] = part[...]
 
 
-def return_kernel(slot_j, ret_ref, unit_ref, inv_ref, book_ref, more_ref, out_ref, total_ref, *sums):
-    total_ref[...] = book_ref[...] + more_ref[...].astype(F32)
+def return_kernel(slot_j, ret_ref, unit_ref, inv_ref, out_ref, *sums):
     for part in sums:
         part[...] = jnp.zeros(part.shape, F32)
     for slot in range(ret_ref.shape[0]):
@@ -277,26 +347,13 @@
         )
 
 
-def unit_rows(local_codes, codebooks):
-    iota = jnp.arange(CODES, dtype=jnp.int32)
-    pieces = [
-        (local_codes[book][:, None] == iota[None, :]).astype(BF16)
-        for book in range(local_codes.shape[0])
-    ]
-    quant = jnp.dot(jnp.concatenate(pieces, axis=1), codebooks, preferred_element_type=F32)
-    inverse = lax.rsqrt(jnp.sum(quant * quant, axis=1, keepdims=True) + EPS)
-    return (quant * inverse, inverse)
-
-
 def shifted(x, k):
     count = lax.axis_size("rep")
     return lax.ppermute(x, "rep", [(i, (i + k) % count) for i in range(count)])
 
 
-def halved(own, axis, partner):
-    half = own.shape[0] // 2
-    pairs = [(i, partner(i)) for i in range(lax.axis_size(axis))]
-    return own[:half], lax.ppermute(own[half:].astype(BF16), axis, pairs)
+def stepped(x, axis, partner):
+    return lax.ppermute(x, axis, [(i, partner(i)) for i in range(lax.axis_size(axis))])
 
 
 def shards(query_embed, positive_ids, pair_blocks, code_ids, codebooks):
@@ -304,7 +361,6 @@
     x_count, z_count, cores = (lax.axis_size(a) for a in BLK)
     owners = x_count * z_count * cores
     here_blk = lax.axis_index(BLK)
-    here_rep = lax.axis_index("rep")
     rows_mine = query_embed[0, 0]
     row_count, feat = rows_mine.shape
     all_rows = reps * row_count
@@ -313,30 +369,52 @@
     cols = pair_count * PR
     local_codes = code_ids[0, 0]
     place = jnp.stack([lax.axis_index(a) for a in AXES]).astype(jnp.int32)
-
+    near = [(i, i ^ 1) for i in range(reps)]
+    cross = [(i, reps - 1 - i) for i in range(reps)]
+    pairs_in = wanted[None, :]
     held = local_codes.shape[1]
+
+    rows_near = lax.ppermute(rows_mine, "rep", near)
     message = call(
-        pack_kernel, sds((owners, BOOKS, LANES), BF16), [], 0, 2, owners * BOOKS * LANES
-    )(local_codes, wanted[None, :])
+        pack_kernel,
+        sds((owners, BOOKS, LANES), BF16),
+        [
+            pltpu.VMEM((BOOKS, held), jnp.int32),
+            pltpu.VMEM((1, pair_count), jnp.int32),
+            pltpu.SemaphoreType.DMA((2,)),
+        ],
+        0,
+        0,
+        owners * BOOKS * LANES,
+        2,
+        WHOLE_VMEM,
+    )(local_codes, pairs_in)
     arrived = lax.all_to_all(message, BLK, 0, 0, tiled=True)
-    query_parts = [rows_mine] + [shifted(rows_mine, k) for k in range(1, reps)]
-
-    targets = positive_ids[0].reshape(1, all_rows)
-    row_in = targets % (PR * reps)
-    tkey = jnp.where(
-        row_in // PR == here_rep, (targets // (PR * reps)) * PR + row_in % PR, -1
-    ).astype(jnp.int32)
-    owner_of = wanted // PBLK_DEV
-    before_me = jnp.sum(
-        ((owner_of[None, :] == owner_of[:, None]) & (wanted[None, :] < wanted[:, None])).astype(
-            jnp.int32
+    rows_pair = jnp.concatenate([rows_mine, rows_near], axis=0)
+    rows_far = lax.ppermute(rows_pair, "rep", cross)
+    pairs, slot_of, tkey, turned_books, unit, inverse_wide = call(
+        side_kernel,
+        (
+            sds((1, pair_count), jnp.int32),
+            sds((1, pair_count), jnp.int32),
+            sds((1, all_rows), jnp.int32),
+            sds((feat, BOOKS * CODES), BF16),
+            sds((held, feat), F32),
+            sds((held, LANES), F32),
         ),
-        axis=1,
-    )
-    slot_of = owner_of * CAP + before_me
-    turned_books = codebooks.T
-    unit, inverse = unit_rows(local_codes, codebooks)
-    inverse_wide = jnp.broadcast_to(inverse, (inverse.shape[0], LANES))
+        [
+            pltpu.VMEM((BOOKS, held), jnp.int32),
+            pltpu.VMEM((1, pair_count), jnp.int32),
+            pltpu.VMEM((reps, row_count), jnp.int32),
+            pltpu.VMEM((BOOKS * CODES, feat), BF16),
+            pltpu.VMEM((BOOKS, held), F32),
+            pltpu.SemaphoreType.DMA((4,)),
+        ],
+        1,
+        0,
+        2 * BOOKS * CODES * feat * held,
+        4,
+    )(place, local_codes, pairs_in, positive_ids[0], codebooks)
 
     units, queries, stats, codes, unit_t, inv_t = call(
         stats_kernel,
@@ -350,12 +428,13 @@
         ),
         [pltpu.VMEM((owners * BOOKS, LANES), F32), pltpu.VMEM((cols, LANES), jnp.int32)],
         2,
-        7,
+        5,
         2 * cols * feat * (BOOKS * CODES + all_rows),
-    )(wanted, place, arrived.reshape(owners * BOOKS, LANES), *query_parts, tkey, turned_books)
-
-    near = [(i, i ^ 1) for i in range(reps)]
-    cross = [(i, reps - 1 - i) for i in range(reps)]
+    )(
+        pairs, place, arrived.reshape(owners * BOOKS, LANES),
+        rows_pair, rows_far, tkey, turned_books,
+    )
+
     stats_near = lax.ppermute(stats, "rep", near)
     hot = call(hot_kernel, sds((BOOKS, CODES, cols), BF16), [], 0, 1, BOOKS * CODES * cols)(codes)
     stats_two = jnp.concatenate(merged(stats, stats_near), axis=0)
@@ -384,34 +463,48 @@
         3,
         8,
         cols * feat * (6 * all_rows + 2 * BOOKS * CODES),
-    )(wanted, slot_of, place, stats_two, stats_far, tkey, units, queries, unit_t, inv_t, hot)
+    )(pairs, slot_of, place, stats_two, stats_far, tkey, units, queries, unit_t, inv_t, hot)
 
     outbound = outbound.reshape(owners, CAP * PR, feat)
     returned = lax.all_to_all(outbound, BLK, 0, 0, tiled=True)
     returned = returned.reshape(owners * CAP, PR, feat)
 
     other = lax.ppermute(give, "c", [(0, 1), (1, 0)])
+    steps = [("z", partner) for partner in z_partners(z_count)]
+    steps = steps[:1] + [("x", partner) for partner in x_partners(x_count)] + steps[1:]
+    held_chunks = chunks // 2
+    stay, pass_on = call(
+        functools.partial(split_kernel, sizes=(x_count, z_count)),
+        (
+            sds((held_chunks, half_rows, feat), F32),
+            sds((held_chunks, half_rows, feat), BF16),
+        ),
+        [pltpu.VMEM((chunks, half_rows, feat), F32)],
+        1,
+        2,
+        cols * feat,
+    )(place, keep, other)
+    passed = stepped(pass_on, *steps[0])
     share_rows = half_rows // reps
-    dealt = chunks * share_rows
+    dealt = held_chunks * share_rows
     mine, *parts = call(
-        functools.partial(deal_kernel, sizes=(x_count, z_count, reps)),
+        deal_kernel,
         (sds((dealt, feat), F32), *[sds((dealt + feat, row_count), BF16)] * 3),
-        [pltpu.VMEM((chunks, half_rows, feat), F32)],
+        [pltpu.VMEM((held_chunks, half_rows, feat), F32)],
         1,
         5,
         cols * feat,
-    )(place, keep, other, far1, far2, far3)
+    )(place, stay, passed, far1, far2, far3)
     parts = [shifted(part, k + 1) for k, part in enumerate(parts)]
     query_grad_t = own_t
     for part in parts:
         mine = mine + part[:dealt].astype(F32)
         query_grad_t = query_grad_t + part[dealt:].astype(F32)
-    steps = [("x", partner) for partner in x_partners(x_count)]
-    steps += [("z", partner) for partner in z_partners(z_count)]
-    for axis, partner in steps[:-1]:
-        kept, more = halved(mine, axis, partner)
-        mine = kept + more.astype(F32)
-    book_kept, book_more = halved(mine, *steps[-1])
+    for axis, partner in steps[1:]:
+        half = mine.shape[0] // 2
+        more = stepped(mine[half:].astype(BF16), axis, partner)
+        mine = mine[:half] + more.astype(F32)
+    codebook_grad = mine
 
     directory = arrived[:, 0, held : held + pair_count].astype(jnp.int32)
     local_iota = jnp.arange(PBLK_DEV, dtype=jnp.int32)
@@ -427,14 +520,14 @@
             rank = rank + named[:, j].astype(jnp.int32)
         slot_j.append(found)
     slot_j = jnp.stack(slot_j, axis=1).reshape(-1)
-    passage_grad, codebook_grad = call(
+    passage_grad = call(
         return_kernel,
-        (sds((PBLK_DEV * PR, feat), F32), sds((share_rows, feat), F32)),
+        sds((PBLK_DEV * PR, feat), F32),
         [pltpu.VMEM((PBLK_DEV + 1, PR, feat), F32) for _ in range(4)],
         1,
-        5,
+        3,
         owners * CAP * PR * feat,
-    )(slot_j, returned, unit, inverse_wide, book_kept, book_more)
+    )(slot_j, returned, unit, inverse_wide)
     return (
         loss[None],
         query_grad_t.T[None, None],

time: 99 us -> 98.8 us (level)
  the two profiles are of different devices: /device:TPU:14 before, /device:TPU:32 now
where the time goes in v3:
time: 98.8 us; the launch traced here: 97.6 us
  waiting for transfers between devices  40.6 us (41%)
  starting transfers between devices  34.2 us (35%)
  Pallas kernels  15.5 us (16%)
  local copies, waits for them, and re-layouts  4.35 us (4%)
  other arithmetic  2.11 us (2%)
    ppermute x5, waiting for transfers between devices, stepped(): lax.ppermute(x, axis, [(i, partner(i)) for i in range(lax.axis_size(axis))])  13.7 us
    all_to_all x1, starting transfers between devices, shards(): arrived = lax.all_to_all(message, BLK, 0, 0, tiled=True)  11.6 us
    ppermute x3, waiting for transfers between devices, shifted(): return lax.ppermute(x, 'rep', [(i, (i + k) % count) for i in range(count)])  8.26 us
    ppermute x5, starting transfers between devices, stepped(): lax.ppermute(x, axis, [(i, partner(i)) for i in range(lax.axis_size(axis))])  8.11 us
    all_to_all x1, starting transfers between devices, shards(): returned = lax.all_to_all(outbound, BLK, 0, 0, tiled=True)  5.91 us
    all_to_all x1, waiting for transfers between devices, shards(): arrived = lax.all_to_all(message, BLK, 0, 0, tiled=True)  5.3 us
    pallas_call x1, Pallas kernels, shards(): call(grads_kernel, (sds((owners * CAP, PR, feat), BF16), sds((1, row_coun...  5.06 us
    unnamed x9, local copies, waits for them, and re-layouts  4.09 us
  transfers between devices with their start and end apart: 15, of which 12 were waited for; matrix products, arithmetic and copies ran while one was open for 2% of the time, Pallas kernels for 4%

profile of v3, /device:TPU:32, one launch (start us, length us, event | category | flops | bytes accessed | tf_op | source)
XLA Modules:
  0.0 97.6 jit_solution(12944953781708642054)
XLA Ops:
  0.6 1.7 %collective-permute-start = (bf16[256,256]{1,0:T(8,128)(2,1)}, bf16[256,256]{1,0:T(8,128)(2,1)S(1)}, u32[]{:S(2)}, u32[]{:S(2)}) collective-permute-start(bf16[256,256]{1,0:T(8,128)(2,1)} %bitcast.23), channel_id=1, source_target_pairs={{0,1},{1,0},{2,3},{3,2},{4,5},{5,4},{6,7},{7,6},{8,9},{9,8},{10,11... | collective-permute-start | bytes 393224 | tf_op jit(solution)/shard_map/ppermute | solution.py:377
  2.3 3.9 %collective-permute-done = bf16[256,256]{1,0:T(8,128)(2,1)S(1)} collective-permute-done((bf16[256,256]{1,0:T(8,128)(2,1)}, bf16[256,256]{1,0:T(8,128)(2,1)S(1)}, u32[]{:S(2)}, u32[]{:S(2)}) %collective-permute-start) | collective-permute-done | bytes 131104 | tf_op jit(solution)/shard_map/ppermute | solution.py:377
  6.2 0.9 pad_maximum_fusion.near_ref
  7.1 3.1 %collective-permute-start.1 = (bf16[512,256]{1,0:T(8,128)(2,1)S(1)}, bf16[512,256]{1,0:T(8,128)(2,1)S(1)}, u32[]{:S(2)}, u32[]{:S(2)}) collective-permute-start(bf16[512,256]{1,0:T(8,128)(2,1)S(1)} %pad_maximum_fusion.near_ref), channel_id=1, source_target_pairs={{0,3},{1,2},{2,1},{3,0},{4,7},{5,6},{6,5},{7,4},{8,11},{9,10},{10,... | collective-permute-start | bytes 786440 | tf_op jit(solution)/shard_map/ppermute | solution.py:394
  10.2 1.4 %shard_map.85 = bf16[64,8,128]{2,1,0:T(8,128)(2,1)} custom-call(s32[8,64]{1,0:T(8,128)} %bitcast.19, s32[1,64]{1,0:T(1,128)} %pairs_hbm.3), custom_call_target="tpu_custom_call" | custom-call | flops 65536 | bytes 262144 | tf_op jit(solution)/shard_map/pallas_call | solution.py:378
  11.6 11.6 %all-to-all-start = ((bf16[64,8,128]{2,1,0:T(8,128)(2,1)}), bf16[64,8,128]{2,1,0:T(8,128)(2,1)S(1)}, u32[]{:S(2)}, u32[]{:S(2)}) async-start(bf16[64,8,128]{2,1,0:T(8,128)(2,1)} %shard_map.85), calls=%async_computation | async-start | bytes 262144 | tf_op jit(solution)/shard_map/all_to_all | solution.py:392
  23.3 0.1 pad_add_fusion.1.place_s
  23.3 1.2 %copy-done = bf16[2048,256]{1,0:T(8,128)(2,1)S(1)} copy-done((bf16[2048,256]{1,0:T(8,128)(2,1)S(1)}, bf16[2048,256]{1,0:T(8,128)(2,1)}, u32[]{:S(2)}) %copy-start) | copy-done | bytes 1048600
  24.6 0.7 copy-done.1
  25.2 0.7 copy-done.2
  25.9 0.7 copy-done.3
  26.6 1.4 %shard_map.84 = (s32[1,64]{1,0:T(1,128)S(1)}, s32[1,64]{1,0:T(1,128)S(1)}, s32[1,1024]{1,0:T(1,128)S(1)}, bf16[256,2048]{1,0:T(8,128)(2,1)S(1)}, f32[64,256]{1,0:T(8,128)S(1)}, /*index=5*/f32[64,128]{1,0:T(8,128)S(1)}) custom-call(s32[4]{0:T(128)S(1)} %pad_add_fusion.1.place_s, s32[8,64]{1,0:T(8,128)S(1)} %bitcast.20, s32[1,64]{1,0:T(1,128)S(1)} %copy-done.3, ...), custom_call_target="tpu_custom_call" | custom-call | flops 67108864 | bytes 2302976 | tf_op jit(solution)/shard_map/pallas_call | solution.py:395
  28.0 5.3 %all-to-all-done = bf16[64,8,128]{2,1,0:T(8,128)(2,1)S(1)} async-done(((bf16[64,8,128]{2,1,0:T(8,128)(2,1)}), bf16[64,8,128]{2,1,0:T(8,128)(2,1)S(1)}, u32[]{:S(2)}, u32[]{:S(2)}) %all-to-all-start) | async-done | bytes 131104 | tf_op jit(solution)/shard_map/all_to_all | solution.py:392
  33.3 4.0 %shard_map.86 = (bf16[1024,256]{1,0:T(8,128)(2,1)S(1)}, bf16[1024,256]{1,0:T(8,128)(2,1)S(1)}, f32[3,1024]{1,0:T(4,128)S(1)}, f32[8,1024]{1,0:T(8,128)S(1)}, f32...) custom-call(s32[1,64]{1,0:T(1,128)S(1)} %get-tuple-element.30.pair_s, s32[4]{0:T(128)S(1)} %pad_add_fusion.1.place_s, ...), custom_call_target="tpu_custom_call" | custom-call | flops 1610612736 | bytes 4292608 | tf_op jit(solution)/shard_map/pallas_call | solution.py:419
  37.2 0.2 collective-permute-start.2
  37.5 3.6 %collective-permute-done.2 = f32[3,1024]{1,0:T(4,128)S(1)} collective-permute-done((f32[3,1024]{1,0:T(4,128)S(1)}, f32[3,1024]{1,0:T(4,128)S(1)}, u32[]{:S(2)}, u32[]{:S(2)}) %collective-permute-start.2) | collective-permute-done | bytes 12320 | tf_op jit(solution)/shard_map/ppermute | solution.py:438
  41.1 0.3 collective-permute-start.3
  41.4 0.7 shard_map.87.hot_ref
  42.1 4.0 %collective-permute-done.3.stb_ref = f32[3,1024]{1,0:T(4,128)S(1)} collective-permute-done((f32[3,1024]{1,0:T(4,128)S(1)}, f32[3,1024]{1,0:T(4,128)S(1)}, u32[]{:S(2)}, u32[]{:S(2)}) %collective-permute-start.3) | collective-permute-done | bytes 12320 | tf_op jit(solution)/shard_map/ppermute | solution.py:441
  46.2 5.1 %shard_map.88 = (bf16[128,16,256]{2,1,0:T(8,128)(2,1)}, f32[1,256]{1,0:T(1,128)}, f32[256,256]{1,0:T(8,128)S(1)}, bf16[256,256]{1,0:T(8,128)(2,1)S(1)}, bf16[256...) custom-call(s32[1,64]{1,0:T(1,128)S(1)} %get-tuple-element.30.pair_s, ...), custom_call_target="tpu_custom_call" | custom-call | flops 2684354560 | bytes 6555648 | tf_op jit(solution)/shard_map/pallas_call | solution.py:446
  51.2 1.9 %collective-permute-done.4.recv_ref = bf16[32,32,256]{2,1,0:T(8,128)(2,1)S(1)} collective-permute-done((bf16[32,32,256]{2,1,0:T(8,128)(2,1)S(1)}, bf16[32,32,256]{2,1,0:T(8,128)(2,1)S(1)}, u32[]{:S(2)}, u32[]{:S(2)}) %collective-permute-start.4) | collective-permute-done | bytes 524320 | tf_op jit(solution)/shard_map/ppermute | solution.py:472
  53.1 0.7 shard_map.89
  53.9 1.0 %collective-permute-start.5 = (bf16[16,32,256]{2,1,0:T(8,128)(2,1)S(1)}, bf16[16,32,256]{2,1,0:T(8,128)(2,1)S(1)}, u32[]{:S(2)}, u32[]{:S(2)}) collective-permute-start(bf16[16,32,256]{2,1,0:T(8,128)(2,1)S(1)} %get-tuple-element.45), channel_id=1, source_target_pairs={{0,8},{8,0},{16,24},{24,16},{32,40},{40,32},{48,56},{56,48},{1,9},... | collective-permute-start | bytes 786440 | tf_op jit(solution)/shard_map/ppermute | solution.py:356
  54.8 5.9 %all-to-all-start.1 = ((bf16[64,32,256]{2,1,0:T(8,128)(2,1)}), bf16[64,32,256]{2,1,0:T(8,128)(2,1)S(1)}, u32[]{:S(2)}, u32[]{:S(2)}) async-start(bf16[64,32,256]{2,1,0:T(8,128)(2,1)} %bitcast.12), calls=%async_computation.1 | async-start | bytes 2097152 | tf_op jit(solution)/shard_map/all_to_all | solution.py:469
  60.8 2.2 %collective-permute-done.5.recv_ref = bf16[16,32,256]{2,1,0:T(8,128)(2,1)S(1)} collective-permute-done((bf16[16,32,256]{2,1,0:T(8,128)(2,1)S(1)}, bf16[16,32,256]{2,1,0:T(8,128)(2,1)S(1)}, u32[]{:S(2)}, u32[]{:S(2)}) %collective-permute-start.5) | collective-permute-done | bytes 262176 | tf_op jit(solution)/shard_map/ppermute | solution.py:356
  63.0 0.7 shard_map.90
  63.7 0.1 collective-permute-start.6
  63.8 1.7 %collective-permute-start.7 = (bf16[384,256]{1,0:T(8,128)(2,1)S(1)}, bf16[384,256]{1,0:T(8,128)(2,1)S(1)}, u32[]{:S(2)}, u32[]{:S(2)}) collective-permute-start(bf16[384,256]{1,0:T(8,128)(2,1)S(1)} %get-tuple-element.50), channel_id=1, source_target_pairs={{0,2},{1,3},{2,0},{3,1},{4,6},{5,7},{6,4},{7,5},{8,10},{9,11},{10,... | collective-permute-start | bytes 589832 | tf_op jit(solution)/shard_map/ppermute | solution.py:352
  65.4 1.6 %collective-permute-start.8 = (bf16[384,256]{1,0:T(8,128)(2,1)S(1)}, bf16[384,256]{1,0:T(8,128)(2,1)S(1)}, u32[]{:S(2)}, u32[]{:S(2)}) collective-permute-start(bf16[384,256]{1,0:T(8,128)(2,1)S(1)} %get-tuple-element.51), channel_id=1, source_target_pairs={{0,3},{1,0},{2,1},{3,2},{4,7},{5,4},{6,5},{7,6},{8,11},{9,8},{10,9... | collective-permute-start | bytes 589832 | tf_op jit(solution)/shard_map/ppermute | solution.py:352
  67.0 0.1 slice_convert_fusion.2
  67.1 7.6 %collective-permute-done.6 = bf16[384,256]{1,0:T(8,128)(2,1)S(1)} collective-permute-done((bf16[384,256]{1,0:T(8,128)(2,1)S(1)}, bf16[384,256]{1,0:T(8,128)(2,1)S(1)}, u32[]{:S(2)}, u32[]{:S(2)}) %collective-permute-start.6) | collective-permute-done | bytes 196640 | tf_op jit(solution)/shard_map/ppermute | solution.py:352
  74.8 0.6 collective-permute-done.8
  75.4 0.8 collective-permute-start.9
  76.2 0.2 compare_reduce_fusion
  76.4 3.4 %collective-permute-done.9 = bf16[64,256]{1,0:T(8,128)(2,1)S(1)} collective-permute-done((bf16[64,256]{1,0:T(8,128)(2,1)S(1)}, bf16[64,256]{1,0:T(8,128)(2,1)S(1)}, u32[]{:S(2)}, u32[]{:S(2)}) %collective-permute-start.9) | collective-permute-done | bytes 32800 | tf_op jit(solution)/shard_map/ppermute | solution.py:356
  79.8 2.1 %collective-permute-start.10 = (bf16[32,256]{1,0:T(8,128)(2,1)S(1)}, bf16[32,256]{1,0:T(8,128)(2,1)S(1)}, u32[]{:S(2)}, u32[]{:S(2)}) collective-permute-start(bf16[32,256]{1,0:T(8,128)(2,1)S(1)} %slice.175), channel_id=1, source_target_pairs={{0,192},{64,128},{128,64},{192,0},{1,193},{65,129},{129,65},{193,1... | collective-permute-start | bytes 49160 | tf_op jit(solution)/shard_map/ppermute | solution.py:356
  81.9 3.1 %collective-permute-done.10 = bf16[32,256]{1,0:T(8,128)(2,1)S(1)} collective-permute-done((bf16[32,256]{1,0:T(8,128)(2,1)S(1)}, bf16[32,256]{1,0:T(8,128)(2,1)S(1)}, u32[]{:S(2)}, u32[]{:S(2)}) %collective-permute-start.10) | collective-permute-done | bytes 16416 | tf_op jit(solution)/shard_map/ppermute | solution.py:356
  85.0 0.5 collective-permute-start.11
  85.5 0.1 copy.13
  85.6 0.1 reshape.33.slot_j
  85.8 3.0 %collective-permute-done.11 = bf16[16,256]{1,0:T(8,128)(2,1)S(1)} collective-permute-done((bf16[16,256]{1,0:T(8,128)(2,1)S(1)}, bf16[16,256]{1,0:T(8,128)(2,1)S(1)}, u32[]{:S(2)}, u32[]{:S(2)}) %collective-permute-start.11) | collective-permute-done | bytes 8224 | tf_op jit(solution)/shard_map/ppermute | solution.py:356
  88.7 3.8 %collective-permute-start.12 = (bf16[8,256]{1,0:T(8,128)(2,1)S(1)}, bf16[8,256]{1,0:T(8,128)(2,1)S(1)}, u32[]{:S(2)}, u32[]{:S(2)}) collective-permute-start(bf16[8,256]{1,0:T(8,128)(2,1)S(1)} %slice.177), channel_id=1, source_target_pairs={{0,24},{8,48},{16,40},{24,0},{32,56},{40,16},{48,8},{56,32},{1,25}... | collective-permute-start | bytes 12296 | tf_op jit(solution)/shard_map/ppermute | solution.py:356
  92.5 0.1 add_bitcast_fusion
  92.6 0.8 copy.14
  93.4 2.0 %collective-permute-done.12 = bf16[8,256]{1,0:T(8,128)(2,1)S(1)} collective-permute-done((bf16[8,256]{1,0:T(8,128)(2,1)S(1)}, bf16[8,256]{1,0:T(8,128)(2,1)S(1)}, u32[]{:S(2)}, u32[]{:S(2)}) %collective-permute-start.12) | collective-permute-done | bytes 4128 | tf_op jit(solution)/shard_map/ppermute | solution.py:356
  95.4 0.6 slice_add_fusion.3
  96.0 0.0 all-to-all-done.1
  96.0 1.5 %shard_map.91 = f32[64,256]{1,0:T(8,128)} custom-call(s32[128]{0:T(128)S(1)} %reshape.33.slot_j, bf16[128,16,256]{2,1,0:T(8,128)(2,1)S(1)} %bitcast.17, f32[64,256]{1,0:T(8,128)S(1)} %get-tuple-element.53.unit_ref, f32[64,128]{1,0:T(8,128)S(1)} %get-tuple-element.54.inv_ref), custom_call_target="tpu_custom_call" | custom-call | flops 524288 | bytes 131072 | tf_op jit(solution)/shard_map/pallas_call | solution.py:523
  (20 shorter events, 0.2 us)
Async XLA Ops:
  0.6 5.5 %collective-permute-start = (bf16[256,256]{1,0:T(8,128)(2,1)}, bf16[256,256]{1,0:T(8,128)(2,1)S(1)}, u32[]{:S(2)}, u32[]{:S(2)}) collective-permute-start(bf16[256,256]{1,0:T(8,128)(2,1)} %bitcast.23), channel_id=1, source_target_pairs={{0,1},{1,0},{2,3},{3,2},{4,5},{5,4},{6,7},{7,6},{8,9},{9,8},{10,11... | collective-permute-start | bytes 393224 | tf_op jit(solution)/shard_map/ppermute | solution.py:377
  7.1 26.2 %collective-permute-start.1 = (bf16[512,256]{1,0:T(8,128)(2,1)S(1)}, bf16[512,256]{1,0:T(8,128)(2,1)S(1)}, u32[]{:S(2)}, u32[]{:S(2)}) collective-permute-start(bf16[512,256]{1,0:T(8,128)(2,1)S(1)} %pad_maximum_fusion.near_ref), channel_id=1, source_target_pairs={{0,3},{1,2},{2,1},{3,0},{4,7},{5,6},{6,5},{7,4},{8,11},{9,10},{10,... | collective-permute-start | bytes 786440 | tf_op jit(solution)/shard_map/ppermute | solution.py:394
  11.6 21.6 %all-to-all-start = ((bf16[64,8,128]{2,1,0:T(8,128)(2,1)}), bf16[64,8,128]{2,1,0:T(8,128)(2,1)S(1)}, u32[]{:S(2)}, u32[]{:S(2)}) async-start(bf16[64,8,128]{2,1,0:T(8,128)(2,1)} %shard_map.85), calls=%async_computation | async-start | bytes 262144 | tf_op jit(solution)/shard_map/all_to_all | solution.py:392
  23.3 1.2 %copy-start = (bf16[2048,256]{1,0:T(8,128)(2,1)S(1)}, bf16[2048,256]{1,0:T(8,128)(2,1)}, u32[]{:S(2)}) copy-start(bf16[2048,256]{1,0:T(8,128)(2,1)} %books_hbm.1) | copy-start | bytes 3145732
  24.6 0.7 copy-start.1
  25.2 0.7 copy-start.2
  25.9 0.7 copy-start.3
  37.2 3.8 %collective-permute-start.2 = (f32[3,1024]{1,0:T(4,128)S(1)}, f32[3,1024]{1,0:T(4,128)S(1)}, u32[]{:S(2)}, u32[]{:S(2)}) collective-permute-start(f32[3,1024]{1,0:T(4,128)S(1)} %get-tuple-element.34), channel_id=1, source_target_pairs={{0,1},{1,0},{2,3},{3,2},{4,5},{5,4},{6,7},{7,6},{8,9},{9,8},{10,11... | collective-permute-start | bytes 36872 | tf_op jit(solution)/shard_map/ppermute | solution.py:438
  41.1 5.0 %collective-permute-start.3 = (f32[3,1024]{1,0:T(4,128)S(1)}, f32[3,1024]{1,0:T(4,128)S(1)}, u32[]{:S(2)}, u32[]{:S(2)}) collective-permute-start(f32[3,1024]{1,0:T(4,128)S(1)} %pad_maximum_fusion.1.sta_ref), channel_id=1, source_target_pairs={{0,3},{1,2},{2,1},{3,0},{4,7},{5,6},{6,5},{7,4},{8,11},{9,10},{10,... | collective-permute-start | bytes 36872 | tf_op jit(solution)/shard_map/ppermute | solution.py:441
  51.2 1.9 %collective-permute-start.4 = (bf16[32,32,256]{2,1,0:T(8,128)(2,1)S(1)}, bf16[32,32,256]{2,1,0:T(8,128)(2,1)S(1)}, u32[]{:S(2)}, u32[]{:S(2)}) collective-permute-start(bf16[32,32,256]{2,1,0:T(8,128)(2,1)S(1)} %get-tuple-element.43), channel_id=1, source_target_pairs={{0,4},{4,0},{1,5},{5,1},{2,6},{6,2},{3,7},{7,3},{8,12},{12,8},{9,1... | collective-permute-start | bytes 1572872 | tf_op jit(solution)/shard_map/ppermute | solution.py:472
  53.9 9.1 %collective-permute-start.5 = (bf16[16,32,256]{2,1,0:T(8,128)(2,1)S(1)}, bf16[16,32,256]{2,1,0:T(8,128)(2,1)S(1)}, u32[]{:S(2)}, u32[]{:S(2)}) collective-permute-start(bf16[16,32,256]{2,1,0:T(8,128)(2,1)S(1)} %get-tuple-element.45), channel_id=1, source_target_pairs={{0,8},{8,0},{16,24},{24,16},{32,40},{40,32},{48,56},{56,48},{1,9},... | collective-permute-start | bytes 786440 | tf_op jit(solution)/shard_map/ppermute | solution.py:356
  54.8 41.2 %all-to-all-start.1 = ((bf16[64,32,256]{2,1,0:T(8,128)(2,1)}), bf16[64,32,256]{2,1,0:T(8,128)(2,1)S(1)}, u32[]{:S(2)}, u32[]{:S(2)}) async-start(bf16[64,32,256]{2,1,0:T(8,128)(2,1)} %bitcast.12), calls=%async_computation.1 | async-start | bytes 2097152 | tf_op jit(solution)/shard_map/all_to_all | solution.py:469
  63.7 11.1 %collective-permute-start.6 = (bf16[384,256]{1,0:T(8,128)(2,1)S(1)}, bf16[384,256]{1,0:T(8,128)(2,1)S(1)}, u32[]{:S(2)}, u32[]{:S(2)}) collective-permute-start(bf16[384,256]{1,0:T(8,128)(2,1)S(1)} %get-tuple-element.49), channel_id=1, source_target_pairs={{0,1},{1,2},{2,3},{3,0},{4,5},{5,6},{6,7},{7,4},{8,9},{9,10},{10,1... | collective-permute-start | bytes 589832 | tf_op jit(solution)/shard_map/ppermute | solution.py:352
  63.8 11.0 %collective-permute-start.7 = (bf16[384,256]{1,0:T(8,128)(2,1)S(1)}, bf16[384,256]{1,0:T(8,128)(2,1)S(1)}, u32[]{:S(2)}, u32[]{:S(2)}) collective-permute-start(bf16[384,256]{1,0:T(8,128)(2,1)S(1)} %get-tuple-element.50), channel_id=1, source_target_pairs={{0,2},{1,3},{2,0},{3,1},{4,6},{5,7},{6,4},{7,5},{8,10},{9,11},{10,... | collective-permute-start | bytes 589832 | tf_op jit(solution)/shard_map/ppermute | solution.py:352
  65.4 9.9 %collective-permute-start.8 = (bf16[384,256]{1,0:T(8,128)(2,1)S(1)}, bf16[384,256]{1,0:T(8,128)(2,1)S(1)}, u32[]{:S(2)}, u32[]{:S(2)}) collective-permute-start(bf16[384,256]{1,0:T(8,128)(2,1)S(1)} %get-tuple-element.51), channel_id=1, source_target_pairs={{0,3},{1,0},{2,1},{3,2},{4,7},{5,4},{6,5},{7,6},{8,11},{9,8},{10,9... | collective-permute-start | bytes 589832 | tf_op jit(solution)/shard_map/ppermute | solution.py:352
  75.4 4.3 %collective-permute-start.9 = (bf16[64,256]{1,0:T(8,128)(2,1)S(1)}, bf16[64,256]{1,0:T(8,128)(2,1)S(1)}, u32[]{:S(2)}, u32[]{:S(2)}) collective-permute-start(bf16[64,256]{1,0:T(8,128)(2,1)S(1)} %slice.174), channel_id=1, source_target_pairs={{0,64},{64,0},{128,192},{192,128},{1,65},{65,1},{129,193},{193,129... | collective-permute-start | bytes 98312 | tf_op jit(solution)/shard_map/ppermute | solution.py:356
  79.8 5.2 %collective-permute-start.10 = (bf16[32,256]{1,0:T(8,128)(2,1)S(1)}, bf16[32,256]{1,0:T(8,128)(2,1)S(1)}, u32[]{:S(2)}, u32[]{:S(2)}) collective-permute-start(bf16[32,256]{1,0:T(8,128)(2,1)S(1)} %slice.175), channel_id=1, source_target_pairs={{0,192},{64,128},{128,64},{192,0},{1,193},{65,129},{129,65},{193,1... | collective-permute-start | bytes 49160 | tf_op jit(solution)/shard_map/ppermute | solution.py:356
  85.0 3.7 %collective-permute-start.11 = (bf16[16,256]{1,0:T(8,128)(2,1)S(1)}, bf16[16,256]{1,0:T(8,128)(2,1)S(1)}, u32[]{:S(2)}, u32[]{:S(2)}) collective-permute-start(bf16[16,256]{1,0:T(8,128)(2,1)S(1)} %slice.176), channel_id=1, source_target_pairs={{0,56},{8,16},{16,8},{24,32},{32,24},{40,48},{48,40},{56,0},{1,57}... | collective-permute-start | bytes 24584 | tf_op jit(solution)/shard_map/ppermute | solution.py:356
  88.7 6.7 %collective-permute-start.12 = (bf16[8,256]{1,0:T(8,128)(2,1)S(1)}, bf16[8,256]{1,0:T(8,128)(2,1)S(1)}, u32[]{:S(2)}, u32[]{:S(2)}) collective-permute-start(bf16[8,256]{1,0:T(8,128)(2,1)S(1)} %slice.177), channel_id=1, source_target_pairs={{0,24},{8,48},{16,40},{24,0},{32,56},{40,16},{48,8},{56,32},{1,25}... | collective-permute-start | bytes 12296 | tf_op jit(solution)/shard_map/ppermute | solution.py:356

commit v4 on v3

--- a/solution.py
+++ b/solution.py
@@ -19,7 +19,7 @@
 BLK = ("x", "z", "c")
 EPS = 1e-06
 INTERPRET = False
-VMEM_LIMIT = 24 << 20
+VMEM_LIMIT = 10 << 20
 WHOLE_VMEM = 63_000_000
 
 F32 = jnp.float32
@@ -136,9 +136,17 @@
     st_ref[2:3, :] = hit
 
 
-def hot_kernel(codes_ref, hot_ref):
+def hot_kernel(codes_ref, u_ref, q_ref, st_ref, hot_ref, exp_ref):
     for book in range(BOOKS):
         hot_ref[book] = one_hot_of(codes_ref, book, CODES)
+    cols = u_ref.shape[0]
+    step = min(256, cols)
+    for start in range(0, cols, step):
+        span = slice(start, start + step)
+        scores = lax.dot_general(
+            u_ref[span, :], q_ref[...], CONTRACT_LAST, preferred_element_type=F32
+        )
+        exp_ref[span, :] = jnp.exp(scores - st_ref[0:1, :])
 
 
 def pack_kernel(codes_hbm, pairs_hbm, out_ref, codes_ref, pairs_ref, sems):
@@ -162,7 +170,7 @@
 
 def side_kernel(
     place_s, codes_hbm, pairs_hbm, targets_hbm, books_hbm,
-    pairs_ref, slot_ref, tkey_ref, cbt_ref, unit_ref, inv_ref,
+    pairs_ref, slot_ref, tkey_ref, cbt_ref, unit_ref,
     codes_ref, near_ref, targets_ref, books_ref, float_ref, sems,
 ):
     moves = (
@@ -195,7 +203,7 @@
             mine, block * PR + within - rep * PR, -1
         )
     float_ref[...] = codes_ref[...].astype(F32)
-    quant = jnp.zeros(unit_ref.shape, F32)
+    quant = jnp.zeros((unit_ref.shape[0], cbt_ref.shape[0]), F32)
     for book in range(BOOKS):
         span = slice(book * CODES, (book + 1) * CODES)
         words = books_ref[span, :]
@@ -204,8 +212,9 @@
             one_hot_of(float_ref, book, CODES), words, CONTRACT_FIRST, preferred_element_type=F32
         )
     inverse = lax.rsqrt(jnp.sum(quant * quant, axis=1, keepdims=True) + EPS)
-    unit_ref[...] = quant * inverse
-    inv_ref[...] = jnp.broadcast_to(inverse, inv_ref.shape)
+    feat = quant.shape[1]
+    unit_ref[:, 0:feat] = quant * inverse
+    unit_ref[:, feat:] = jnp.broadcast_to(inverse, (quant.shape[0], LANES))
 
 
 def merged(first, second):
@@ -215,16 +224,19 @@
 
 
 def grads_kernel(
-    pair_s, slot_s, place_s, sta_ref, stb_ref, tkey_ref, u_ref, q_ref, unit_ref, inv_ref, hot_ref,
-    send_ref, loss_ref, own_ref, far1, far2, far3, keep_ref, give_ref,
-    key_ref, lse_ref, qgt_ref, pg_ref, sum_ref,
+    pair_s, slot_s, place_s,
+    st_ref, sta_ref, stb_ref, tkey_ref, u_ref, q_ref, unit_ref, inv_ref, hot_ref, exp_ref,
+    send_ref, loss_ref, own_ref, far_ref, stay_ref, give_ref,
+    key_ref, lse_ref, qgt_ref, pg_ref, sum_ref, *, sizes,
 ):
     cols = u_ref.shape[0]
     pair_count = cols // PR
-    core, rep = place_s[2], place_s[3]
+    x_here, z_here, rep = place_s[0], place_s[1], place_s[3]
+    x_count, z_count = sizes
     rows = own_ref.shape[1]
     peak, total, hit = merged(sta_ref[...], stb_ref[...])
     lse = peak + jnp.log(total)
+    factor = jnp.exp(st_ref[0:1, :] - lse)
     lse_ref[0:1, :] = lse - hit
     loss_ref[...] = lse_ref[0:1, pl.ds(pl.multiple_of(rep * rows, rows), rows)]
     fill_keys(pair_s, key_ref, pair_count)
@@ -234,9 +246,8 @@
     for start in range(0, cols, step):
         span = slice(start, start + step)
         u_part = u_ref[span, :]
-        scores = lax.dot_general(u_part, q_ref[...], CONTRACT_LAST, preferred_element_type=F32)
         hit_mask = hits(key_ref, start, step, tkey_ref)
-        weight = (jnp.exp(scores - lse) - jnp.where(hit_mask, 1.0, 0.0)).astype(BF16)
+        weight = (exp_ref[span, :] * factor - jnp.where(hit_mask, 1.0, 0.0)).astype(BF16)
         grad = jnp.dot(weight, q_ref[...], preferred_element_type=F32)
         narrow = grad.astype(BF16)
         for place in range(step // PR):
@@ -249,21 +260,26 @@
         grown = term if grown is None else grown + term
     qgt_ref[...] = grown
     count = q_ref.shape[0] // rows
-    for k, out in enumerate((own_ref, far1, far2, far3)):
+    for k in range(count):
         owner = lax.rem(rep + k, count)
         part = qgt_ref[:, pl.ds(pl.multiple_of(owner * rows, rows), rows)]
-        out[...] = part.astype(out.dtype)
+        if k:
+            far_ref[k - 1] = part.astype(BF16)
+        else:
+            own_ref[...] = part
     for book in range(BOOKS):
         sum_ref[book * CODES : (book + 1) * CODES, :] = lax.dot_general(
             hot_ref[book], pg_ref[...], CONTRACT_LAST, preferred_element_type=F32
         )
-    half = keep_ref.shape[1]
-    for chunk in range(keep_ref.shape[0]):
-        base = chunk * 2 * half
-        keep_ref[chunk] = sum_ref[pl.ds(pl.multiple_of(base + core * half, half), half), :]
-        give_ref[chunk] = sum_ref[
-            pl.ds(pl.multiple_of(base + (1 - core) * half, half), half), :
-        ].astype(BF16)
+    half = z_count // 2
+    size = stay_ref.shape[1]
+    z_order = halving_order(z_here, z_partners(z_count))
+    for at, px in enumerate(halving_order(x_here, x_partners(x_count))):
+        for k in range(half):
+            near = pl.multiple_of((px * z_count + z_order[k]) * size, size)
+            there = pl.multiple_of((px * z_count + z_order[half + k]) * size, size)
+            stay_ref[at * half + k] = sum_ref[pl.ds(near, size), :]
+            give_ref[at * half + k] = sum_ref[pl.ds(there, size), :].astype(BF16)
 
 
 def x_partners(count):
@@ -298,19 +314,18 @@
     return order
 
 
-def split_kernel(place_s, keep_ref, recv_ref, stay_ref, give_ref, sum_ref, *, sizes):
-    x_here, z_here = place_s[0], place_s[1]
-    x_count, z_count = sizes
-    half = z_count // 2
-    sum_ref[...] = keep_ref[...] + recv_ref[...].astype(F32)
-    z_order = halving_order(z_here, z_partners(z_count))
-    for at, px in enumerate(halving_order(x_here, x_partners(x_count))):
-        for k in range(half):
-            stay_ref[at * half + k] = sum_ref[px * z_count + z_order[k]]
-            give_ref[at * half + k] = sum_ref[px * z_count + z_order[half + k]].astype(BF16)
-
-
-def deal_kernel(place_s, stay_ref, recv_ref, qg1, qg2, qg3, own_ref, far1, far2, far3, sum_ref):
+def split_kernel(place_s, stay_ref, recv_ref, keep_ref, give_ref, sum_ref):
+    core = place_s[2]
+    half = keep_ref.shape[1]
+    sum_ref[...] = stay_ref[...] + recv_ref[...].astype(F32)
+    mine = pl.ds(pl.multiple_of(core * half, half), half)
+    other = pl.ds(pl.multiple_of((1 - core) * half, half), half)
+    for chunk in range(keep_ref.shape[0]):
+        keep_ref[chunk] = sum_ref[chunk, mine, :]
+        give_ref[chunk] = sum_ref[chunk, other, :].astype(BF16)
+
+
+def deal_kernel(place_s, stay_ref, recv_ref, qg_ref, own_ref, far1, far2, far3, sum_ref):
     rep = place_s[3]
     chunks = stay_ref.shape[0]
     share = own_ref.shape[0] // chunks
@@ -325,11 +340,11 @@
             )
             out[2 * pair * share : (2 * pair + 2) * share, :] = rows.astype(out.dtype)
     dealt = own_ref.shape[0]
-    for out, part in zip((far1, far2, far3), (qg1, qg2, qg3)):
-        out[dealt : dealt + part.shape[0], :] = part[...]
-
-
-def return_kernel(slot_j, ret_ref, unit_ref, inv_ref, out_ref, *sums):
+    for k, out in enumerate((far1, far2, far3)):
+        out[dealt:, :] = qg_ref[k]
+
+
+def return_kernel(slot_j, ret_ref, unit_ref, out_ref, *sums):
     for part in sums:
         part[...] = jnp.zeros(part.shape, F32)
     for slot in range(ret_ref.shape[0]):
@@ -340,8 +355,9 @@
         grad = sums[0][j]
         for part in sums[1:]:
             grad = grad + part[j]
-        unit = unit_ref[j * PR : (j + 1) * PR, :]
-        inverse = inv_ref[j * PR : (j + 1) * PR, 0:1]
+        feat = out_ref.shape[1]
+        unit = unit_ref[j * PR : (j + 1) * PR, 0:feat]
+        inverse = unit_ref[j * PR : (j + 1) * PR, feat : feat + 1]
         out_ref[j * PR : (j + 1) * PR, :] = inverse * (
             grad - unit * jnp.sum(unit * grad, axis=1, keepdims=True)
         )
@@ -392,15 +408,14 @@
     arrived = lax.all_to_all(message, BLK, 0, 0, tiled=True)
     rows_pair = jnp.concatenate([rows_mine, rows_near], axis=0)
     rows_far = lax.ppermute(rows_pair, "rep", cross)
-    pairs, slot_of, tkey, turned_books, unit, inverse_wide = call(
+    pairs, slot_of, tkey, turned_books, unit = call(
         side_kernel,
         (
             sds((1, pair_count), jnp.int32),
             sds((1, pair_count), jnp.int32),
             sds((1, all_rows), jnp.int32),
             sds((feat, BOOKS * CODES), BF16),
-            sds((held, feat), F32),
-            sds((held, LANES), F32),
+            sds((held, feat + LANES), F32),
         ),
         [
             pltpu.VMEM((BOOKS, held), jnp.int32),
@@ -436,22 +451,30 @@
     )
 
     stats_near = lax.ppermute(stats, "rep", near)
-    hot = call(hot_kernel, sds((BOOKS, CODES, cols), BF16), [], 0, 1, BOOKS * CODES * cols)(codes)
+    hot, powers = call(
+        hot_kernel,
+        (sds((BOOKS, CODES, cols), BF16), sds((cols, all_rows), F32)),
+        [],
+        0,
+        4,
+        BOOKS * CODES * cols,
+    )(codes, units, queries, stats)
     stats_two = jnp.concatenate(merged(stats, stats_near), axis=0)
     stats_far = lax.ppermute(stats_two, "rep", cross)
 
     chunks = x_count * z_count
     chunk_rows = codebooks.shape[0] // chunks
     half_rows = chunk_rows // cores
-    outbound, loss, own_t, far1, far2, far3, keep, give = call(
-        grads_kernel,
+    held_chunks = chunks // 2
+    outbound, loss, own_t, far, stay, give = call(
+        functools.partial(grads_kernel, sizes=(x_count, z_count)),
         (
             sds((owners * CAP, PR, feat), BF16),
             sds((1, row_count), F32),
             sds((feat, row_count), F32),
-            *[sds((feat, row_count), BF16)] * 3,
-            sds((chunks, half_rows, feat), F32),
-            sds((chunks, half_rows, feat), BF16),
+            sds((reps - 1, feat, row_count), BF16),
+            sds((held_chunks, chunk_rows, feat), F32),
+            sds((held_chunks, chunk_rows, feat), BF16),
         ),
         [
             pltpu.VMEM((cols, LANES), jnp.int32),
@@ -461,30 +484,32 @@
             pltpu.VMEM((BOOKS * CODES, feat), F32),
         ],
         3,
-        8,
-        cols * feat * (6 * all_rows + 2 * BOOKS * CODES),
-    )(pairs, slot_of, place, stats_two, stats_far, tkey, units, queries, unit_t, inv_t, hot)
+        10,
+        cols * feat * (4 * all_rows + 2 * BOOKS * CODES),
+    )(
+        pairs, slot_of, place,
+        stats, stats_two, stats_far, tkey, units, queries, unit_t, inv_t, hot, powers,
+    )
 
     outbound = outbound.reshape(owners, CAP * PR, feat)
     returned = lax.all_to_all(outbound, BLK, 0, 0, tiled=True)
     returned = returned.reshape(owners * CAP, PR, feat)
 
-    other = lax.ppermute(give, "c", [(0, 1), (1, 0)])
     steps = [("z", partner) for partner in z_partners(z_count)]
     steps = steps[:1] + [("x", partner) for partner in x_partners(x_count)] + steps[1:]
-    held_chunks = chunks // 2
-    stay, pass_on = call(
-        functools.partial(split_kernel, sizes=(x_count, z_count)),
+    passed = stepped(give, *steps[0])
+    keep, hand = call(
+        split_kernel,
         (
             sds((held_chunks, half_rows, feat), F32),
             sds((held_chunks, half_rows, feat), BF16),
         ),
-        [pltpu.VMEM((chunks, half_rows, feat), F32)],
+        [pltpu.VMEM((held_chunks, chunk_rows, feat), F32)],
         1,
         2,
         cols * feat,
-    )(place, keep, other)
-    passed = stepped(pass_on, *steps[0])
+    )(place, stay, passed)
+    other = lax.ppermute(hand, "c", [(0, 1), (1, 0)])
     share_rows = half_rows // reps
     dealt = held_chunks * share_rows
     mine, *parts = call(
@@ -492,9 +517,9 @@
         (sds((dealt, feat), F32), *[sds((dealt + feat, row_count), BF16)] * 3),
         [pltpu.VMEM((held_chunks, half_rows, feat), F32)],
         1,
-        5,
+        3,
         cols * feat,
-    )(place, stay, passed, far1, far2, far3)
+    )(place, keep, other, far)
     parts = [shifted(part, k + 1) for k, part in enumerate(parts)]
     query_grad_t = own_t
     for part in parts:
@@ -525,9 +550,9 @@
         sds((PBLK_DEV * PR, feat), F32),
         [pltpu.VMEM((PBLK_DEV + 1, PR, feat), F32) for _ in range(4)],
         1,
-        3,
+        2,
         owners * CAP * PR * feat,
-    )(slot_j, returned, unit, inverse_wide)
+    )(slot_j, returned, unit)
     return (
         loss[None],
         query_grad_t.T[None, None],

time: 98.8 us -> 105 us (1.063)
  waiting for transfers between devices: 40.6 us -> 44 us
  starting transfers between devices: 34.2 us -> 37 us
    ppermute x5, waiting for transfers between devices: 13.7 us -> 18.6 us  [stepped(): lax.ppermute(x, axis, [(i, partner(i)) for i in range(lax.axis_size(axis))])]
    ppermute x5, starting transfers between devices: 8.11 us -> 11.5 us  [stepped(): lax.ppermute(x, axis, [(i, partner(i)) for i in range(lax.axis_size(axis))])]
    ppermute x1, waiting for transfers between devices: 1.91 us -> 0.01 us  [shards(): other = lax.ppermute(hand, 'c', [(0, 1), (1, 0)])]
    ppermute x3, waiting for transfers between devices: 8.26 us -> 9.61 us  [shifted(): return lax.ppermute(x, 'rep', [(i, (i + k) % count) for i in range(count)])]
  transfers between devices with their start and end apart: 15 -> 15, of which waited for: 12 -> 11; matrix products, arithmetic and copies ran while one was open for 2% -> 2% of each run, Pallas kernels for 4% -> 5%
where the time goes in v4:
time: 105 us; the launch traced here: 104 us
  waiting for transfers between devices  44 us (42%)
  starting transfers between devices  37 us (35%)
  Pallas kernels  16 us (15%)
  local copies, waits for them, and re-layouts  4.35 us (4%)
  other arithmetic  2.11 us (2%)
    ppermute x5, waiting for transfers between devices, stepped(): lax.ppermute(x, axis, [(i, partner(i)) for i in range(lax.axis_size(axis))])  18.6 us
    all_to_all x1, starting transfers between devices, shards(): arrived = lax.all_to_all(message, BLK, 0, 0, tiled=True)  11.6 us
    ppermute x5, starting transfers between devices, stepped(): lax.ppermute(x, axis, [(i, partner(i)) for i in range(lax.axis_size(axis))])  11.5 us
    ppermute x3, waiting for transfers between devices, shifted(): return lax.ppermute(x, 'rep', [(i, (i + k) % count) for i in range(count)])  9.61 us
    all_to_all x1, waiting for transfers between devices, shards(): arrived = lax.all_to_all(message, BLK, 0, 0, tiled=True)  5.3 us
    all_to_all x1, starting transfers between devices, shards(): returned = lax.all_to_all(outbound, BLK, 0, 0, tiled=True)  5.16 us
    pallas_call x1, Pallas kernels, shards(): call(functools.partial(grads_kernel, sizes=(x_count, z_count)), (sds((own...  4.52 us
    unnamed x9, local copies, waits for them, and re-layouts  4.09 us
  transfers between devices with their start and end apart: 15, of which 11 were waited for; matrix products, arithmetic and copies ran while one was open for 2% of the time, Pallas kernels for 5%

profile of v4, /device:TPU:32, one launch (start us, length us, event | category | flops | bytes accessed | tf_op | source)
XLA Modules:
  0.0 104.2 jit_solution(11151589928608649089)
XLA Ops:
  0.6 1.7 %collective-permute-start = (bf16[256,256]{1,0:T(8,128)(2,1)}, bf16[256,256]{1,0:T(8,128)(2,1)S(1)}, u32[]{:S(2)}, u32[]{:S(2)}) collective-permute-start(bf16[256,256]{1,0:T(8,128)(2,1)} %bitcast.23), channel_id=1, source_target_pairs={{0,1},{1,0},{2,3},{3,2},{4,5},{5,4},{6,7},{7,6},{8,9},{9,8},{10,11... | collective-permute-start | bytes 393224 | tf_op jit(solution)/shard_map/ppermute | solution.py:393
  2.3 3.9 %collective-permute-done = bf16[256,256]{1,0:T(8,128)(2,1)S(1)} collective-permute-done((bf16[256,256]{1,0:T(8,128)(2,1)}, bf16[256,256]{1,0:T(8,128)(2,1)S(1)}, u32[]{:S(2)}, u32[]{:S(2)}) %collective-permute-start) | collective-permute-done | bytes 131104 | tf_op jit(solution)/shard_map/ppermute | solution.py:393
  6.2 0.9 pad_maximum_fusion.near_ref
  7.1 3.1 %collective-permute-start.1 = (bf16[512,256]{1,0:T(8,128)(2,1)S(1)}, bf16[512,256]{1,0:T(8,128)(2,1)S(1)}, u32[]{:S(2)}, u32[]{:S(2)}) collective-permute-start(bf16[512,256]{1,0:T(8,128)(2,1)S(1)} %pad_maximum_fusion.near_ref), channel_id=1, source_target_pairs={{0,3},{1,2},{2,1},{3,0},{4,7},{5,6},{6,5},{7,4},{8,11},{9,10},{10,... | collective-permute-start | bytes 786440 | tf_op jit(solution)/shard_map/ppermute | solution.py:410
  10.2 1.4 %shard_map.85 = bf16[64,8,128]{2,1,0:T(8,128)(2,1)} custom-call(s32[8,64]{1,0:T(8,128)} %bitcast.19, s32[1,64]{1,0:T(1,128)} %pairs_hbm.3), custom_call_target="tpu_custom_call" | custom-call | flops 65536 | bytes 262144 | tf_op jit(solution)/shard_map/pallas_call | solution.py:394
  11.6 11.6 %all-to-all-start = ((bf16[64,8,128]{2,1,0:T(8,128)(2,1)}), bf16[64,8,128]{2,1,0:T(8,128)(2,1)S(1)}, u32[]{:S(2)}, u32[]{:S(2)}) async-start(bf16[64,8,128]{2,1,0:T(8,128)(2,1)} %shard_map.85), calls=%async_computation | async-start | bytes 262144 | tf_op jit(solution)/shard_map/all_to_all | solution.py:408
  23.3 0.1 pad_add_fusion.1.place_s
  23.3 1.2 %copy-done = bf16[2048,256]{1,0:T(8,128)(2,1)S(1)} copy-done((bf16[2048,256]{1,0:T(8,128)(2,1)S(1)}, bf16[2048,256]{1,0:T(8,128)(2,1)}, u32[]{:S(2)}) %copy-start) | copy-done | bytes 1048600
  24.6 0.7 copy-done.1
  25.2 0.7 copy-done.2
  25.9 0.7 copy-done.3
  26.6 1.4 %shard_map.84 = (s32[1,64]{1,0:T(1,128)S(1)}, s32[1,64]{1,0:T(1,128)S(1)}, s32[1,1024]{1,0:T(1,128)S(1)}, bf16[256,2048]{1,0:T(8,128)(2,1)S(1)}, f32[64,384]{1,0:T(8,128)S(1)}) custom-call(s32[4]{0:T(128)S(1)} %pad_add_fusion.1.place_s, s32[8,64]{1,0:T(8,128)S(1)} %bitcast.20, s32[1,64]{1,0:T(1,128)S(1)} %copy-done.3, s32[4,256]{1,0:T(4,128)S(1)} %bitcast.21, ...), custom_call_target="tpu_custom_call" | custom-call | flops 67108864 | bytes 2302976 | tf_op jit(solution)/shard_map/pallas_call | solution.py:411
  28.0 5.3 %all-to-all-done = bf16[64,8,128]{2,1,0:T(8,128)(2,1)S(1)} async-done(((bf16[64,8,128]{2,1,0:T(8,128)(2,1)}), bf16[64,8,128]{2,1,0:T(8,128)(2,1)S(1)}, u32[]{:S(2)}, u32[]{:S(2)}) %all-to-all-start) | async-done | bytes 131104 | tf_op jit(solution)/shard_map/all_to_all | solution.py:408
  33.3 4.0 %shard_map.86 = (bf16[1024,256]{1,0:T(8,128)(2,1)S(1)}, bf16[1024,256]{1,0:T(8,128)(2,1)S(1)}, f32[3,1024]{1,0:T(4,128)S(1)}, f32[8,1024]{1,0:T(8,128)S(1)}, f32...) custom-call(s32[1,64]{1,0:T(1,128)S(1)} %get-tuple-element.29.pair_s, s32[4]{0:T(128)S(1)} %pad_add_fusion.1.place_s, ...), custom_call_target="tpu_custom_call" | custom-call | flops 1610612736 | bytes 4292608 | tf_op jit(solution)/shard_map/pallas_call | solution.py:434
  37.3 0.2 collective-permute-start.2
  37.5 3.6 %collective-permute-done.2 = f32[3,1024]{1,0:T(4,128)S(1)} collective-permute-done((f32[3,1024]{1,0:T(4,128)S(1)}, f32[3,1024]{1,0:T(4,128)S(1)}, u32[]{:S(2)}, u32[]{:S(2)}) %collective-permute-start.2) | collective-permute-done | bytes 12320 | tf_op jit(solution)/shard_map/ppermute | solution.py:453
  41.2 0.3 collective-permute-start.3
  41.5 1.7 %shard_map.87 = (bf16[8,256,1024]{2,1,0:T(8,128)(2,1)S(1)}, f32[1024,1024]{1,0:T(8,128)S(1)}) custom-call(f32[8,1024]{1,0:T(8,128)S(1)} %get-tuple-element.38.codes_ref, bf16[1024,256]{1,0:T(8,128)(2,1)S(1)} %get-tuple-element.34.u_ref, bf16[1024,256]{1,0:T(8,128)(2,1)S(1)} %get-tuple-element.35.q_ref, f32[3,1024]{1,0:T(4,128)S(1)} %get-tuple-element.33.st_ref), custom_call_target="tpu_custom_call" | custom-call | flops 2097152 | bytes 16777216 | tf_op jit(solution)/shard_map/pallas_call | solution.py:454
  43.2 3.0 %collective-permute-done.3.stb_ref = f32[3,1024]{1,0:T(4,128)S(1)} collective-permute-done((f32[3,1024]{1,0:T(4,128)S(1)}, f32[3,1024]{1,0:T(4,128)S(1)}, u32[]{:S(2)}, u32[]{:S(2)}) %collective-permute-start.3) | collective-permute-done | bytes 12320 | tf_op jit(solution)/shard_map/ppermute | solution.py:463
  46.2 4.5 %shard_map.88 = (bf16[128,16,256]{2,1,0:T(8,128)(2,1)}, f32[1,256]{1,0:T(1,128)}, f32[256,256]{1,0:T(8,128)S(1)}, bf16[3,256,256]{2,1,0:T(8,128)(2,1)S(1)}, f32[...) custom-call(s32[1,64]{1,0:T(1,128)S(1)} %get-tuple-element.29.pair_s, s32[1,64]{1,0:T(1,128)S(1)} %get-tuple-element.30.slot_s, ...), custom_call_target="tpu_custom_call" | custom-call | flops 2147483648 | bytes 6555648 | tf_op jit(solution)/shard_map/pallas_call | solution.py:469
  50.7 0.7 collective-permute-start.4
  51.4 10.9 %collective-permute-done.4.recv_ref = bf16[16,64,256]{2,1,0:T(8,128)(2,1)S(1)} collective-permute-done((bf16[16,64,256]{2,1,0:T(8,128)(2,1)S(1)}, bf16[16,64,256]{2,1,0:T(8,128)(2,1)S(1)}, u32[]{:S(2)}, u32[]{:S(2)}) %collective-permute-start.4) | collective-permute-done | bytes 524320 | tf_op jit(solution)/shard_map/ppermute | solution.py:372
  62.4 0.7 shard_map.89
  63.1 0.1 collective-permute-start.5
  63.2 5.2 %all-to-all-start.1 = ((bf16[64,32,256]{2,1,0:T(8,128)(2,1)}), bf16[64,32,256]{2,1,0:T(8,128)(2,1)S(1)}, u32[]{:S(2)}, u32[]{:S(2)}) async-start(bf16[64,32,256]{2,1,0:T(8,128)(2,1)} %bitcast.12), calls=%async_computation.1 | async-start | bytes 2097152 | tf_op jit(solution)/shard_map/all_to_all | solution.py:495
  68.4 0.0 collective-permute-done.5.recv_ref
  68.4 0.7 shard_map.90
  69.1 0.1 collective-permute-start.6
  69.2 2.3 %collective-permute-start.7 = (bf16[384,256]{1,0:T(8,128)(2,1)S(1)}, bf16[384,256]{1,0:T(8,128)(2,1)S(1)}, u32[]{:S(2)}, u32[]{:S(2)}) collective-permute-start(bf16[384,256]{1,0:T(8,128)(2,1)S(1)} %get-tuple-element.49), channel_id=1, source_target_pairs={{0,2},{1,3},{2,0},{3,1},{4,6},{5,7},{6,4},{7,5},{8,10},{9,11},{10,... | collective-permute-start | bytes 589832 | tf_op jit(solution)/shard_map/ppermute | solution.py:368
  71.5 0.9 collective-permute-start.8
  72.4 0.1 slice_convert_fusion.2
  72.5 9.0 %collective-permute-done.6 = bf16[384,256]{1,0:T(8,128)(2,1)S(1)} collective-permute-done((bf16[384,256]{1,0:T(8,128)(2,1)S(1)}, bf16[384,256]{1,0:T(8,128)(2,1)S(1)}, u32[]{:S(2)}, u32[]{:S(2)}) %collective-permute-start.6) | collective-permute-done | bytes 196640 | tf_op jit(solution)/shard_map/ppermute | solution.py:368
  81.5 0.6 collective-permute-done.8
  82.2 1.6 %collective-permute-start.9 = (bf16[64,256]{1,0:T(8,128)(2,1)S(1)}, bf16[64,256]{1,0:T(8,128)(2,1)S(1)}, u32[]{:S(2)}, u32[]{:S(2)}) collective-permute-start(bf16[64,256]{1,0:T(8,128)(2,1)S(1)} %slice.174), channel_id=1, source_target_pairs={{0,64},{64,0},{128,192},{192,128},{1,65},{65,1},{129,193},{193,129... | collective-permute-start | bytes 98312 | tf_op jit(solution)/shard_map/ppermute | solution.py:372
  83.7 0.2 compare_reduce_fusion
  84.0 2.5 %collective-permute-done.9 = bf16[64,256]{1,0:T(8,128)(2,1)S(1)} collective-permute-done((bf16[64,256]{1,0:T(8,128)(2,1)S(1)}, bf16[64,256]{1,0:T(8,128)(2,1)S(1)}, u32[]{:S(2)}, u32[]{:S(2)}) %collective-permute-start.9) | collective-permute-done | bytes 32800 | tf_op jit(solution)/shard_map/ppermute | solution.py:372
  86.5 3.0 %collective-permute-start.10 = (bf16[32,256]{1,0:T(8,128)(2,1)S(1)}, bf16[32,256]{1,0:T(8,128)(2,1)S(1)}, u32[]{:S(2)}, u32[]{:S(2)}) collective-permute-start(bf16[32,256]{1,0:T(8,128)(2,1)S(1)} %slice.175), channel_id=1, source_target_pairs={{0,192},{64,128},{128,64},{192,0},{1,193},{65,129},{129,65},{193,1... | collective-permute-start | bytes 49160 | tf_op jit(solution)/shard_map/ppermute | solution.py:372
  89.5 2.0 %collective-permute-done.10 = bf16[32,256]{1,0:T(8,128)(2,1)S(1)} collective-permute-done((bf16[32,256]{1,0:T(8,128)(2,1)S(1)}, bf16[32,256]{1,0:T(8,128)(2,1)S(1)}, u32[]{:S(2)}, u32[]{:S(2)}) %collective-permute-start.10) | collective-permute-done | bytes 16416 | tf_op jit(solution)/shard_map/ppermute | solution.py:372
  91.6 1.4 %collective-permute-start.11 = (bf16[16,256]{1,0:T(8,128)(2,1)S(1)}, bf16[16,256]{1,0:T(8,128)(2,1)S(1)}, u32[]{:S(2)}, u32[]{:S(2)}) collective-permute-start(bf16[16,256]{1,0:T(8,128)(2,1)S(1)} %slice.176), channel_id=1, source_target_pairs={{0,56},{8,16},{16,8},{24,32},{32,24},{40,48},{48,40},{56,0},{1,57}... | collective-permute-start | bytes 24584 | tf_op jit(solution)/shard_map/ppermute | solution.py:372
  93.0 0.1 copy.13
  93.1 0.1 reshape.33.slot_j
  93.3 2.1 %collective-permute-done.11 = bf16[16,256]{1,0:T(8,128)(2,1)S(1)} collective-permute-done((bf16[16,256]{1,0:T(8,128)(2,1)S(1)}, bf16[16,256]{1,0:T(8,128)(2,1)S(1)}, u32[]{:S(2)}, u32[]{:S(2)}) %collective-permute-start.11) | collective-permute-done | bytes 8224 | tf_op jit(solution)/shard_map/ppermute | solution.py:372
  95.4 4.8 %collective-permute-start.12 = (bf16[8,256]{1,0:T(8,128)(2,1)S(1)}, bf16[8,256]{1,0:T(8,128)(2,1)S(1)}, u32[]{:S(2)}, u32[]{:S(2)}) collective-permute-start(bf16[8,256]{1,0:T(8,128)(2,1)S(1)} %slice.177), channel_id=1, source_target_pairs={{0,24},{8,48},{16,40},{24,0},{32,56},{40,16},{48,8},{56,32},{1,25}... | collective-permute-start | bytes 12296 | tf_op jit(solution)/shard_map/ppermute | solution.py:372
  100.1 0.1 add_bitcast_fusion
  100.2 0.8 copy.14
  101.0 1.0 %collective-permute-done.12 = bf16[8,256]{1,0:T(8,128)(2,1)S(1)} collective-permute-done((bf16[8,256]{1,0:T(8,128)(2,1)S(1)}, bf16[8,256]{1,0:T(8,128)(2,1)S(1)}, u32[]{:S(2)}, u32[]{:S(2)}) %collective-permute-start.12) | collective-permute-done | bytes 4128 | tf_op jit(solution)/shard_map/ppermute | solution.py:372
  102.1 0.6 slice_add_fusion.3
  102.7 1.5 %shard_map.91 = f32[64,256]{1,0:T(8,128)} custom-call(s32[128]{0:T(128)S(1)} %reshape.33.slot_j, bf16[128,16,256]{2,1,0:T(8,128)(2,1)S(1)} %bitcast.17, f32[64,384]{1,0:T(8,128)S(1)} %get-tuple-element.52.unit_ref), custom_call_target="tpu_custom_call" | custom-call | flops 524288 | bytes 131072 | tf_op jit(solution)/shard_map/pallas_call | solution.py:548
  (20 shorter events, 0.2 us)
Async XLA Ops:
  0.6 5.5 %collective-permute-start = (bf16[256,256]{1,0:T(8,128)(2,1)}, bf16[256,256]{1,0:T(8,128)(2,1)S(1)}, u32[]{:S(2)}, u32[]{:S(2)}) collective-permute-start(bf16[256,256]{1,0:T(8,128)(2,1)} %bitcast.23), channel_id=1, source_target_pairs={{0,1},{1,0},{2,3},{3,2},{4,5},{5,4},{6,7},{7,6},{8,9},{9,8},{10,11... | collective-permute-start | bytes 393224 | tf_op jit(solution)/shard_map/ppermute | solution.py:393
  7.1 26.2 %collective-permute-start.1 = (bf16[512,256]{1,0:T(8,128)(2,1)S(1)}, bf16[512,256]{1,0:T(8,128)(2,1)S(1)}, u32[]{:S(2)}, u32[]{:S(2)}) collective-permute-start(bf16[512,256]{1,0:T(8,128)(2,1)S(1)} %pad_maximum_fusion.near_ref), channel_id=1, source_target_pairs={{0,3},{1,2},{2,1},{3,0},{4,7},{5,6},{6,5},{7,4},{8,11},{9,10},{10,... | collective-permute-start | bytes 786440 | tf_op jit(solution)/shard_map/ppermute | solution.py:410
  11.6 21.6 %all-to-all-start = ((bf16[64,8,128]{2,1,0:T(8,128)(2,1)}), bf16[64,8,128]{2,1,0:T(8,128)(2,1)S(1)}, u32[]{:S(2)}, u32[]{:S(2)}) async-start(bf16[64,8,128]{2,1,0:T(8,128)(2,1)} %shard_map.85), calls=%async_computation | async-start | bytes 262144 | tf_op jit(solution)/shard_map/all_to_all | solution.py:408
  23.3 1.2 %copy-start = (bf16[2048,256]{1,0:T(8,128)(2,1)S(1)}, bf16[2048,256]{1,0:T(8,128)(2,1)}, u32[]{:S(2)}) copy-start(bf16[2048,256]{1,0:T(8,128)(2,1)} %books_hbm.1) | copy-start | bytes 3145732
  24.6 0.7 copy-start.1
  25.2 0.7 copy-start.2
  25.9 0.7 copy-start.3
  37.3 3.8 %collective-permute-start.2 = (f32[3,1024]{1,0:T(4,128)S(1)}, f32[3,1024]{1,0:T(4,128)S(1)}, u32[]{:S(2)}, u32[]{:S(2)}) collective-permute-start(f32[3,1024]{1,0:T(4,128)S(1)} %get-tuple-element.33.st_ref), channel_id=1, source_target_pairs={{0,1},{1,0},{2,3},{3,2},{4,5},{5,4},{6,7},{7,6},{8,9},{9,8},{10,11... | collective-permute-start | bytes 36872 | tf_op jit(solution)/shard_map/ppermute | solution.py:453
  41.2 5.0 %collective-permute-start.3 = (f32[3,1024]{1,0:T(4,128)S(1)}, f32[3,1024]{1,0:T(4,128)S(1)}, u32[]{:S(2)}, u32[]{:S(2)}) collective-permute-start(f32[3,1024]{1,0:T(4,128)S(1)} %pad_maximum_fusion.1.sta_ref), channel_id=1, source_target_pairs={{0,3},{1,2},{2,1},{3,0},{4,7},{5,6},{6,5},{7,4},{8,11},{9,10},{10,... | collective-permute-start | bytes 36872 | tf_op jit(solution)/shard_map/ppermute | solution.py:463
  50.7 11.6 %collective-permute-start.4 = (bf16[16,64,256]{2,1,0:T(8,128)(2,1)S(1)}, bf16[16,64,256]{2,1,0:T(8,128)(2,1)S(1)}, u32[]{:S(2)}, u32[]{:S(2)}) collective-permute-start(bf16[16,64,256]{2,1,0:T(8,128)(2,1)S(1)} %get-tuple-element.44), channel_id=1, source_target_pairs={{0,8},{8,0},{16,24},{24,16},{32,40},{40,32},{48,56},{56,48},{1,9},... | collective-permute-start | bytes 1572872 | tf_op jit(solution)/shard_map/ppermute | solution.py:372
  63.1 5.3 %collective-permute-start.5 = (bf16[16,32,256]{2,1,0:T(8,128)(2,1)S(1)}, bf16[16,32,256]{2,1,0:T(8,128)(2,1)S(1)}, u32[]{:S(2)}, u32[]{:S(2)}) collective-permute-start(bf16[16,32,256]{2,1,0:T(8,128)(2,1)S(1)} %get-tuple-element.46), channel_id=1, source_target_pairs={{0,4},{4,0},{1,5},{5,1},{2,6},{6,2},{3,7},{7,3},{8,12},{12,8},{9,1... | collective-permute-start | bytes 786440 | tf_op jit(solution)/shard_map/ppermute | solution.py:512
  63.2 39.5 %all-to-all-start.1 = ((bf16[64,32,256]{2,1,0:T(8,128)(2,1)}), bf16[64,32,256]{2,1,0:T(8,128)(2,1)S(1)}, u32[]{:S(2)}, u32[]{:S(2)}) async-start(bf16[64,32,256]{2,1,0:T(8,128)(2,1)} %bitcast.12), calls=%async_computation.1 | async-start | bytes 2097152 | tf_op jit(solution)/shard_map/all_to_all | solution.py:495
  69.1 12.4 %collective-permute-start.6 = (bf16[384,256]{1,0:T(8,128)(2,1)S(1)}, bf16[384,256]{1,0:T(8,128)(2,1)S(1)}, u32[]{:S(2)}, u32[]{:S(2)}) collective-permute-start(bf16[384,256]{1,0:T(8,128)(2,1)S(1)} %get-tuple-element.48), channel_id=1, source_target_pairs={{0,1},{1,2},{2,3},{3,0},{4,5},{5,6},{6,7},{7,4},{8,9},{9,10},{10,1... | collective-permute-start | bytes 589832 | tf_op jit(solution)/shard_map/ppermute | solution.py:368
  69.2 12.3 %collective-permute-start.7 = (bf16[384,256]{1,0:T(8,128)(2,1)S(1)}, bf16[384,256]{1,0:T(8,128)(2,1)S(1)}, u32[]{:S(2)}, u32[]{:S(2)}) collective-permute-start(bf16[384,256]{1,0:T(8,128)(2,1)S(1)} %get-tuple-element.49), channel_id=1, source_target_pairs={{0,2},{1,3},{2,0},{3,1},{4,6},{5,7},{6,4},{7,5},{8,10},{9,11},{10,... | collective-permute-start | bytes 589832 | tf_op jit(solution)/shard_map/ppermute | solution.py:368
  71.5 10.6 %collective-permute-start.8 = (bf16[384,256]{1,0:T(8,128)(2,1)S(1)}, bf16[384,256]{1,0:T(8,128)(2,1)S(1)}, u32[]{:S(2)}, u32[]{:S(2)}) collective-permute-start(bf16[384,256]{1,0:T(8,128)(2,1)S(1)} %get-tuple-element.50), channel_id=1, source_target_pairs={{0,3},{1,0},{2,1},{3,2},{4,7},{5,4},{6,5},{7,6},{8,11},{9,8},{10,9... | collective-permute-start | bytes 589832 | tf_op jit(solution)/shard_map/ppermute | solution.py:368
  82.2 4.3 %collective-permute-start.9 = (bf16[64,256]{1,0:T(8,128)(2,1)S(1)}, bf16[64,256]{1,0:T(8,128)(2,1)S(1)}, u32[]{:S(2)}, u32[]{:S(2)}) collective-permute-start(bf16[64,256]{1,0:T(8,128)(2,1)S(1)} %slice.174), channel_id=1, source_target_pairs={{0,64},{64,0},{128,192},{192,128},{1,65},{65,1},{129,193},{193,129... | collective-permute-start | bytes 98312 | tf_op jit(solution)/shard_map/ppermute | solution.py:372
  86.5 5.1 %collective-permute-start.10 = (bf16[32,256]{1,0:T(8,128)(2,1)S(1)}, bf16[32,256]{1,0:T(8,128)(2,1)S(1)}, u32[]{:S(2)}, u32[]{:S(2)}) collective-permute-start(bf16[32,256]{1,0:T(8,128)(2,1)S(1)} %slice.175), channel_id=1, source_target_pairs={{0,192},{64,128},{128,64},{192,0},{1,193},{65,129},{129,65},{193,1... | collective-permute-start | bytes 49160 | tf_op jit(solution)/shard_map/ppermute | solution.py:372
  91.6 3.8 %collective-permute-start.11 = (bf16[16,256]{1,0:T(8,128)(2,1)S(1)}, bf16[16,256]{1,0:T(8,128)(2,1)S(1)}, u32[]{:S(2)}, u32[]{:S(2)}) collective-permute-start(bf16[16,256]{1,0:T(8,128)(2,1)S(1)} %slice.176), channel_id=1, source_target_pairs={{0,56},{8,16},{16,8},{24,32},{32,24},{40,48},{48,40},{56,0},{1,57}... | collective-permute-start | bytes 24584 | tf_op jit(solution)/shard_map/ppermute | solution.py:372
  95.4 6.7 %collective-permute-start.12 = (bf16[8,256]{1,0:T(8,128)(2,1)S(1)}, bf16[8,256]{1,0:T(8,128)(2,1)S(1)}, u32[]{:S(2)}, u32[]{:S(2)}) collective-permute-start(bf16[8,256]{1,0:T(8,128)(2,1)S(1)} %slice.177), channel_id=1, source_target_pairs={{0,24},{8,48},{16,40},{24,0},{32,56},{40,16},{48,8},{56,32},{1,25}... | collective-permute-start | bytes 12296 | tf_op jit(solution)/shard_map/ppermute | solution.py:372

commit v5 on v4

--- a/solution.py
+++ b/solution.py
@@ -226,14 +226,14 @@
 def grads_kernel(
     pair_s, slot_s, place_s,
     st_ref, sta_ref, stb_ref, tkey_ref, u_ref, q_ref, unit_ref, inv_ref, hot_ref, exp_ref,
-    send_ref, loss_ref, own_ref, far_ref, stay_ref, give_ref,
+    send_ref, loss_ref, held_ref, lent_ref, stay_ref, give_ref,
     key_ref, lse_ref, qgt_ref, pg_ref, sum_ref, *, sizes,
 ):
     cols = u_ref.shape[0]
     pair_count = cols // PR
     x_here, z_here, rep = place_s[0], place_s[1], place_s[3]
     x_count, z_count = sizes
-    rows = own_ref.shape[1]
+    rows = held_ref.shape[2]
     peak, total, hit = merged(sta_ref[...], stb_ref[...])
     lse = peak + jnp.log(total)
     factor = jnp.exp(st_ref[0:1, :] - lse)
@@ -260,13 +260,10 @@
         grown = term if grown is None else grown + term
     qgt_ref[...] = grown
     count = q_ref.shape[0] // rows
-    for k in range(count):
-        owner = lax.rem(rep + k, count)
-        part = qgt_ref[:, pl.ds(pl.multiple_of(owner * rows, rows), rows)]
-        if k:
-            far_ref[k - 1] = part.astype(BF16)
-        else:
-            own_ref[...] = part
+    for out, first in ((held_ref, rep), (lent_ref, rep ^ 1)):
+        for k, owner in enumerate((first, count - 1 - first)):
+            part = qgt_ref[:, pl.ds(pl.multiple_of(owner * rows, rows), rows)]
+            out[k] = part.astype(out.dtype)
     for book in range(BOOKS):
         sum_ref[book * CODES : (book + 1) * CODES, :] = lax.dot_general(
             hot_ref[book], pg_ref[...], CONTRACT_LAST, preferred_element_type=F32
@@ -314,7 +311,11 @@
     return order
 
 
-def split_kernel(place_s, stay_ref, recv_ref, keep_ref, give_ref, sum_ref):
+def split_kernel(
+    place_s, stay_ref, recv_ref, held_ref, back_ref, keep_ref, give_ref, own_ref, far_ref, sum_ref
+):
+    own_ref[...] = held_ref[0] + back_ref[0].astype(F32)
+    far_ref[...] = (held_ref[1] + back_ref[1].astype(F32)).astype(BF16)
     core = place_s[2]
     half = keep_ref.shape[1]
     sum_ref[...] = stay_ref[...] + recv_ref[...].astype(F32)
@@ -325,7 +326,7 @@
         give_ref[chunk] = sum_ref[chunk, other, :].astype(BF16)
 
 
-def deal_kernel(place_s, stay_ref, recv_ref, qg_ref, own_ref, far1, far2, far3, sum_ref):
+def deal_kernel(place_s, stay_ref, recv_ref, own_ref, far1, far2, far3, sum_ref):
     rep = place_s[3]
     chunks = stay_ref.shape[0]
     share = own_ref.shape[0] // chunks
@@ -339,9 +340,10 @@
                 [sum_ref[2 * pair, at, :], sum_ref[2 * pair + 1, at, :]], axis=0
             )
             out[2 * pair * share : (2 * pair + 2) * share, :] = rows.astype(out.dtype)
-    dealt = own_ref.shape[0]
-    for k, out in enumerate((far1, far2, far3)):
-        out[dealt:, :] = qg_ref[k]
+
+
+def last_kernel(own_ref, far_ref, out_ref):
+    out_ref[...] = (own_ref[...] + far_ref[...].astype(F32)).T
 
 
 def return_kernel(slot_j, ret_ref, unit_ref, out_ref, *sums):
@@ -466,13 +468,13 @@
     chunk_rows = codebooks.shape[0] // chunks
     half_rows = chunk_rows // cores
     held_chunks = chunks // 2
-    outbound, loss, own_t, far, stay, give = call(
+    outbound, loss, held_t, lent_t, stay, give = call(
         functools.partial(grads_kernel, sizes=(x_count, z_count)),
         (
             sds((owners * CAP, PR, feat), BF16),
             sds((1, row_count), F32),
-            sds((feat, row_count), F32),
-            sds((reps - 1, feat, row_count), BF16),
+            sds((2, feat, row_count), F32),
+            sds((2, feat, row_count), BF16),
             sds((held_chunks, chunk_rows, feat), F32),
             sds((held_chunks, chunk_rows, feat), BF16),
         ),
@@ -498,33 +500,38 @@
     steps = [("z", partner) for partner in z_partners(z_count)]
     steps = steps[:1] + [("x", partner) for partner in x_partners(x_count)] + steps[1:]
     passed = stepped(give, *steps[0])
-    keep, hand = call(
+    lent_back = lax.ppermute(lent_t, "rep", near)
+    keep, hand, own_t, far_t = call(
         split_kernel,
         (
             sds((held_chunks, half_rows, feat), F32),
             sds((held_chunks, half_rows, feat), BF16),
+            sds((feat, row_count), F32),
+            sds((feat, row_count), BF16),
         ),
         [pltpu.VMEM((held_chunks, chunk_rows, feat), F32)],
         1,
-        2,
+        4,
         cols * feat,
-    )(place, stay, passed)
+    )(place, stay, passed, held_t, lent_back)
     other = lax.ppermute(hand, "c", [(0, 1), (1, 0)])
+    far_t = lax.ppermute(far_t, "rep", cross)
     share_rows = half_rows // reps
     dealt = held_chunks * share_rows
     mine, *parts = call(
         deal_kernel,
-        (sds((dealt, feat), F32), *[sds((dealt + feat, row_count), BF16)] * 3),
+        (sds((dealt, feat), F32), *[sds((dealt, feat), BF16)] * 3),
         [pltpu.VMEM((held_chunks, half_rows, feat), F32)],
         1,
-        3,
+        2,
         cols * feat,
-    )(place, keep, other, far)
+    )(place, keep, other)
     parts = [shifted(part, k + 1) for k, part in enumerate(parts)]
-    query_grad_t = own_t
     for part in parts:
-        mine = mine + part[:dealt].astype(F32)
-        query_grad_t = query_grad_t + part[dealt:].astype(F32)
+        mine = mine + part.astype(F32)
+    query_grad = call(
+        last_kernel, sds((row_count, feat), F32), [], 0, 2, row_count * feat
+    )(own_t, far_t)
     for axis, partner in steps[1:]:
         half = mine.shape[0] // 2
         more = stepped(mine[half:].astype(BF16), axis, partner)
@@ -555,7 +562,7 @@
     )(slot_j, returned, unit)
     return (
         loss[None],
-        query_grad_t.T[None, None],
+        query_grad[None, None],
         passage_grad[None, None],
         codebook_grad,
     )

time: 105 us -> 103 us (0.981); the launches traced: 104 us -> 101 us
  waiting for transfers between devices: 44 us -> 41 us
    ppermute x0 -> x2, waiting for transfers between devices: none -> 6.37 us  [the longest x1 6.37 us: shards(): lent_back = lax.ppermute(lent_t, 'rep', near)]
    ppermute x3, waiting for transfers between devices: 9.61 us -> 4.06 us  [shifted(): return lax.ppermute(x, 'rep', [(i, (i + k) % count) for i in range(count)])]
    ppermute x5, waiting for transfers between devices: 18.6 us -> 14.8 us  [stepped(): lax.ppermute(x, axis, [(i, partner(i)) for i in range(lax.axis_size(axis))])]
    ppermute x0 -> x2, starting transfers between devices: none -> 2.54 us  [the longest x1 2.54 us: shards(): far_t = lax.ppermute(far_t, 'rep', cross)]
    ppermute x5, starting transfers between devices: 11.5 us -> 9.05 us  [stepped(): lax.ppermute(x, axis, [(i, partner(i)) for i in range(lax.axis_size(axis))])]
    unnamed x9 -> x8, local copies, waits for them, and re-layouts: 4.09 us -> 3.25 us
  transfers between devices with their start and end apart: 15 -> 17, of which waited for: 11 -> 12; matrix products, arithmetic and copies ran while one was open for 2% -> 1% of each run, Pallas kernels for 5% -> 6%
where the time goes in v5:
time: 103 us; the launch traced here: 101 us
  waiting for transfers between devices  41 us (40%)
  starting transfers between devices  37.1 us (36%)
  Pallas kernels  16.8 us (16%)
  local copies, waits for them, and re-layouts  3.51 us (3%)
  other arithmetic  2.04 us (2%)
    ppermute x5, waiting for transfers between devices, stepped(): lax.ppermute(x, axis, [(i, partner(i)) for i in range(lax.axis_size(axis))])  14.8 us
    all_to_all x1, starting transfers between devices, shards(): arrived = lax.all_to_all(message, BLK, 0, 0, tiled=True)  11.6 us
    ppermute x5, starting transfers between devices, stepped(): lax.ppermute(x, axis, [(i, partner(i)) for i in range(lax.axis_size(axis))])  9.05 us
    ppermute x1, waiting for transfers between devices, shards(): lent_back = lax.ppermute(lent_t, 'rep', near)  6.37 us
    all_to_all x1, waiting for transfers between devices, shards(): arrived = lax.all_to_all(message, BLK, 0, 0, tiled=True)  5.3 us
    all_to_all x1, starting transfers between devices, shards(): returned = lax.all_to_all(outbound, BLK, 0, 0, tiled=True)  5.17 us
    pallas_call x1, Pallas kernels, shards(): call(functools.partial(grads_kernel, sizes=(x_count, z_count)), (sds((own...  4.4 us
    ppermute x3, waiting for transfers between devices, shifted(): return lax.ppermute(x, 'rep', [(i, (i + k) % count) for i in range(count)])  4.06 us
  transfers between devices with their start and end apart: 17, of which 12 were waited for; matrix products, arithmetic and copies ran while one was open for 1% of the time, Pallas kernels for 6%

profile of v5, /device:TPU:32, one launch (start us, length us, event | category | flops | bytes accessed | tf_op | source)
XLA Modules:
  0.0 101.1 jit_solution(2836836200968154526)
XLA Ops:
  0.6 1.7 %collective-permute-start = (bf16[256,256]{1,0:T(8,128)(2,1)}, bf16[256,256]{1,0:T(8,128)(2,1)S(1)}, u32[]{:S(2)}, u32[]{:S(2)}) collective-permute-start(bf16[256,256]{1,0:T(8,128)(2,1)} %bitcast.21), channel_id=1, source_target_pairs={{0,1},{1,0},{2,3},{3,2},{4,5},{5,4},{6,7},{7,6},{8,9},{9,8},{10,11... | collective-permute-start | bytes 393224 | tf_op jit(solution)/shard_map/ppermute | solution.py:395
  2.3 3.9 %collective-permute-done = bf16[256,256]{1,0:T(8,128)(2,1)S(1)} collective-permute-done((bf16[256,256]{1,0:T(8,128)(2,1)}, bf16[256,256]{1,0:T(8,128)(2,1)S(1)}, u32[]{:S(2)}, u32[]{:S(2)}) %collective-permute-start) | collective-permute-done | bytes 131104 | tf_op jit(solution)/shard_map/ppermute | solution.py:395
  6.2 0.9 pad_maximum_fusion.near_ref
  7.1 3.1 %collective-permute-start.1 = (bf16[512,256]{1,0:T(8,128)(2,1)S(1)}, bf16[512,256]{1,0:T(8,128)(2,1)S(1)}, u32[]{:S(2)}, u32[]{:S(2)}) collective-permute-start(bf16[512,256]{1,0:T(8,128)(2,1)S(1)} %pad_maximum_fusion.near_ref), channel_id=1, source_target_pairs={{0,3},{1,2},{2,1},{3,0},{4,7},{5,6},{6,5},{7,4},{8,11},{9,10},{10,... | collective-permute-start | bytes 786440 | tf_op jit(solution)/shard_map/ppermute | solution.py:412
  10.2 1.4 %shard_map.85 = bf16[64,8,128]{2,1,0:T(8,128)(2,1)} custom-call(s32[8,64]{1,0:T(8,128)} %bitcast.16, s32[1,64]{1,0:T(1,128)} %pairs_hbm.3), custom_call_target="tpu_custom_call" | custom-call | flops 65536 | bytes 262144 | tf_op jit(solution)/shard_map/pallas_call | solution.py:396
  11.6 11.6 %all-to-all-start = ((bf16[64,8,128]{2,1,0:T(8,128)(2,1)}), bf16[64,8,128]{2,1,0:T(8,128)(2,1)S(1)}, u32[]{:S(2)}, u32[]{:S(2)}) async-start(bf16[64,8,128]{2,1,0:T(8,128)(2,1)} %shard_map.85), calls=%async_computation | async-start | bytes 262144 | tf_op jit(solution)/shard_map/all_to_all | solution.py:410
  23.3 0.1 pad_add_fusion.1.place_s
  23.3 1.2 %copy-done = bf16[2048,256]{1,0:T(8,128)(2,1)S(1)} copy-done((bf16[2048,256]{1,0:T(8,128)(2,1)S(1)}, bf16[2048,256]{1,0:T(8,128)(2,1)}, u32[]{:S(2)}) %copy-start) | copy-done | bytes 1048600
  24.6 0.7 copy-done.1
  25.2 0.7 copy-done.2
  25.9 0.7 copy-done.3
  26.6 1.4 %shard_map.84 = (s32[1,64]{1,0:T(1,128)S(1)}, s32[1,64]{1,0:T(1,128)S(1)}, s32[1,1024]{1,0:T(1,128)S(1)}, bf16[256,2048]{1,0:T(8,128)(2,1)S(1)}, f32[64,384]{1,0:T(8,128)S(1)}) custom-call(s32[4]{0:T(128)S(1)} %pad_add_fusion.1.place_s, s32[8,64]{1,0:T(8,128)S(1)} %bitcast.17, s32[1,64]{1,0:T(1,128)S(1)} %copy-done.3, s32[4,256]{1,0:T(4,128)S(1)} %bitcast.18, ...), custom_call_target="tpu_custom_call" | custom-call | flops 67108864 | bytes 2302976 | tf_op jit(solution)/shard_map/pallas_call | solution.py:413
  28.0 5.3 %all-to-all-done = bf16[64,8,128]{2,1,0:T(8,128)(2,1)S(1)} async-done(((bf16[64,8,128]{2,1,0:T(8,128)(2,1)}), bf16[64,8,128]{2,1,0:T(8,128)(2,1)S(1)}, u32[]{:S(2)}, u32[]{:S(2)}) %all-to-all-start) | async-done | bytes 131104 | tf_op jit(solution)/shard_map/all_to_all | solution.py:410
  33.3 4.0 %shard_map.86 = (bf16[1024,256]{1,0:T(8,128)(2,1)S(1)}, bf16[1024,256]{1,0:T(8,128)(2,1)S(1)}, f32[3,1024]{1,0:T(4,128)S(1)}, f32[8,1024]{1,0:T(8,128)S(1)}, f32...) custom-call(s32[1,64]{1,0:T(1,128)S(1)} %get-tuple-element.31.pair_s, s32[4]{0:T(128)S(1)} %pad_add_fusion.1.place_s, ...), custom_call_target="tpu_custom_call" | custom-call | flops 1610612736 | bytes 4292608 | tf_op jit(solution)/shard_map/pallas_call | solution.py:436
  37.3 0.2 collective-permute-start.2
  37.5 3.6 %collective-permute-done.2 = f32[3,1024]{1,0:T(4,128)S(1)} collective-permute-done((f32[3,1024]{1,0:T(4,128)S(1)}, f32[3,1024]{1,0:T(4,128)S(1)}, u32[]{:S(2)}, u32[]{:S(2)}) %collective-permute-start.2) | collective-permute-done | bytes 12320 | tf_op jit(solution)/shard_map/ppermute | solution.py:455
  41.2 0.3 collective-permute-start.3
  41.5 1.7 %shard_map.87 = (bf16[8,256,1024]{2,1,0:T(8,128)(2,1)S(1)}, f32[1024,1024]{1,0:T(8,128)S(1)}) custom-call(f32[8,1024]{1,0:T(8,128)S(1)} %get-tuple-element.40.codes_ref, bf16[1024,256]{1,0:T(8,128)(2,1)S(1)} %get-tuple-element.36.u_ref, bf16[1024,256]{1,0:T(8,128)(2,1)S(1)} %get-tuple-element.37.q_ref, f32[3,1024]{1,0:T(4,128)S(1)} %get-tuple-element.35.st_ref), custom_call_target="tpu_custom_call" | custom-call | flops 2097152 | bytes 16777216 | tf_op jit(solution)/shard_map/pallas_call | solution.py:456
  43.2 3.0 %collective-permute-done.3.stb_ref = f32[3,1024]{1,0:T(4,128)S(1)} collective-permute-done((f32[3,1024]{1,0:T(4,128)S(1)}, f32[3,1024]{1,0:T(4,128)S(1)}, u32[]{:S(2)}, u32[]{:S(2)}) %collective-permute-start.3) | collective-permute-done | bytes 12320 | tf_op jit(solution)/shard_map/ppermute | solution.py:465
  46.2 4.4 %shard_map.88 = (bf16[128,16,256]{2,1,0:T(8,128)(2,1)}, f32[1,256]{1,0:T(1,128)}, f32[2,256,256]{2,1,0:T(8,128)S(1)}, bf16[2,256,256]{2,1,0:T(8,128)(2,1)S(1)}, ...) custom-call(s32[1,64]{1,0:T(1,128)S(1)} %get-tuple-element.31.pair_s, s32[1,64]{1,0:T(1,128)S(1)} %get-tuple-element.32.slot_s, ...), custom_call_target="tpu_custom_call" | custom-call | flops 2147483648 | bytes 6817792 | tf_op jit(solution)/shard_map/pallas_call | solution.py:471
  50.6 0.7 collective-permute-start.4
  51.3 6.4 %collective-permute-done.5.back_ref = bf16[2,256,256]{2,1,0:T(8,128)(2,1)S(1)} collective-permute-done((bf16[2,256,256]{2,1,0:T(8,128)(2,1)S(1)}, bf16[2,256,256]{2,1,0:T(8,128)(2,1)S(1)}, u32[]{:S(2)}, u32[]{:S(2)}) %collective-permute-start.5) | collective-permute-done | bytes 262176 | tf_op jit(solution)/shard_map/ppermute | solution.py:503
  57.7 4.6 %collective-permute-done.4.recv_ref = bf16[16,64,256]{2,1,0:T(8,128)(2,1)S(1)} collective-permute-done((bf16[16,64,256]{2,1,0:T(8,128)(2,1)S(1)}, bf16[16,64,256]{2,1,0:T(8,128)(2,1)S(1)}, u32[]{:S(2)}, u32[]{:S(2)}) %collective-permute-start.4) | collective-permute-done | bytes 524320 | tf_op jit(solution)/shard_map/ppermute | solution.py:374
  62.2 0.8 shard_map.89
  63.0 0.1 collective-permute-start.7
  63.1 5.2 %all-to-all-start.1 = ((bf16[64,32,256]{2,1,0:T(8,128)(2,1)}), bf16[64,32,256]{2,1,0:T(8,128)(2,1)S(1)}, u32[]{:S(2)}, u32[]{:S(2)}) async-start(bf16[64,32,256]{2,1,0:T(8,128)(2,1)} %bitcast.11), calls=%async_computation.1 | async-start | bytes 2097152 | tf_op jit(solution)/shard_map/all_to_all | solution.py:497
  68.3 0.7 shard_map.92
  69.0 0.1 collective-permute-start.8
  69.1 2.3 %collective-permute-start.9 = (bf16[128,256]{1,0:T(8,128)(2,1)S(1)}, bf16[128,256]{1,0:T(8,128)(2,1)S(1)}, u32[]{:S(2)}, u32[]{:S(2)}) collective-permute-start(bf16[128,256]{1,0:T(8,128)(2,1)S(1)} %get-tuple-element.56), channel_id=1, source_target_pairs={{0,2},{1,3},{2,0},{3,1},{4,6},{5,7},{6,4},{7,5},{8,10},{9,11},{10,... | collective-permute-start | bytes 196616 | tf_op jit(solution)/shard_map/ppermute | solution.py:370
  71.4 0.9 collective-permute-start.10
  72.3 3.5 %collective-permute-done.8 = bf16[128,256]{1,0:T(8,128)(2,1)S(1)} collective-permute-done((bf16[128,256]{1,0:T(8,128)(2,1)S(1)}, bf16[128,256]{1,0:T(8,128)(2,1)S(1)}, u32[]{:S(2)}, u32[]{:S(2)}) %collective-permute-start.8) | collective-permute-done | bytes 65568 | tf_op jit(solution)/shard_map/ppermute | solution.py:370
  75.8 0.6 collective-permute-done.10
  76.4 1.6 %collective-permute-start.11 = (bf16[64,256]{1,0:T(8,128)(2,1)S(1)}, bf16[64,256]{1,0:T(8,128)(2,1)S(1)}, u32[]{:S(2)}, u32[]{:S(2)}) collective-permute-start(bf16[64,256]{1,0:T(8,128)(2,1)S(1)} %slice.138), channel_id=1, source_target_pairs={{0,64},{64,0},{128,192},{192,128},{1,65},{65,1},{129,193},{193,129... | collective-permute-start | bytes 98312 | tf_op jit(solution)/shard_map/ppermute | solution.py:374
  78.0 0.1 slice_convert_fusion.2
  78.1 3.0 %collective-permute-done.11 = bf16[64,256]{1,0:T(8,128)(2,1)S(1)} collective-permute-done((bf16[64,256]{1,0:T(8,128)(2,1)S(1)}, bf16[64,256]{1,0:T(8,128)(2,1)S(1)}, u32[]{:S(2)}, u32[]{:S(2)}) %collective-permute-start.11) | collective-permute-done | bytes 32800 | tf_op jit(solution)/shard_map/ppermute | solution.py:374
  81.2 2.8 %collective-permute-start.12 = (bf16[32,256]{1,0:T(8,128)(2,1)S(1)}, bf16[32,256]{1,0:T(8,128)(2,1)S(1)}, u32[]{:S(2)}, u32[]{:S(2)}) collective-permute-start(bf16[32,256]{1,0:T(8,128)(2,1)S(1)} %slice.139), channel_id=1, source_target_pairs={{0,192},{64,128},{128,64},{192,0},{1,193},{65,129},{129,65},{193,1... | collective-permute-start | bytes 49160 | tf_op jit(solution)/shard_map/ppermute | solution.py:374
  84.0 0.2 compare_reduce_fusion
  84.2 2.1 %collective-permute-done.12 = bf16[32,256]{1,0:T(8,128)(2,1)S(1)} collective-permute-done((bf16[32,256]{1,0:T(8,128)(2,1)S(1)}, bf16[32,256]{1,0:T(8,128)(2,1)S(1)}, u32[]{:S(2)}, u32[]{:S(2)}) %collective-permute-start.12) | collective-permute-done | bytes 16416 | tf_op jit(solution)/shard_map/ppermute | solution.py:374
  86.3 1.3 %collective-permute-start.13 = (bf16[16,256]{1,0:T(8,128)(2,1)S(1)}, bf16[16,256]{1,0:T(8,128)(2,1)S(1)}, u32[]{:S(2)}, u32[]{:S(2)}) collective-permute-start(bf16[16,256]{1,0:T(8,128)(2,1)S(1)} %slice.140), channel_id=1, source_target_pairs={{0,56},{8,16},{16,8},{24,32},{32,24},{40,48},{48,40},{56,0},{1,57}... | collective-permute-start | bytes 24584 | tf_op jit(solution)/shard_map/ppermute | solution.py:374
  87.5 2.5 %collective-permute-start.6 = (bf16[256,256]{1,0:T(8,128)(2,1)S(1)}, bf16[256,256]{1,0:T(8,128)(2,1)S(1)}, u32[]{:S(2)}, u32[]{:S(2)}) collective-permute-start(bf16[256,256]{1,0:T(8,128)(2,1)S(1)} %get-tuple-element.49), channel_id=1, source_target_pairs={{0,3},{1,2},{2,1},{3,0},{4,7},{5,6},{6,5},{7,4},{8,11},{9,10},{10,... | collective-permute-start | bytes 393224 | tf_op jit(solution)/shard_map/ppermute | solution.py:518
  90.1 2.2 %collective-permute-done.13 = bf16[16,256]{1,0:T(8,128)(2,1)S(1)} collective-permute-done((bf16[16,256]{1,0:T(8,128)(2,1)S(1)}, bf16[16,256]{1,0:T(8,128)(2,1)S(1)}, u32[]{:S(2)}, u32[]{:S(2)}) %collective-permute-start.13) | collective-permute-done | bytes 8224 | tf_op jit(solution)/shard_map/ppermute | solution.py:374
  92.3 2.8 %collective-permute-start.14 = (bf16[8,256]{1,0:T(8,128)(2,1)S(1)}, bf16[8,256]{1,0:T(8,128)(2,1)S(1)}, u32[]{:S(2)}, u32[]{:S(2)}) collective-permute-start(bf16[8,256]{1,0:T(8,128)(2,1)S(1)} %slice.141), channel_id=1, source_target_pairs={{0,24},{8,48},{16,40},{24,0},{32,56},{40,16},{48,8},{56,32},{1,25}... | collective-permute-start | bytes 12296 | tf_op jit(solution)/shard_map/ppermute | solution.py:374
  95.1 0.1 copy.10
  95.2 0.1 reshape.33.slot_j
  95.3 0.8 shard_map.90
  96.2 2.8 %collective-permute-done.14 = bf16[8,256]{1,0:T(8,128)(2,1)S(1)} collective-permute-done((bf16[8,256]{1,0:T(8,128)(2,1)S(1)}, bf16[8,256]{1,0:T(8,128)(2,1)S(1)}, u32[]{:S(2)}, u32[]{:S(2)}) %collective-permute-start.14) | collective-permute-done | bytes 4128 | tf_op jit(solution)/shard_map/ppermute | solution.py:374
  99.0 0.6 slice_add_fusion.3
  99.6 1.5 %shard_map.91 = f32[64,256]{1,0:T(8,128)} custom-call(s32[128]{0:T(128)S(1)} %reshape.33.slot_j, bf16[128,16,256]{2,1,0:T(8,128)(2,1)S(1)} %bitcast.14, f32[64,384]{1,0:T(8,128)S(1)} %get-tuple-element.51.unit_ref), custom_call_target="tpu_custom_call" | custom-call | flops 524288 | bytes 131072 | tf_op jit(solution)/shard_map/pallas_call | solution.py:555
  (23 shorter events, 0.2 us)
Async XLA Ops:
  0.6 5.5 %collective-permute-start = (bf16[256,256]{1,0:T(8,128)(2,1)}, bf16[256,256]{1,0:T(8,128)(2,1)S(1)}, u32[]{:S(2)}, u32[]{:S(2)}) collective-permute-start(bf16[256,256]{1,0:T(8,128)(2,1)} %bitcast.21), channel_id=1, source_target_pairs={{0,1},{1,0},{2,3},{3,2},{4,5},{5,4},{6,7},{7,6},{8,9},{9,8},{10,11... | collective-permute-start | bytes 393224 | tf_op jit(solution)/shard_map/ppermute | solution.py:395
  7.1 26.2 %collective-permute-start.1 = (bf16[512,256]{1,0:T(8,128)(2,1)S(1)}, bf16[512,256]{1,0:T(8,128)(2,1)S(1)}, u32[]{:S(2)}, u32[]{:S(2)}) collective-permute-start(bf16[512,256]{1,0:T(8,128)(2,1)S(1)} %pad_maximum_fusion.near_ref), channel_id=1, source_target_pairs={{0,3},{1,2},{2,1},{3,0},{4,7},{5,6},{6,5},{7,4},{8,11},{9,10},{10,... | collective-permute-start | bytes 786440 | tf_op jit(solution)/shard_map/ppermute | solution.py:412
  11.6 21.6 %all-to-all-start = ((bf16[64,8,128]{2,1,0:T(8,128)(2,1)}), bf16[64,8,128]{2,1,0:T(8,128)(2,1)S(1)}, u32[]{:S(2)}, u32[]{:S(2)}) async-start(bf16[64,8,128]{2,1,0:T(8,128)(2,1)} %shard_map.85), calls=%async_computation | async-start | bytes 262144 | tf_op jit(solution)/shard_map/all_to_all | solution.py:410
  23.3 1.2 %copy-start = (bf16[2048,256]{1,0:T(8,128)(2,1)S(1)}, bf16[2048,256]{1,0:T(8,128)(2,1)}, u32[]{:S(2)}) copy-start(bf16[2048,256]{1,0:T(8,128)(2,1)} %books_hbm.1) | copy-start | bytes 3145732
  24.6 0.7 copy-start.1
  25.2 0.7 copy-start.2
  25.9 0.7 copy-start.3
  37.3 3.8 %collective-permute-start.2 = (f32[3,1024]{1,0:T(4,128)S(1)}, f32[3,1024]{1,0:T(4,128)S(1)}, u32[]{:S(2)}, u32[]{:S(2)}) collective-permute-start(f32[3,1024]{1,0:T(4,128)S(1)} %get-tuple-element.35.st_ref), channel_id=1, source_target_pairs={{0,1},{1,0},{2,3},{3,2},{4,5},{5,4},{6,7},{7,6},{8,9},{9,8},{10,11... | collective-permute-start | bytes 36872 | tf_op jit(solution)/shard_map/ppermute | solution.py:455
  41.2 5.0 %collective-permute-start.3 = (f32[3,1024]{1,0:T(4,128)S(1)}, f32[3,1024]{1,0:T(4,128)S(1)}, u32[]{:S(2)}, u32[]{:S(2)}) collective-permute-start(f32[3,1024]{1,0:T(4,128)S(1)} %pad_maximum_fusion.1.sta_ref), channel_id=1, source_target_pairs={{0,3},{1,2},{2,1},{3,0},{4,7},{5,6},{6,5},{7,4},{8,11},{9,10},{10,... | collective-permute-start | bytes 36872 | tf_op jit(solution)/shard_map/ppermute | solution.py:465
  50.6 11.6 %collective-permute-start.4 = (bf16[16,64,256]{2,1,0:T(8,128)(2,1)S(1)}, bf16[16,64,256]{2,1,0:T(8,128)(2,1)S(1)}, u32[]{:S(2)}, u32[]{:S(2)}) collective-permute-start(bf16[16,64,256]{2,1,0:T(8,128)(2,1)S(1)} %get-tuple-element.45), channel_id=1, source_target_pairs={{0,8},{8,0},{16,24},{24,16},{32,40},{40,32},{48,56},{56,48},{1,9},... | collective-permute-start | bytes 1572872 | tf_op jit(solution)/shard_map/ppermute | solution.py:374
  51.3 6.4 %collective-permute-start.5 = (bf16[2,256,256]{2,1,0:T(8,128)(2,1)S(1)}, bf16[2,256,256]{2,1,0:T(8,128)(2,1)S(1)}, u32[]{:S(2)}, u32[]{:S(2)}) collective-permute-start(bf16[2,256,256]{2,1,0:T(8,128)(2,1)S(1)} %get-tuple-element.47), channel_id=1, source_target_pairs={{0,1},{1,0},{2,3},{3,2},{4,5},{5,4},{6,7},{7,6},{8,9},{9,8},{10,11... | collective-permute-start | bytes 786440 | tf_op jit(solution)/shard_map/ppermute | solution.py:503
  63.0 5.3 %collective-permute-start.7 = (bf16[16,32,256]{2,1,0:T(8,128)(2,1)S(1)}, bf16[16,32,256]{2,1,0:T(8,128)(2,1)S(1)}, u32[]{:S(2)}, u32[]{:S(2)}) collective-permute-start(bf16[16,32,256]{2,1,0:T(8,128)(2,1)S(1)} %get-tuple-element.53), channel_id=1, source_target_pairs={{0,4},{4,0},{1,5},{5,1},{2,6},{6,2},{3,7},{7,3},{8,12},{12,8},{9,1... | collective-permute-start | bytes 786440 | tf_op jit(solution)/shard_map/ppermute | solution.py:517
  63.1 36.5 %all-to-all-start.1 = ((bf16[64,32,256]{2,1,0:T(8,128)(2,1)}), bf16[64,32,256]{2,1,0:T(8,128)(2,1)S(1)}, u32[]{:S(2)}, u32[]{:S(2)}) async-start(bf16[64,32,256]{2,1,0:T(8,128)(2,1)} %bitcast.11), calls=%async_computation.1 | async-start | bytes 2097152 | tf_op jit(solution)/shard_map/all_to_all | solution.py:497
  69.0 6.8 %collective-permute-start.8 = (bf16[128,256]{1,0:T(8,128)(2,1)S(1)}, bf16[128,256]{1,0:T(8,128)(2,1)S(1)}, u32[]{:S(2)}, u32[]{:S(2)}) collective-permute-start(bf16[128,256]{1,0:T(8,128)(2,1)S(1)} %get-tuple-element.55), channel_id=1, source_target_pairs={{0,1},{1,2},{2,3},{3,0},{4,5},{5,6},{6,7},{7,4},{8,9},{9,10},{10,1... | collective-permute-start | bytes 196616 | tf_op jit(solution)/shard_map/ppermute | solution.py:370
  69.1 6.7 %collective-permute-start.9 = (bf16[128,256]{1,0:T(8,128)(2,1)S(1)}, bf16[128,256]{1,0:T(8,128)(2,1)S(1)}, u32[]{:S(2)}, u32[]{:S(2)}) collective-permute-start(bf16[128,256]{1,0:T(8,128)(2,1)S(1)} %get-tuple-element.56), channel_id=1, source_target_pairs={{0,2},{1,3},{2,0},{3,1},{4,6},{5,7},{6,4},{7,5},{8,10},{9,11},{10,... | collective-permute-start | bytes 196616 | tf_op jit(solution)/shard_map/ppermute | solution.py:370
  71.4 4.9 %collective-permute-start.10 = (bf16[128,256]{1,0:T(8,128)(2,1)S(1)}, bf16[128,256]{1,0:T(8,128)(2,1)S(1)}, u32[]{:S(2)}, u32[]{:S(2)}) collective-permute-start(bf16[128,256]{1,0:T(8,128)(2,1)S(1)} %get-tuple-element.57), channel_id=1, source_target_pairs={{0,3},{1,0},{2,1},{3,2},{4,7},{5,4},{6,5},{7,6},{8,11},{9,8},{10,9... | collective-permute-start | bytes 196616 | tf_op jit(solution)/shard_map/ppermute | solution.py:370
  76.4 4.7 %collective-permute-start.11 = (bf16[64,256]{1,0:T(8,128)(2,1)S(1)}, bf16[64,256]{1,0:T(8,128)(2,1)S(1)}, u32[]{:S(2)}, u32[]{:S(2)}) collective-permute-start(bf16[64,256]{1,0:T(8,128)(2,1)S(1)} %slice.138), channel_id=1, source_target_pairs={{0,64},{64,0},{128,192},{192,128},{1,65},{65,1},{129,193},{193,129... | collective-permute-start | bytes 98312 | tf_op jit(solution)/shard_map/ppermute | solution.py:374
  81.2 5.1 %collective-permute-start.12 = (bf16[32,256]{1,0:T(8,128)(2,1)S(1)}, bf16[32,256]{1,0:T(8,128)(2,1)S(1)}, u32[]{:S(2)}, u32[]{:S(2)}) collective-permute-start(bf16[32,256]{1,0:T(8,128)(2,1)S(1)} %slice.139), channel_id=1, source_target_pairs={{0,192},{64,128},{128,64},{192,0},{1,193},{65,129},{129,65},{193,1... | collective-permute-start | bytes 49160 | tf_op jit(solution)/shard_map/ppermute | solution.py:374
  86.3 6.0 %collective-permute-start.13 = (bf16[16,256]{1,0:T(8,128)(2,1)S(1)}, bf16[16,256]{1,0:T(8,128)(2,1)S(1)}, u32[]{:S(2)}, u32[]{:S(2)}) collective-permute-start(bf16[16,256]{1,0:T(8,128)(2,1)S(1)} %slice.140), channel_id=1, source_target_pairs={{0,56},{8,16},{16,8},{24,32},{32,24},{40,48},{48,40},{56,0},{1,57}... | collective-permute-start | bytes 24584 | tf_op jit(solution)/shard_map/ppermute | solution.py:374
  87.5 7.8 %collective-permute-start.6 = (bf16[256,256]{1,0:T(8,128)(2,1)S(1)}, bf16[256,256]{1,0:T(8,128)(2,1)S(1)}, u32[]{:S(2)}, u32[]{:S(2)}) collective-permute-start(bf16[256,256]{1,0:T(8,128)(2,1)S(1)} %get-tuple-element.49), channel_id=1, source_target_pairs={{0,3},{1,2},{2,1},{3,0},{4,7},{5,6},{6,5},{7,4},{8,11},{9,10},{10,... | collective-permute-start | bytes 393224 | tf_op jit(solution)/shard_map/ppermute | solution.py:518
  92.3 6.7 %collective-permute-start.14 = (bf16[8,256]{1,0:T(8,128)(2,1)S(1)}, bf16[8,256]{1,0:T(8,128)(2,1)S(1)}, u32[]{:S(2)}, u32[]{:S(2)}) collective-permute-start(bf16[8,256]{1,0:T(8,128)(2,1)S(1)} %slice.141), channel_id=1, source_target_pairs={{0,24},{8,48},{16,40},{24,0},{32,56},{40,16},{48,8},{56,32},{1,25}... | collective-permute-start | bytes 12296 | tf_op jit(solution)/shard_map/ppermute | solution.py:374

commit v6 on v5

--- a/solution.py
+++ b/solution.py
@@ -311,11 +311,7 @@
     return order
 
 
-def split_kernel(
-    place_s, stay_ref, recv_ref, held_ref, back_ref, keep_ref, give_ref, own_ref, far_ref, sum_ref
-):
-    own_ref[...] = held_ref[0] + back_ref[0].astype(F32)
-    far_ref[...] = (held_ref[1] + back_ref[1].astype(F32)).astype(BF16)
+def split_kernel(place_s, stay_ref, recv_ref, keep_ref, give_ref, sum_ref):
     core = place_s[2]
     half = keep_ref.shape[1]
     sum_ref[...] = stay_ref[...] + recv_ref[...].astype(F32)
@@ -326,7 +322,12 @@
         give_ref[chunk] = sum_ref[chunk, other, :].astype(BF16)
 
 
-def deal_kernel(place_s, stay_ref, recv_ref, own_ref, far1, far2, far3, sum_ref):
+def deal_kernel(
+    place_s, stay_ref, recv_ref, held_ref, back_ref,
+    own_ref, far1, far2, far3, half_ref, over_ref, sum_ref,
+):
+    half_ref[...] = held_ref[0] + back_ref[0].astype(F32)
+    over_ref[...] = (held_ref[1] + back_ref[1].astype(F32)).astype(BF16)
     rep = place_s[3]
     chunks = stay_ref.shape[0]
     share = own_ref.shape[0] // chunks
@@ -501,31 +502,34 @@
     steps = steps[:1] + [("x", partner) for partner in x_partners(x_count)] + steps[1:]
     passed = stepped(give, *steps[0])
     lent_back = lax.ppermute(lent_t, "rep", near)
-    keep, hand, own_t, far_t = call(
+    keep, hand = call(
         split_kernel,
         (
             sds((held_chunks, half_rows, feat), F32),
             sds((held_chunks, half_rows, feat), BF16),
+        ),
+        [pltpu.VMEM((held_chunks, chunk_rows, feat), F32)],
+        1,
+        2,
+        cols * feat,
+    )(place, stay, passed)
+    other = lax.ppermute(hand, "c", [(0, 1), (1, 0)])
+    share_rows = half_rows // reps
+    dealt = held_chunks * share_rows
+    mine, *parts, own_t, far_t = call(
+        deal_kernel,
+        (
+            sds((dealt, feat), F32),
+            *[sds((dealt, feat), BF16)] * 3,
             sds((feat, row_count), F32),
             sds((feat, row_count), BF16),
         ),
-        [pltpu.VMEM((held_chunks, chunk_rows, feat), F32)],
+        [pltpu.VMEM((held_chunks, half_rows, feat), F32)],
         1,
         4,
         cols * feat,
-    )(place, stay, passed, held_t, lent_back)
-    other = lax.ppermute(hand, "c", [(0, 1), (1, 0)])
+    )(place, keep, other, held_t, lent_back)
     far_t = lax.ppermute(far_t, "rep", cross)
-    share_rows = half_rows // reps
-    dealt = held_chunks * share_rows
-    mine, *parts = call(
-        deal_kernel,
-        (sds((dealt, feat), F32), *[sds((dealt, feat), BF16)] * 3),
-        [pltpu.VMEM((held_chunks, half_rows, feat), F32)],
-        1,
-        2,
-        cols * feat,
-    )(place, keep, other)
     parts = [shifted(part, k + 1) for k, part in enumerate(parts)]
     for part in parts:
         mine = mine + part.astype(F32)

time: 103 us -> 108 us (1.049)
  the two profiles are of different devices: /device:TPU:32 before, /device:TPU:6 now
where the time goes in v6:
time: 108 us; the launch traced here: 107 us
  waiting for transfers between devices  46.9 us (43%)
  starting transfers between devices  37.2 us (34%)
  Pallas kernels  16.8 us (16%)
  local copies, waits for them, and re-layouts  3.51 us (3%)
  other arithmetic  2.04 us (2%)
    ppermute x5, waiting for transfers between devices, stepped(): lax.ppermute(x, axis, [(i, partner(i)) for i in range(lax.axis_size(axis))])  23.9 us
    all_to_all x1, starting transfers between devices, shards(): arrived = lax.all_to_all(message, BLK, 0, 0, tiled=True)  12.2 us
    ppermute x5, starting transfers between devices, stepped(): lax.ppermute(x, axis, [(i, partner(i)) for i in range(lax.axis_size(axis))])  8.98 us
    all_to_all x1, starting transfers between devices, shards(): returned = lax.all_to_all(outbound, BLK, 0, 0, tiled=True)  6.37 us
    pallas_call x1, Pallas kernels, shards(): call(functools.partial(grads_kernel, sizes=(x_count, z_count)), (sds((own...  4.37 us
    ppermute x1, waiting for transfers between devices, shards(): far_t = lax.ppermute(far_t, 'rep', cross)  4.32 us
    all_to_all x1, waiting for transfers between devices, shards(): arrived = lax.all_to_all(message, BLK, 0, 0, tiled=True)  4.12 us
    ppermute x3, waiting for transfers between devices, shifted(): return lax.ppermute(x, 'rep', [(i, (i + k) % count) for i in range(count)])  4.07 us
  transfers between devices with their start and end apart: 17, of which 12 were waited for; matrix products, arithmetic and copies ran while one was open for 1% of the time, Pallas kernels for 6%

profile of v6, /device:TPU:6, one launch (start us, length us, event | category | flops | bytes accessed | tf_op | source)
XLA Modules:
  0.0 107.3 jit_solution(3265726037932710752)
XLA Ops:
  0.6 1.7 %collective-permute-start = (bf16[256,256]{1,0:T(8,128)(2,1)}, bf16[256,256]{1,0:T(8,128)(2,1)S(1)}, u32[]{:S(2)}, u32[]{:S(2)}) collective-permute-start(bf16[256,256]{1,0:T(8,128)(2,1)} %bitcast.21), channel_id=1, source_target_pairs={{0,1},{1,0},{2,3},{3,2},{4,5},{5,4},{6,7},{7,6},{8,9},{9,8},{10,11... | collective-permute-start | bytes 393224 | tf_op jit(solution)/shard_map/ppermute | solution.py:396
  2.3 3.9 %collective-permute-done = bf16[256,256]{1,0:T(8,128)(2,1)S(1)} collective-permute-done((bf16[256,256]{1,0:T(8,128)(2,1)}, bf16[256,256]{1,0:T(8,128)(2,1)S(1)}, u32[]{:S(2)}, u32[]{:S(2)}) %collective-permute-start) | collective-permute-done | bytes 131104 | tf_op jit(solution)/shard_map/ppermute | solution.py:396
  6.2 0.9 pad_maximum_fusion.near_ref
  7.1 3.1 %collective-permute-start.1 = (bf16[512,256]{1,0:T(8,128)(2,1)S(1)}, bf16[512,256]{1,0:T(8,128)(2,1)S(1)}, u32[]{:S(2)}, u32[]{:S(2)}) collective-permute-start(bf16[512,256]{1,0:T(8,128)(2,1)S(1)} %pad_maximum_fusion.near_ref), channel_id=1, source_target_pairs={{0,3},{1,2},{2,1},{3,0},{4,7},{5,6},{6,5},{7,4},{8,11},{9,10},{10,... | collective-permute-start | bytes 786440 | tf_op jit(solution)/shard_map/ppermute | solution.py:413
  10.2 1.4 %shard_map.85 = bf16[64,8,128]{2,1,0:T(8,128)(2,1)} custom-call(s32[8,64]{1,0:T(8,128)} %bitcast.16, s32[1,64]{1,0:T(1,128)} %pairs_hbm.3), custom_call_target="tpu_custom_call" | custom-call | flops 65536 | bytes 262144 | tf_op jit(solution)/shard_map/pallas_call | solution.py:397
  11.6 12.2 %all-to-all-start = ((bf16[64,8,128]{2,1,0:T(8,128)(2,1)}), bf16[64,8,128]{2,1,0:T(8,128)(2,1)S(1)}, u32[]{:S(2)}, u32[]{:S(2)}) async-start(bf16[64,8,128]{2,1,0:T(8,128)(2,1)} %shard_map.85), calls=%async_computation | async-start | bytes 262144 | tf_op jit(solution)/shard_map/all_to_all | solution.py:411
  23.8 0.1 pad_add_fusion.1.place_s
  23.9 1.2 %copy-done = bf16[2048,256]{1,0:T(8,128)(2,1)S(1)} copy-done((bf16[2048,256]{1,0:T(8,128)(2,1)S(1)}, bf16[2048,256]{1,0:T(8,128)(2,1)}, u32[]{:S(2)}) %copy-start) | copy-done | bytes 1048600
  25.1 0.7 copy-done.1
  25.8 0.7 copy-done.2
  26.5 0.7 copy-done.3
  27.2 1.4 %shard_map.84 = (s32[1,64]{1,0:T(1,128)S(1)}, s32[1,64]{1,0:T(1,128)S(1)}, s32[1,1024]{1,0:T(1,128)S(1)}, bf16[256,2048]{1,0:T(8,128)(2,1)S(1)}, f32[64,384]{1,0:T(8,128)S(1)}) custom-call(s32[4]{0:T(128)S(1)} %pad_add_fusion.1.place_s, s32[8,64]{1,0:T(8,128)S(1)} %bitcast.17, s32[1,64]{1,0:T(1,128)S(1)} %copy-done.3, s32[4,256]{1,0:T(4,128)S(1)} %bitcast.18, ...), custom_call_target="tpu_custom_call" | custom-call | flops 67108864 | bytes 2302976 | tf_op jit(solution)/shard_map/pallas_call | solution.py:414
  28.6 4.1 %all-to-all-done = bf16[64,8,128]{2,1,0:T(8,128)(2,1)S(1)} async-done(((bf16[64,8,128]{2,1,0:T(8,128)(2,1)}), bf16[64,8,128]{2,1,0:T(8,128)(2,1)S(1)}, u32[]{:S(2)}, u32[]{:S(2)}) %all-to-all-start) | async-done | bytes 131104 | tf_op jit(solution)/shard_map/all_to_all | solution.py:411
  32.7 4.0 %shard_map.86 = (bf16[1024,256]{1,0:T(8,128)(2,1)S(1)}, bf16[1024,256]{1,0:T(8,128)(2,1)S(1)}, f32[3,1024]{1,0:T(4,128)S(1)}, f32[8,1024]{1,0:T(8,128)S(1)}, f32...) custom-call(s32[1,64]{1,0:T(1,128)S(1)} %get-tuple-element.31.pair_s, s32[4]{0:T(128)S(1)} %pad_add_fusion.1.place_s, ...), custom_call_target="tpu_custom_call" | custom-call | flops 1610612736 | bytes 4292608 | tf_op jit(solution)/shard_map/pallas_call | solution.py:437
  36.7 0.2 collective-permute-start.2
  36.9 3.6 %collective-permute-done.2 = f32[3,1024]{1,0:T(4,128)S(1)} collective-permute-done((f32[3,1024]{1,0:T(4,128)S(1)}, f32[3,1024]{1,0:T(4,128)S(1)}, u32[]{:S(2)}, u32[]{:S(2)}) %collective-permute-start.2) | collective-permute-done | bytes 12320 | tf_op jit(solution)/shard_map/ppermute | solution.py:456
  40.6 0.3 collective-permute-start.3
  40.9 1.7 %shard_map.87 = (bf16[8,256,1024]{2,1,0:T(8,128)(2,1)S(1)}, f32[1024,1024]{1,0:T(8,128)S(1)}) custom-call(f32[8,1024]{1,0:T(8,128)S(1)} %get-tuple-element.40.codes_ref, bf16[1024,256]{1,0:T(8,128)(2,1)S(1)} %get-tuple-element.36.u_ref, bf16[1024,256]{1,0:T(8,128)(2,1)S(1)} %get-tuple-element.37.q_ref, f32[3,1024]{1,0:T(4,128)S(1)} %get-tuple-element.35.st_ref), custom_call_target="tpu_custom_call" | custom-call | flops 2097152 | bytes 16777216 | tf_op jit(solution)/shard_map/pallas_call | solution.py:457
  42.6 3.0 %collective-permute-done.3.stb_ref = f32[3,1024]{1,0:T(4,128)S(1)} collective-permute-done((f32[3,1024]{1,0:T(4,128)S(1)}, f32[3,1024]{1,0:T(4,128)S(1)}, u32[]{:S(2)}, u32[]{:S(2)}) %collective-permute-start.3) | collective-permute-done | bytes 12320 | tf_op jit(solution)/shard_map/ppermute | solution.py:466
  45.6 4.4 %shard_map.88 = (bf16[128,16,256]{2,1,0:T(8,128)(2,1)}, f32[1,256]{1,0:T(1,128)}, f32[2,256,256]{2,1,0:T(8,128)S(1)}, bf16[2,256,256]{2,1,0:T(8,128)(2,1)S(1)}, ...) custom-call(s32[1,64]{1,0:T(1,128)S(1)} %get-tuple-element.31.pair_s, s32[1,64]{1,0:T(1,128)S(1)} %get-tuple-element.32.slot_s, ...), custom_call_target="tpu_custom_call" | custom-call | flops 2147483648 | bytes 6817792 | tf_op jit(solution)/shard_map/pallas_call | solution.py:472
  50.0 0.8 collective-permute-start.4
  50.8 10.8 %collective-permute-done.4.recv_ref = bf16[16,64,256]{2,1,0:T(8,128)(2,1)S(1)} collective-permute-done((bf16[16,64,256]{2,1,0:T(8,128)(2,1)S(1)}, bf16[16,64,256]{2,1,0:T(8,128)(2,1)S(1)}, u32[]{:S(2)}, u32[]{:S(2)}) %collective-permute-start.4) | collective-permute-done | bytes 524320 | tf_op jit(solution)/shard_map/ppermute | solution.py:375
  61.6 0.7 shard_map.89
  62.3 0.1 collective-permute-start.5
  62.4 6.4 %all-to-all-start.1 = ((bf16[64,32,256]{2,1,0:T(8,128)(2,1)}), bf16[64,32,256]{2,1,0:T(8,128)(2,1)S(1)}, u32[]{:S(2)}, u32[]{:S(2)}) async-start(bf16[64,32,256]{2,1,0:T(8,128)(2,1)} %bitcast.11), calls=%async_computation.1 | async-start | bytes 2097152 | tf_op jit(solution)/shard_map/all_to_all | solution.py:498
  68.8 0.7 shard_map.90
  69.6 0.1 collective-permute-start.8
  69.7 2.4 %collective-permute-start.9 = (bf16[128,256]{1,0:T(8,128)(2,1)S(1)}, bf16[128,256]{1,0:T(8,128)(2,1)S(1)}, u32[]{:S(2)}, u32[]{:S(2)}) collective-permute-start(bf16[128,256]{1,0:T(8,128)(2,1)S(1)} %get-tuple-element.56), channel_id=1, source_target_pairs={{0,2},{1,3},{2,0},{3,1},{4,6},{5,7},{6,4},{7,5},{8,10},{9,11},{10,... | collective-permute-start | bytes 196616 | tf_op jit(solution)/shard_map/ppermute | solution.py:371
  72.0 0.9 collective-permute-start.10
  72.9 3.5 %collective-permute-done.8 = bf16[128,256]{1,0:T(8,128)(2,1)S(1)} collective-permute-done((bf16[128,256]{1,0:T(8,128)(2,1)S(1)}, bf16[128,256]{1,0:T(8,128)(2,1)S(1)}, u32[]{:S(2)}, u32[]{:S(2)}) %collective-permute-start.8) | collective-permute-done | bytes 65568 | tf_op jit(solution)/shard_map/ppermute | solution.py:371
  76.4 0.6 collective-permute-done.10
  77.0 0.8 collective-permute-start.11
  77.8 0.1 slice_convert_fusion.2
  78.0 3.4 %collective-permute-done.11 = bf16[64,256]{1,0:T(8,128)(2,1)S(1)} collective-permute-done((bf16[64,256]{1,0:T(8,128)(2,1)S(1)}, bf16[64,256]{1,0:T(8,128)(2,1)S(1)}, u32[]{:S(2)}, u32[]{:S(2)}) %collective-permute-start.11) | collective-permute-done | bytes 32800 | tf_op jit(solution)/shard_map/ppermute | solution.py:375
  81.4 0.1 collective-permute-start.12
  81.5 0.2 compare_reduce_fusion
  81.7 4.8 %collective-permute-done.12 = bf16[32,256]{1,0:T(8,128)(2,1)S(1)} collective-permute-done((bf16[32,256]{1,0:T(8,128)(2,1)S(1)}, bf16[32,256]{1,0:T(8,128)(2,1)S(1)}, u32[]{:S(2)}, u32[]{:S(2)}) %collective-permute-start.12) | collective-permute-done | bytes 16416 | tf_op jit(solution)/shard_map/ppermute | solution.py:375
  86.6 2.6 %collective-permute-start.13 = (bf16[16,256]{1,0:T(8,128)(2,1)S(1)}, bf16[16,256]{1,0:T(8,128)(2,1)S(1)}, u32[]{:S(2)}, u32[]{:S(2)}) collective-permute-start(bf16[16,256]{1,0:T(8,128)(2,1)S(1)} %slice.140), channel_id=1, source_target_pairs={{0,56},{8,16},{16,8},{24,32},{32,24},{40,48},{48,40},{56,0},{1,57}... | collective-permute-start | bytes 24584 | tf_op jit(solution)/shard_map/ppermute | solution.py:375
  89.1 4.5 %collective-permute-done.13 = bf16[16,256]{1,0:T(8,128)(2,1)S(1)} collective-permute-done((bf16[16,256]{1,0:T(8,128)(2,1)S(1)}, bf16[16,256]{1,0:T(8,128)(2,1)S(1)}, u32[]{:S(2)}, u32[]{:S(2)}) %collective-permute-start.13) | collective-permute-done | bytes 8224 | tf_op jit(solution)/shard_map/ppermute | solution.py:375
  93.7 4.7 %collective-permute-start.14 = (bf16[8,256]{1,0:T(8,128)(2,1)S(1)}, bf16[8,256]{1,0:T(8,128)(2,1)S(1)}, u32[]{:S(2)}, u32[]{:S(2)}) collective-permute-start(bf16[8,256]{1,0:T(8,128)(2,1)S(1)} %slice.141), channel_id=1, source_target_pairs={{0,24},{8,48},{16,40},{24,0},{32,56},{40,16},{48,8},{56,32},{1,25}... | collective-permute-start | bytes 12296 | tf_op jit(solution)/shard_map/ppermute | solution.py:375
  98.4 0.1 copy.10
  98.5 0.1 reshape.33.slot_j
  98.6 1.0 collective-permute-start.7
  99.6 0.3 collective-permute-done.14
  99.9 0.6 slice_add_fusion.3
  100.5 4.3 %collective-permute-done.7.far_ref = bf16[256,256]{1,0:T(8,128)(2,1)S(1)} collective-permute-done((bf16[256,256]{1,0:T(8,128)(2,1)S(1)}, bf16[256,256]{1,0:T(8,128)(2,1)S(1)}, u32[]{:S(2)}, u32[]{:S(2)}) %collective-permute-start.7) | collective-permute-done | bytes 131104 | tf_op jit(solution)/shard_map/ppermute | solution.py:532
  104.9 0.8 shard_map.91
  105.7 1.5 %shard_map.92 = f32[64,256]{1,0:T(8,128)} custom-call(s32[128]{0:T(128)S(1)} %reshape.33.slot_j, bf16[128,16,256]{2,1,0:T(8,128)(2,1)S(1)} %bitcast.14, f32[64,384]{1,0:T(8,128)S(1)} %get-tuple-element.53.unit_ref), custom_call_target="tpu_custom_call" | custom-call | flops 524288 | bytes 131072 | tf_op jit(solution)/shard_map/pallas_call | solution.py:559
  (23 shorter events, 0.2 us)
Async XLA Ops:
  0.6 5.5 %collective-permute-start = (bf16[256,256]{1,0:T(8,128)(2,1)}, bf16[256,256]{1,0:T(8,128)(2,1)S(1)}, u32[]{:S(2)}, u32[]{:S(2)}) collective-permute-start(bf16[256,256]{1,0:T(8,128)(2,1)} %bitcast.21), channel_id=1, source_target_pairs={{0,1},{1,0},{2,3},{3,2},{4,5},{5,4},{6,7},{7,6},{8,9},{9,8},{10,11... | collective-permute-start | bytes 393224 | tf_op jit(solution)/shard_map/ppermute | solution.py:396
  7.1 25.6 %collective-permute-start.1 = (bf16[512,256]{1,0:T(8,128)(2,1)S(1)}, bf16[512,256]{1,0:T(8,128)(2,1)S(1)}, u32[]{:S(2)}, u32[]{:S(2)}) collective-permute-start(bf16[512,256]{1,0:T(8,128)(2,1)S(1)} %pad_maximum_fusion.near_ref), channel_id=1, source_target_pairs={{0,3},{1,2},{2,1},{3,0},{4,7},{5,6},{6,5},{7,4},{8,11},{9,10},{10,... | collective-permute-start | bytes 786440 | tf_op jit(solution)/shard_map/ppermute | solution.py:413
  11.6 21.0 %all-to-all-start = ((bf16[64,8,128]{2,1,0:T(8,128)(2,1)}), bf16[64,8,128]{2,1,0:T(8,128)(2,1)S(1)}, u32[]{:S(2)}, u32[]{:S(2)}) async-start(bf16[64,8,128]{2,1,0:T(8,128)(2,1)} %shard_map.85), calls=%async_computation | async-start | bytes 262144 | tf_op jit(solution)/shard_map/all_to_all | solution.py:411
  23.9 1.2 %copy-start = (bf16[2048,256]{1,0:T(8,128)(2,1)S(1)}, bf16[2048,256]{1,0:T(8,128)(2,1)}, u32[]{:S(2)}) copy-start(bf16[2048,256]{1,0:T(8,128)(2,1)} %books_hbm.1) | copy-start | bytes 3145732
  25.1 0.7 copy-start.1
  25.8 0.7 copy-start.2
  26.5 0.7 copy-start.3
  36.7 3.8 %collective-permute-start.2 = (f32[3,1024]{1,0:T(4,128)S(1)}, f32[3,1024]{1,0:T(4,128)S(1)}, u32[]{:S(2)}, u32[]{:S(2)}) collective-permute-start(f32[3,1024]{1,0:T(4,128)S(1)} %get-tuple-element.35.st_ref), channel_id=1, source_target_pairs={{0,1},{1,0},{2,3},{3,2},{4,5},{5,4},{6,7},{7,6},{8,9},{9,8},{10,11... | collective-permute-start | bytes 36872 | tf_op jit(solution)/shard_map/ppermute | solution.py:456
  40.6 5.0 %collective-permute-start.3 = (f32[3,1024]{1,0:T(4,128)S(1)}, f32[3,1024]{1,0:T(4,128)S(1)}, u32[]{:S(2)}, u32[]{:S(2)}) collective-permute-start(f32[3,1024]{1,0:T(4,128)S(1)} %pad_maximum_fusion.1.sta_ref), channel_id=1, source_target_pairs={{0,3},{1,2},{2,1},{3,0},{4,7},{5,6},{6,5},{7,4},{8,11},{9,10},{10,... | collective-permute-start | bytes 36872 | tf_op jit(solution)/shard_map/ppermute | solution.py:466
  50.0 11.6 %collective-permute-start.4 = (bf16[16,64,256]{2,1,0:T(8,128)(2,1)S(1)}, bf16[16,64,256]{2,1,0:T(8,128)(2,1)S(1)}, u32[]{:S(2)}, u32[]{:S(2)}) collective-permute-start(bf16[16,64,256]{2,1,0:T(8,128)(2,1)S(1)} %get-tuple-element.45), channel_id=1, source_target_pairs={{0,8},{8,0},{16,24},{24,16},{32,40},{40,32},{48,56},{56,48},{1,9},... | collective-permute-start | bytes 1572872 | tf_op jit(solution)/shard_map/ppermute | solution.py:375
  50.8 18.0 %collective-permute-start.6 = (bf16[2,256,256]{2,1,0:T(8,128)(2,1)S(1)}, bf16[2,256,256]{2,1,0:T(8,128)(2,1)S(1)}, u32[]{:S(2)}, u32[]{:S(2)}) collective-permute-start(bf16[2,256,256]{2,1,0:T(8,128)(2,1)S(1)} %get-tuple-element.49), channel_id=1, source_target_pairs={{0,1},{1,0},{2,3},{3,2},{4,5},{5,4},{6,7},{7,6},{8,9},{9,8},{10,11... | collective-permute-start | bytes 786440 | tf_op jit(solution)/shard_map/ppermute | solution.py:504
  62.3 6.5 %collective-permute-start.5 = (bf16[16,32,256]{2,1,0:T(8,128)(2,1)S(1)}, bf16[16,32,256]{2,1,0:T(8,128)(2,1)S(1)}, u32[]{:S(2)}, u32[]{:S(2)}) collective-permute-start(bf16[16,32,256]{2,1,0:T(8,128)(2,1)S(1)} %get-tuple-element.47), channel_id=1, source_target_pairs={{0,4},{4,0},{1,5},{5,1},{2,6},{6,2},{3,7},{7,3},{8,12},{12,8},{9,1... | collective-permute-start | bytes 786440 | tf_op jit(solution)/shard_map/ppermute | solution.py:516
  62.4 43.3 %all-to-all-start.1 = ((bf16[64,32,256]{2,1,0:T(8,128)(2,1)}), bf16[64,32,256]{2,1,0:T(8,128)(2,1)S(1)}, u32[]{:S(2)}, u32[]{:S(2)}) async-start(bf16[64,32,256]{2,1,0:T(8,128)(2,1)} %bitcast.11), calls=%async_computation.1 | async-start | bytes 2097152 | tf_op jit(solution)/shard_map/all_to_all | solution.py:498
  69.6 6.8 %collective-permute-start.8 = (bf16[128,256]{1,0:T(8,128)(2,1)S(1)}, bf16[128,256]{1,0:T(8,128)(2,1)S(1)}, u32[]{:S(2)}, u32[]{:S(2)}) collective-permute-start(bf16[128,256]{1,0:T(8,128)(2,1)S(1)} %get-tuple-element.55), channel_id=1, source_target_pairs={{0,1},{1,2},{2,3},{3,0},{4,5},{5,6},{6,7},{7,4},{8,9},{9,10},{10,1... | collective-permute-start | bytes 196616 | tf_op jit(solution)/shard_map/ppermute | solution.py:371
  69.7 6.7 %collective-permute-start.9 = (bf16[128,256]{1,0:T(8,128)(2,1)S(1)}, bf16[128,256]{1,0:T(8,128)(2,1)S(1)}, u32[]{:S(2)}, u32[]{:S(2)}) collective-permute-start(bf16[128,256]{1,0:T(8,128)(2,1)S(1)} %get-tuple-element.56), channel_id=1, source_target_pairs={{0,2},{1,3},{2,0},{3,1},{4,6},{5,7},{6,4},{7,5},{8,10},{9,11},{10,... | collective-permute-start | bytes 196616 | tf_op jit(solution)/shard_map/ppermute | solution.py:371
  72.0 4.9 %collective-permute-start.10 = (bf16[128,256]{1,0:T(8,128)(2,1)S(1)}, bf16[128,256]{1,0:T(8,128)(2,1)S(1)}, u32[]{:S(2)}, u32[]{:S(2)}) collective-permute-start(bf16[128,256]{1,0:T(8,128)(2,1)S(1)} %get-tuple-element.57), channel_id=1, source_target_pairs={{0,3},{1,0},{2,1},{3,2},{4,7},{5,4},{6,5},{7,6},{8,11},{9,8},{10,9... | collective-permute-start | bytes 196616 | tf_op jit(solution)/shard_map/ppermute | solution.py:371
  77.0 4.4 %collective-permute-start.11 = (bf16[64,256]{1,0:T(8,128)(2,1)S(1)}, bf16[64,256]{1,0:T(8,128)(2,1)S(1)}, u32[]{:S(2)}, u32[]{:S(2)}) collective-permute-start(bf16[64,256]{1,0:T(8,128)(2,1)S(1)} %slice.138), channel_id=1, source_target_pairs={{0,64},{64,0},{128,192},{192,128},{1,65},{65,1},{129,193},{193,129... | collective-permute-start | bytes 98312 | tf_op jit(solution)/shard_map/ppermute | solution.py:375
  81.4 5.1 %collective-permute-start.12 = (bf16[32,256]{1,0:T(8,128)(2,1)S(1)}, bf16[32,256]{1,0:T(8,128)(2,1)S(1)}, u32[]{:S(2)}, u32[]{:S(2)}) collective-permute-start(bf16[32,256]{1,0:T(8,128)(2,1)S(1)} %slice.139), channel_id=1, source_target_pairs={{0,192},{64,128},{128,64},{192,0},{1,193},{65,129},{129,65},{193,1... | collective-permute-start | bytes 49160 | tf_op jit(solution)/shard_map/ppermute | solution.py:375
  86.6 7.1 %collective-permute-start.13 = (bf16[16,256]{1,0:T(8,128)(2,1)S(1)}, bf16[16,256]{1,0:T(8,128)(2,1)S(1)}, u32[]{:S(2)}, u32[]{:S(2)}) collective-permute-start(bf16[16,256]{1,0:T(8,128)(2,1)S(1)} %slice.140), channel_id=1, source_target_pairs={{0,56},{8,16},{16,8},{24,32},{32,24},{40,48},{48,40},{56,0},{1,57}... | collective-permute-start | bytes 24584 | tf_op jit(solution)/shard_map/ppermute | solution.py:375
  93.7 6.3 %collective-permute-start.14 = (bf16[8,256]{1,0:T(8,128)(2,1)S(1)}, bf16[8,256]{1,0:T(8,128)(2,1)S(1)}, u32[]{:S(2)}, u32[]{:S(2)}) collective-permute-start(bf16[8,256]{1,0:T(8,128)(2,1)S(1)} %slice.141), channel_id=1, source_target_pairs={{0,24},{8,48},{16,40},{24,0},{32,56},{40,16},{48,8},{56,32},{1,25}... | collective-permute-start | bytes 12296 | tf_op jit(solution)/shard_map/ppermute | solution.py:375
  98.6 6.3 %collective-permute-start.7 = (bf16[256,256]{1,0:T(8,128)(2,1)S(1)}, bf16[256,256]{1,0:T(8,128)(2,1)S(1)}, u32[]{:S(2)}, u32[]{:S(2)}) collective-permute-start(bf16[256,256]{1,0:T(8,128)(2,1)S(1)} %get-tuple-element.51), channel_id=1, source_target_pairs={{0,3},{1,2},{2,1},{3,0},{4,7},{5,6},{6,5},{7,4},{8,11},{9,10},{10,... | collective-permute-start | bytes 393224 | tf_op jit(solution)/shard_map/ppermute | solution.py:532

commit v7 on v6

--- a/solution.py
+++ b/solution.py
@@ -326,8 +326,8 @@
     place_s, stay_ref, recv_ref, held_ref, back_ref,
     own_ref, far1, far2, far3, half_ref, over_ref, sum_ref,
 ):
-    half_ref[...] = held_ref[0] + back_ref[0].astype(F32)
-    over_ref[...] = (held_ref[1] + back_ref[1].astype(F32)).astype(BF16)
+    half_ref[...] = held_ref[0].astype(F32) + back_ref[0].astype(F32)
+    over_ref[...] = (held_ref[1].astype(F32) + back_ref[1].astype(F32)).astype(BF16)
     rep = place_s[3]
     chunks = stay_ref.shape[0]
     share = own_ref.shape[0] // chunks
@@ -474,7 +474,7 @@
         (
             sds((owners * CAP, PR, feat), BF16),
             sds((1, row_count), F32),
-            sds((2, feat, row_count), F32),
+            sds((2, feat, row_count), BF16),
             sds((2, feat, row_count), BF16),
             sds((held_chunks, chunk_rows, feat), F32),
             sds((held_chunks, chunk_rows, feat), BF16),

time: 108 us -> 108 us (level)
  no operation moved by 1% of the time
where the time goes in v7:
time: 108 us; the launch traced here: 107 us
  waiting for transfers between devices  46.9 us (43%)
  starting transfers between devices  37.2 us (34%)
  Pallas kernels  16.8 us (16%)
  local copies, waits for them, and re-layouts  3.51 us (3%)
  other arithmetic  2.04 us (2%)
    ppermute x5, waiting for transfers between devices, stepped(): lax.ppermute(x, axis, [(i, partner(i)) for i in range(lax.axis_size(axis))])  23.9 us
    all_to_all x1, starting transfers between devices, shards(): arrived = lax.all_to_all(message, BLK, 0, 0, tiled=True)  12.2 us
    ppermute x5, starting transfers between devices, stepped(): lax.ppermute(x, axis, [(i, partner(i)) for i in range(lax.axis_size(axis))])  8.99 us
    all_to_all x1, starting transfers between devices, shards(): returned = lax.all_to_all(outbound, BLK, 0, 0, tiled=True)  6.37 us
    pallas_call x1, Pallas kernels, shards(): call(functools.partial(grads_kernel, sizes=(x_count, z_count)), (sds((own...  4.36 us
    ppermute x1, waiting for transfers between devices, shards(): far_t = lax.ppermute(far_t, 'rep', cross)  4.32 us
    all_to_all x1, waiting for transfers between devices, shards(): arrived = lax.all_to_all(message, BLK, 0, 0, tiled=True)  4.12 us
    ppermute x3, waiting for transfers between devices, shifted(): return lax.ppermute(x, 'rep', [(i, (i + k) % count) for i in range(count)])  4.07 us
  transfers between devices with their start and end apart: 17, of which 12 were waited for; matrix products, arithmetic and copies ran while one was open for 1% of the time, Pallas kernels for 6%

profile of v7, /device:TPU:6, one launch (start us, length us, event | category | flops | bytes accessed | tf_op | source)
XLA Modules:
  0.0 107.2 jit_solution(2571727147076130285)
XLA Ops:
  0.6 1.7 %collective-permute-start = (bf16[256,256]{1,0:T(8,128)(2,1)}, bf16[256,256]{1,0:T(8,128)(2,1)S(1)}, u32[]{:S(2)}, u32[]{:S(2)}) collective-permute-start(bf16[256,256]{1,0:T(8,128)(2,1)} %bitcast.21), channel_id=1, source_target_pairs={{0,1},{1,0},{2,3},{3,2},{4,5},{5,4},{6,7},{7,6},{8,9},{9,8},{10,11... | collective-permute-start | bytes 393224 | tf_op jit(solution)/shard_map/ppermute | solution.py:396
  2.3 3.9 %collective-permute-done = bf16[256,256]{1,0:T(8,128)(2,1)S(1)} collective-permute-done((bf16[256,256]{1,0:T(8,128)(2,1)}, bf16[256,256]{1,0:T(8,128)(2,1)S(1)}, u32[]{:S(2)}, u32[]{:S(2)}) %collective-permute-start) | collective-permute-done | bytes 131104 | tf_op jit(solution)/shard_map/ppermute | solution.py:396
  6.2 0.9 pad_maximum_fusion.near_ref
  7.1 3.1 %collective-permute-start.1 = (bf16[512,256]{1,0:T(8,128)(2,1)S(1)}, bf16[512,256]{1,0:T(8,128)(2,1)S(1)}, u32[]{:S(2)}, u32[]{:S(2)}) collective-permute-start(bf16[512,256]{1,0:T(8,128)(2,1)S(1)} %pad_maximum_fusion.near_ref), channel_id=1, source_target_pairs={{0,3},{1,2},{2,1},{3,0},{4,7},{5,6},{6,5},{7,4},{8,11},{9,10},{10,... | collective-permute-start | bytes 786440 | tf_op jit(solution)/shard_map/ppermute | solution.py:413
  10.2 1.4 %shard_map.85 = bf16[64,8,128]{2,1,0:T(8,128)(2,1)} custom-call(s32[8,64]{1,0:T(8,128)} %bitcast.16, s32[1,64]{1,0:T(1,128)} %pairs_hbm.3), custom_call_target="tpu_custom_call" | custom-call | flops 65536 | bytes 262144 | tf_op jit(solution)/shard_map/pallas_call | solution.py:397
  11.6 12.2 %all-to-all-start = ((bf16[64,8,128]{2,1,0:T(8,128)(2,1)}), bf16[64,8,128]{2,1,0:T(8,128)(2,1)S(1)}, u32[]{:S(2)}, u32[]{:S(2)}) async-start(bf16[64,8,128]{2,1,0:T(8,128)(2,1)} %shard_map.85), calls=%async_computation | async-start | bytes 262144 | tf_op jit(solution)/shard_map/all_to_all | solution.py:411
  23.8 0.1 pad_add_fusion.1.place_s
  23.9 1.2 %copy-done = bf16[2048,256]{1,0:T(8,128)(2,1)S(1)} copy-done((bf16[2048,256]{1,0:T(8,128)(2,1)S(1)}, bf16[2048,256]{1,0:T(8,128)(2,1)}, u32[]{:S(2)}) %copy-start) | copy-done | bytes 1048600
  25.1 0.7 copy-done.1
  25.8 0.7 copy-done.2
  26.5 0.7 copy-done.3
  27.2 1.4 %shard_map.84 = (s32[1,64]{1,0:T(1,128)S(1)}, s32[1,64]{1,0:T(1,128)S(1)}, s32[1,1024]{1,0:T(1,128)S(1)}, bf16[256,2048]{1,0:T(8,128)(2,1)S(1)}, f32[64,384]{1,0:T(8,128)S(1)}) custom-call(s32[4]{0:T(128)S(1)} %pad_add_fusion.1.place_s, s32[8,64]{1,0:T(8,128)S(1)} %bitcast.17, s32[1,64]{1,0:T(1,128)S(1)} %copy-done.3, s32[4,256]{1,0:T(4,128)S(1)} %bitcast.18, ...), custom_call_target="tpu_custom_call" | custom-call | flops 67108864 | bytes 2302976 | tf_op jit(solution)/shard_map/pallas_call | solution.py:414
  28.6 4.1 %all-to-all-done = bf16[64,8,128]{2,1,0:T(8,128)(2,1)S(1)} async-done(((bf16[64,8,128]{2,1,0:T(8,128)(2,1)}), bf16[64,8,128]{2,1,0:T(8,128)(2,1)S(1)}, u32[]{:S(2)}, u32[]{:S(2)}) %all-to-all-start) | async-done | bytes 131104 | tf_op jit(solution)/shard_map/all_to_all | solution.py:411
  32.7 4.0 %shard_map.86 = (bf16[1024,256]{1,0:T(8,128)(2,1)S(1)}, bf16[1024,256]{1,0:T(8,128)(2,1)S(1)}, f32[3,1024]{1,0:T(4,128)S(1)}, f32[8,1024]{1,0:T(8,128)S(1)}, f32...) custom-call(s32[1,64]{1,0:T(1,128)S(1)} %get-tuple-element.31.pair_s, s32[4]{0:T(128)S(1)} %pad_add_fusion.1.place_s, ...), custom_call_target="tpu_custom_call" | custom-call | flops 1610612736 | bytes 4292608 | tf_op jit(solution)/shard_map/pallas_call | solution.py:437
  36.7 0.2 collective-permute-start.2
  36.9 3.6 %collective-permute-done.2 = f32[3,1024]{1,0:T(4,128)S(1)} collective-permute-done((f32[3,1024]{1,0:T(4,128)S(1)}, f32[3,1024]{1,0:T(4,128)S(1)}, u32[]{:S(2)}, u32[]{:S(2)}) %collective-permute-start.2) | collective-permute-done | bytes 12320 | tf_op jit(solution)/shard_map/ppermute | solution.py:456
  40.6 0.3 collective-permute-start.3
  40.9 1.7 %shard_map.87 = (bf16[8,256,1024]{2,1,0:T(8,128)(2,1)S(1)}, f32[1024,1024]{1,0:T(8,128)S(1)}) custom-call(f32[8,1024]{1,0:T(8,128)S(1)} %get-tuple-element.40.codes_ref, bf16[1024,256]{1,0:T(8,128)(2,1)S(1)} %get-tuple-element.36.u_ref, bf16[1024,256]{1,0:T(8,128)(2,1)S(1)} %get-tuple-element.37.q_ref, f32[3,1024]{1,0:T(4,128)S(1)} %get-tuple-element.35.st_ref), custom_call_target="tpu_custom_call" | custom-call | flops 2097152 | bytes 16777216 | tf_op jit(solution)/shard_map/pallas_call | solution.py:457
  42.6 3.0 %collective-permute-done.3.stb_ref = f32[3,1024]{1,0:T(4,128)S(1)} collective-permute-done((f32[3,1024]{1,0:T(4,128)S(1)}, f32[3,1024]{1,0:T(4,128)S(1)}, u32[]{:S(2)}, u32[]{:S(2)}) %collective-permute-start.3) | collective-permute-done | bytes 12320 | tf_op jit(solution)/shard_map/ppermute | solution.py:466
  45.6 4.4 %shard_map.88 = (bf16[128,16,256]{2,1,0:T(8,128)(2,1)}, f32[1,256]{1,0:T(1,128)}, bf16[2,256,256]{2,1,0:T(8,128)(2,1)S(1)}, bf16[2,256,256]{2,1,0:T(8,128)(2,1)S...) custom-call(s32[1,64]{1,0:T(1,128)S(1)} %get-tuple-element.31.pair_s, ...), custom_call_target="tpu_custom_call" | custom-call | flops 2147483648 | bytes 6293504 | tf_op jit(solution)/shard_map/pallas_call | solution.py:472
  50.0 0.8 collective-permute-start.4
  50.8 10.8 %collective-permute-done.4.recv_ref = bf16[16,64,256]{2,1,0:T(8,128)(2,1)S(1)} collective-permute-done((bf16[16,64,256]{2,1,0:T(8,128)(2,1)S(1)}, bf16[16,64,256]{2,1,0:T(8,128)(2,1)S(1)}, u32[]{:S(2)}, u32[]{:S(2)}) %collective-permute-start.4) | collective-permute-done | bytes 524320 | tf_op jit(solution)/shard_map/ppermute | solution.py:375
  61.6 0.7 shard_map.89
  62.3 0.1 collective-permute-start.5
  62.4 6.4 %all-to-all-start.1 = ((bf16[64,32,256]{2,1,0:T(8,128)(2,1)}), bf16[64,32,256]{2,1,0:T(8,128)(2,1)S(1)}, u32[]{:S(2)}, u32[]{:S(2)}) async-start(bf16[64,32,256]{2,1,0:T(8,128)(2,1)} %bitcast.11), calls=%async_computation.1 | async-start | bytes 2097152 | tf_op jit(solution)/shard_map/all_to_all | solution.py:498
  68.8 0.7 shard_map.90
  69.6 0.1 collective-permute-start.8
  69.7 2.4 %collective-permute-start.9 = (bf16[128,256]{1,0:T(8,128)(2,1)S(1)}, bf16[128,256]{1,0:T(8,128)(2,1)S(1)}, u32[]{:S(2)}, u32[]{:S(2)}) collective-permute-start(bf16[128,256]{1,0:T(8,128)(2,1)S(1)} %get-tuple-element.56), channel_id=1, source_target_pairs={{0,2},{1,3},{2,0},{3,1},{4,6},{5,7},{6,4},{7,5},{8,10},{9,11},{10,... | collective-permute-start | bytes 196616 | tf_op jit(solution)/shard_map/ppermute | solution.py:371
  72.0 0.9 collective-permute-start.10
  72.9 3.5 %collective-permute-done.8 = bf16[128,256]{1,0:T(8,128)(2,1)S(1)} collective-permute-done((bf16[128,256]{1,0:T(8,128)(2,1)S(1)}, bf16[128,256]{1,0:T(8,128)(2,1)S(1)}, u32[]{:S(2)}, u32[]{:S(2)}) %collective-permute-start.8) | collective-permute-done | bytes 65568 | tf_op jit(solution)/shard_map/ppermute | solution.py:371
  76.4 0.6 collective-permute-done.10
  77.0 0.8 collective-permute-start.11
  77.9 0.1 slice_convert_fusion.2
  78.0 3.4 %collective-permute-done.11 = bf16[64,256]{1,0:T(8,128)(2,1)S(1)} collective-permute-done((bf16[64,256]{1,0:T(8,128)(2,1)S(1)}, bf16[64,256]{1,0:T(8,128)(2,1)S(1)}, u32[]{:S(2)}, u32[]{:S(2)}) %collective-permute-start.11) | collective-permute-done | bytes 32800 | tf_op jit(solution)/shard_map/ppermute | solution.py:375
  81.4 0.1 collective-permute-start.12
  81.5 0.2 compare_reduce_fusion
  81.7 4.8 %collective-permute-done.12 = bf16[32,256]{1,0:T(8,128)(2,1)S(1)} collective-permute-done((bf16[32,256]{1,0:T(8,128)(2,1)S(1)}, bf16[32,256]{1,0:T(8,128)(2,1)S(1)}, u32[]{:S(2)}, u32[]{:S(2)}) %collective-permute-start.12) | collective-permute-done | bytes 16416 | tf_op jit(solution)/shard_map/ppermute | solution.py:375
  86.6 2.6 %collective-permute-start.13 = (bf16[16,256]{1,0:T(8,128)(2,1)S(1)}, bf16[16,256]{1,0:T(8,128)(2,1)S(1)}, u32[]{:S(2)}, u32[]{:S(2)}) collective-permute-start(bf16[16,256]{1,0:T(8,128)(2,1)S(1)} %slice.140), channel_id=1, source_target_pairs={{0,56},{8,16},{16,8},{24,32},{32,24},{40,48},{48,40},{56,0},{1,57}... | collective-permute-start | bytes 24584 | tf_op jit(solution)/shard_map/ppermute | solution.py:375
  89.2 4.5 %collective-permute-done.13 = bf16[16,256]{1,0:T(8,128)(2,1)S(1)} collective-permute-done((bf16[16,256]{1,0:T(8,128)(2,1)S(1)}, bf16[16,256]{1,0:T(8,128)(2,1)S(1)}, u32[]{:S(2)}, u32[]{:S(2)}) %collective-permute-start.13) | collective-permute-done | bytes 8224 | tf_op jit(solution)/shard_map/ppermute | solution.py:375
  93.7 4.7 %collective-permute-start.14 = (bf16[8,256]{1,0:T(8,128)(2,1)S(1)}, bf16[8,256]{1,0:T(8,128)(2,1)S(1)}, u32[]{:S(2)}, u32[]{:S(2)}) collective-permute-start(bf16[8,256]{1,0:T(8,128)(2,1)S(1)} %slice.141), channel_id=1, source_target_pairs={{0,24},{8,48},{16,40},{24,0},{32,56},{40,16},{48,8},{56,32},{1,25}... | collective-permute-start | bytes 12296 | tf_op jit(solution)/shard_map/ppermute | solution.py:375
  98.3 0.1 copy.10
  98.4 0.1 reshape.33.slot_j
  98.6 1.0 collective-permute-start.7
  99.6 0.3 collective-permute-done.14
  99.9 0.6 slice_add_fusion.3
  100.5 4.3 %collective-permute-done.7.far_ref = bf16[256,256]{1,0:T(8,128)(2,1)S(1)} collective-permute-done((bf16[256,256]{1,0:T(8,128)(2,1)S(1)}, bf16[256,256]{1,0:T(8,128)(2,1)S(1)}, u32[]{:S(2)}, u32[]{:S(2)}) %collective-permute-start.7) | collective-permute-done | bytes 131104 | tf_op jit(solution)/shard_map/ppermute | solution.py:532
  104.9 0.8 shard_map.91
  105.7 1.5 %shard_map.92 = f32[64,256]{1,0:T(8,128)} custom-call(s32[128]{0:T(128)S(1)} %reshape.33.slot_j, bf16[128,16,256]{2,1,0:T(8,128)(2,1)S(1)} %bitcast.14, f32[64,384]{1,0:T(8,128)S(1)} %get-tuple-element.53.unit_ref), custom_call_target="tpu_custom_call" | custom-call | flops 524288 | bytes 131072 | tf_op jit(solution)/shard_map/pallas_call | solution.py:559
  (23 shorter events, 0.2 us)
Async XLA Ops:
  0.6 5.5 %collective-permute-start = (bf16[256,256]{1,0:T(8,128)(2,1)}, bf16[256,256]{1,0:T(8,128)(2,1)S(1)}, u32[]{:S(2)}, u32[]{:S(2)}) collective-permute-start(bf16[256,256]{1,0:T(8,128)(2,1)} %bitcast.21), channel_id=1, source_target_pairs={{0,1},{1,0},{2,3},{3,2},{4,5},{5,4},{6,7},{7,6},{8,9},{9,8},{10,11... | collective-permute-start | bytes 393224 | tf_op jit(solution)/shard_map/ppermute | solution.py:396
  7.1 25.6 %collective-permute-start.1 = (bf16[512,256]{1,0:T(8,128)(2,1)S(1)}, bf16[512,256]{1,0:T(8,128)(2,1)S(1)}, u32[]{:S(2)}, u32[]{:S(2)}) collective-permute-start(bf16[512,256]{1,0:T(8,128)(2,1)S(1)} %pad_maximum_fusion.near_ref), channel_id=1, source_target_pairs={{0,3},{1,2},{2,1},{3,0},{4,7},{5,6},{6,5},{7,4},{8,11},{9,10},{10,... | collective-permute-start | bytes 786440 | tf_op jit(solution)/shard_map/ppermute | solution.py:413
  11.6 21.0 %all-to-all-start = ((bf16[64,8,128]{2,1,0:T(8,128)(2,1)}), bf16[64,8,128]{2,1,0:T(8,128)(2,1)S(1)}, u32[]{:S(2)}, u32[]{:S(2)}) async-start(bf16[64,8,128]{2,1,0:T(8,128)(2,1)} %shard_map.85), calls=%async_computation | async-start | bytes 262144 | tf_op jit(solution)/shard_map/all_to_all | solution.py:411
  23.9 1.2 %copy-start = (bf16[2048,256]{1,0:T(8,128)(2,1)S(1)}, bf16[2048,256]{1,0:T(8,128)(2,1)}, u32[]{:S(2)}) copy-start(bf16[2048,256]{1,0:T(8,128)(2,1)} %books_hbm.1) | copy-start | bytes 3145732
  25.1 0.7 copy-start.1
  25.8 0.7 copy-start.2
  26.5 0.7 copy-start.3
  36.7 3.8 %collective-permute-start.2 = (f32[3,1024]{1,0:T(4,128)S(1)}, f32[3,1024]{1,0:T(4,128)S(1)}, u32[]{:S(2)}, u32[]{:S(2)}) collective-permute-start(f32[3,1024]{1,0:T(4,128)S(1)} %get-tuple-element.35.st_ref), channel_id=1, source_target_pairs={{0,1},{1,0},{2,3},{3,2},{4,5},{5,4},{6,7},{7,6},{8,9},{9,8},{10,11... | collective-permute-start | bytes 36872 | tf_op jit(solution)/shard_map/ppermute | solution.py:456
  40.6 5.0 %collective-permute-start.3 = (f32[3,1024]{1,0:T(4,128)S(1)}, f32[3,1024]{1,0:T(4,128)S(1)}, u32[]{:S(2)}, u32[]{:S(2)}) collective-permute-start(f32[3,1024]{1,0:T(4,128)S(1)} %pad_maximum_fusion.1.sta_ref), channel_id=1, source_target_pairs={{0,3},{1,2},{2,1},{3,0},{4,7},{5,6},{6,5},{7,4},{8,11},{9,10},{10,... | collective-permute-start | bytes 36872 | tf_op jit(solution)/shard_map/ppermute | solution.py:466
  50.0 11.6 %collective-permute-start.4 = (bf16[16,64,256]{2,1,0:T(8,128)(2,1)S(1)}, bf16[16,64,256]{2,1,0:T(8,128)(2,1)S(1)}, u32[]{:S(2)}, u32[]{:S(2)}) collective-permute-start(bf16[16,64,256]{2,1,0:T(8,128)(2,1)S(1)} %get-tuple-element.45), channel_id=1, source_target_pairs={{0,8},{8,0},{16,24},{24,16},{32,40},{40,32},{48,56},{56,48},{1,9},... | collective-permute-start | bytes 1572872 | tf_op jit(solution)/shard_map/ppermute | solution.py:375
  50.8 18.0 %collective-permute-start.6 = (bf16[2,256,256]{2,1,0:T(8,128)(2,1)S(1)}, bf16[2,256,256]{2,1,0:T(8,128)(2,1)S(1)}, u32[]{:S(2)}, u32[]{:S(2)}) collective-permute-start(bf16[2,256,256]{2,1,0:T(8,128)(2,1)S(1)} %get-tuple-element.49), channel_id=1, source_target_pairs={{0,1},{1,0},{2,3},{3,2},{4,5},{5,4},{6,7},{7,6},{8,9},{9,8},{10,11... | collective-permute-start | bytes 786440 | tf_op jit(solution)/shard_map/ppermute | solution.py:504
  62.3 6.5 %collective-permute-start.5 = (bf16[16,32,256]{2,1,0:T(8,128)(2,1)S(1)}, bf16[16,32,256]{2,1,0:T(8,128)(2,1)S(1)}, u32[]{:S(2)}, u32[]{:S(2)}) collective-permute-start(bf16[16,32,256]{2,1,0:T(8,128)(2,1)S(1)} %get-tuple-element.47), channel_id=1, source_target_pairs={{0,4},{4,0},{1,5},{5,1},{2,6},{6,2},{3,7},{7,3},{8,12},{12,8},{9,1... | collective-permute-start | bytes 786440 | tf_op jit(solution)/shard_map/ppermute | solution.py:516
  62.4 43.3 %all-to-all-start.1 = ((bf16[64,32,256]{2,1,0:T(8,128)(2,1)}), bf16[64,32,256]{2,1,0:T(8,128)(2,1)S(1)}, u32[]{:S(2)}, u32[]{:S(2)}) async-start(bf16[64,32,256]{2,1,0:T(8,128)(2,1)} %bitcast.11), calls=%async_computation.1 | async-start | bytes 2097152 | tf_op jit(solution)/shard_map/all_to_all | solution.py:498
  69.6 6.8 %collective-permute-start.8 = (bf16[128,256]{1,0:T(8,128)(2,1)S(1)}, bf16[128,256]{1,0:T(8,128)(2,1)S(1)}, u32[]{:S(2)}, u32[]{:S(2)}) collective-permute-start(bf16[128,256]{1,0:T(8,128)(2,1)S(1)} %get-tuple-element.55), channel_id=1, source_target_pairs={{0,1},{1,2},{2,3},{3,0},{4,5},{5,6},{6,7},{7,4},{8,9},{9,10},{10,1... | collective-permute-start | bytes 196616 | tf_op jit(solution)/shard_map/ppermute | solution.py:371
  69.7 6.7 %collective-permute-start.9 = (bf16[128,256]{1,0:T(8,128)(2,1)S(1)}, bf16[128,256]{1,0:T(8,128)(2,1)S(1)}, u32[]{:S(2)}, u32[]{:S(2)}) collective-permute-start(bf16[128,256]{1,0:T(8,128)(2,1)S(1)} %get-tuple-element.56), channel_id=1, source_target_pairs={{0,2},{1,3},{2,0},{3,1},{4,6},{5,7},{6,4},{7,5},{8,10},{9,11},{10,... | collective-permute-start | bytes 196616 | tf_op jit(solution)/shard_map/ppermute | solution.py:371
  72.0 4.9 %collective-permute-start.10 = (bf16[128,256]{1,0:T(8,128)(2,1)S(1)}, bf16[128,256]{1,0:T(8,128)(2,1)S(1)}, u32[]{:S(2)}, u32[]{:S(2)}) collective-permute-start(bf16[128,256]{1,0:T(8,128)(2,1)S(1)} %get-tuple-element.57), channel_id=1, source_target_pairs={{0,3},{1,0},{2,1},{3,2},{4,7},{5,4},{6,5},{7,6},{8,11},{9,8},{10,9... | collective-permute-start | bytes 196616 | tf_op jit(solution)/shard_map/ppermute | solution.py:371
  77.0 4.4 %collective-permute-start.11 = (bf16[64,256]{1,0:T(8,128)(2,1)S(1)}, bf16[64,256]{1,0:T(8,128)(2,1)S(1)}, u32[]{:S(2)}, u32[]{:S(2)}) collective-permute-start(bf16[64,256]{1,0:T(8,128)(2,1)S(1)} %slice.138), channel_id=1, source_target_pairs={{0,64},{64,0},{128,192},{192,128},{1,65},{65,1},{129,193},{193,129... | collective-permute-start | bytes 98312 | tf_op jit(solution)/shard_map/ppermute | solution.py:375
  81.4 5.1 %collective-permute-start.12 = (bf16[32,256]{1,0:T(8,128)(2,1)S(1)}, bf16[32,256]{1,0:T(8,128)(2,1)S(1)}, u32[]{:S(2)}, u32[]{:S(2)}) collective-permute-start(bf16[32,256]{1,0:T(8,128)(2,1)S(1)} %slice.139), channel_id=1, source_target_pairs={{0,192},{64,128},{128,64},{192,0},{1,193},{65,129},{129,65},{193,1... | collective-permute-start | bytes 49160 | tf_op jit(solution)/shard_map/ppermute | solution.py:375
  86.6 7.1 %collective-permute-start.13 = (bf16[16,256]{1,0:T(8,128)(2,1)S(1)}, bf16[16,256]{1,0:T(8,128)(2,1)S(1)}, u32[]{:S(2)}, u32[]{:S(2)}) collective-permute-start(bf16[16,256]{1,0:T(8,128)(2,1)S(1)} %slice.140), channel_id=1, source_target_pairs={{0,56},{8,16},{16,8},{24,32},{32,24},{40,48},{48,40},{56,0},{1,57}... | collective-permute-start | bytes 24584 | tf_op jit(solution)/shard_map/ppermute | solution.py:375
  93.7 6.3 %collective-permute-start.14 = (bf16[8,256]{1,0:T(8,128)(2,1)S(1)}, bf16[8,256]{1,0:T(8,128)(2,1)S(1)}, u32[]{:S(2)}, u32[]{:S(2)}) collective-permute-start(bf16[8,256]{1,0:T(8,128)(2,1)S(1)} %slice.141), channel_id=1, source_target_pairs={{0,24},{8,48},{16,40},{24,0},{32,56},{40,16},{48,8},{56,32},{1,25}... | collective-permute-start | bytes 12296 | tf_op jit(solution)/shard_map/ppermute | solution.py:375
  98.6 6.3 %collective-permute-start.7 = (bf16[256,256]{1,0:T(8,128)(2,1)S(1)}, bf16[256,256]{1,0:T(8,128)(2,1)S(1)}, u32[]{:S(2)}, u32[]{:S(2)}) collective-permute-start(bf16[256,256]{1,0:T(8,128)(2,1)S(1)} %get-tuple-element.51), channel_id=1, source_target_pairs={{0,3},{1,2},{2,1},{3,0},{4,7},{5,6},{6,5},{7,4},{8,11},{9,10},{10,... | collective-permute-start | bytes 393224 | tf_op jit(solution)/shard_map/ppermute | solution.py:532
